TPU v7x, 32 devices: a whole 2x2x4 slice. The times are simulated.
32 devices in a mesh: gx: 4 (over x, core), gy: 4 (over z), gz: 2 (over y).
Axes of the slice: x: 2, y: 2, z: 4, core: 2. Of those that a mesh axis runs over, the one named last changes fastest.
Arguments:
- positions: float32 [3, 512, 128], P(None, ('gx', 'gy', 'gz')), may hold values from -6 to 6
- velocities: float32 [3, 512, 128], P(None, ('gx', 'gy', 'gz')), may hold values from -6 to 6
- weights: float32 [512, 128], P(('gx', 'gy', 'gz')), may hold values from 0.5 to 2
- counts: int32 [512], P(('gx', 'gy', 'gz')), may hold values from 32 to 128
- link_offset: int32 [512, 3], P(('gx', 'gy', 'gz')), may hold values from -16 to 16
- link_mask: int32 [512, 3], P(('gx', 'gy', 'gz')), may hold values 0 or 1
- bin_box: int32 [512, 1], P(('gx', 'gy', 'gz')), may hold values from 0 to 15; in each aligned block of 16 rows (0 to 15, 16 to 31, ...) at most 2 rows name the same one
- bin_cell: int32 [512], P(('gx', 'gy', 'gz')), may hold values from 0 to 4095
- fluid: float32 [3, 16, 32, 256], P(None, 'gx', 'gy', 'gz'), may hold values from -6 to 6
Outputs:
- positions_out: float32 [3, 512, 128], P(None, ('gx', 'gy', 'gz'))
- velocities_out: float32 [3, 512, 128], P(None, ('gx', 'gy', 'gz'))
- fluid_out: float32 [3, 16, 32, 256], P(None, 'gx', 'gy', 'gz')
Inputs may be any that keep to these rules, and one draw needn't show every extreme that they name: `bin_box`: the bins of one device name one value at most 2 times; the cell lies in the box at the bin owner's index of gz. `bin_cell`: index of the cell inside its box, first dimension slowest. Slots 0 to counts - 1 of a bin are occupied.
All inputs are finite; a program needn't handle non-finite values. No bound on the sum of `link_mask` on one device may be relied on, other than what follows from the above.
Results may differ from a plain program's by a relative error of at most 0.0001.
Values sent between devices are 32-bit elements; how exact they have to be, the bound alone decides.
No kernel may reach another device: no remote copies, remote signals or barrier semaphores. Data moves between devices by JAX's collectives and lax.ppermute only.
A program may use at most 128 MiB of HBM per device.

v0:
```python
import jax
import jax.numpy as jnp
from jax import lax
from jax.sharding import PartitionSpec as P

SUBSTEPS = 2


step_sub = 0.1
stiffness = 0.05
damping = 0.05
drag_rate = 1.0
coupling = 0.004
viscosity = 0.12
highest = lax.Precision.HIGHEST


def padded_2(cells, sides, width):
    for axis, dim in sides:
        count = lax.axis_size(axis)
        ends = count - 1
        head = lax.slice_in_dim(cells, 0, width, axis=dim)
        tail = lax.slice_in_dim(cells, cells.shape[dim] - width, cells.shape[dim], axis=dim)
        cells = jnp.concatenate(
            [
                lax.ppermute(tail, axis, [(i, (i + 1) % count) for i in range(ends)]),
                cells,
                lax.ppermute(head, axis, [((i + 1) % count, i) for i in range(ends)]),
            ],
            axis=dim,
        )
    return cells


def contact(own_pos, own_vel, near_pos, near_vel, near_weight):
    distance = jnp.zeros(
        near_weight.shape[:2] + (own_pos.shape[2], near_weight.shape[2]), jnp.float32
    )
    for component in range(3):
        offset = own_pos[component][:, None, :, None] - near_pos[component][:, :, None, :]
        distance = distance + offset * offset
    kernel = near_weight[:, :, None, :] * jnp.exp(-0.5 * distance)
    weight_sum = jnp.sum(kernel, axis=(1, 3))
    pull_pos = jnp.einsum("bqij,cbqj->cbi", kernel, near_pos, precision=highest)
    pull_vel = jnp.einsum("bqij,cbqj->cbi", kernel, near_vel, precision=highest)
    return stiffness * (own_pos * weight_sum[None] - pull_pos) - damping * (
        own_vel * weight_sum[None] - pull_vel
    )


def advance(
    widened, state_pos, state_vel, carried, occupied, fluid_seen, neighbour, link_weight, block_bins
):
    bin_count = state_pos.shape[1]

    def one_block(block_id, running):
        nearby = widened[:, neighbour]
        near_pos = jnp.concatenate([state_pos[:, :, None], nearby[0:3]], 2)
        near_vel = jnp.concatenate([state_vel[:, :, None], nearby[3:6]], 2)
        near_weight = jnp.concatenate([carried[:, None], nearby[6] * link_weight[:, :, None]], 1)
        contact_force = contact(state_pos, state_vel, near_pos, near_vel, near_weight)
        drag_force = drag_rate * (fluid_seen[:, :, None] - state_vel)
        moved_vel = state_vel + step_sub * occupied[None] * (contact_force + drag_force)
        moved_pos = state_pos + step_sub * occupied[None] * moved_vel
        pulled_block = jnp.sum(carried[None] * drag_force, axis=2)
        return (moved_pos, moved_vel, pulled_block)

    start_state = (
        jnp.zeros_like(state_pos),
        jnp.zeros_like(state_vel),
        jnp.zeros((3, bin_count), jnp.float32),
    )
    return lax.fori_loop(0, bin_count // block_bins, one_block, start_state)


def stencil(padded):
    centre = padded[:, 1:-1, 1:-1, 1:-1]
    beside_all = padded[:, 2:, 1:-1, 1:-1] + padded[:, :-2, 1:-1, 1:-1]
    beside_all = beside_all + padded[:, 1:-1, 2:, 1:-1] + padded[:, 1:-1, :-2, 1:-1]
    beside_all = beside_all + padded[:, 1:-1, 1:-1, 2:] + padded[:, 1:-1, 1:-1, :-2]
    return beside_all - 6.0 * centre


def local(positions, velocities, weights, counts, link_offset, link_mask, bin_box, bin_cell, fluid):
    bin_count = positions.shape[1]
    slot_count = positions.shape[2]
    box_count = lax.axis_size(("gx", "gy"))
    cell_count = fluid.shape[1] * fluid.shape[2] * fluid.shape[3]
    flat_fluid = fluid.reshape(3, cell_count)
    occupied = (
        lax.broadcasted_iota(jnp.int32, (bin_count, slot_count), 1) < counts[:, None]
    ).astype(jnp.float32)
    carried = weights * occupied
    target = bin_box[:, 0]
    capacity = 2 * bin_count // box_count
    chosen = (target[:, None] == lax.broadcasted_iota(jnp.int32, (1, box_count), 1)).astype(
        jnp.int32
    )
    before = jnp.cumsum(chosen, axis=0) - chosen
    slot_index = target * capacity + jnp.sum(before * chosen, axis=1)
    asking = (
        jnp.zeros((box_count * capacity,), jnp.int32)
        .at[slot_index]
        .set(bin_cell)
        .reshape(box_count, capacity)
    )
    received = lax.all_to_all(asking, ("gx", "gy"), split_axis=0, concat_axis=0, tiled=True)
    values = jnp.moveaxis(flat_fluid[:, received], 0, 2)
    replies = lax.all_to_all(values, ("gx", "gy"), split_axis=0, concat_axis=0, tiled=True)
    fluid_seen = replies.reshape(box_count * capacity, 3)[slot_index].T
    neighbour = lax.broadcasted_iota(jnp.int32, (bin_count, 1), 0) + link_offset + bin_count
    link_weight = link_mask.astype(jnp.float32)
    block_bins = 16
    state_pos = positions
    state_vel = velocities
    pulled_total = jnp.zeros((3, bin_count), jnp.float32)
    for substep in range(SUBSTEPS):
        packed = jnp.concatenate([state_pos, state_vel, carried[None]], 0)
        widened = padded_2(packed, ((("gx", "gy", "gz"), 1),), bin_count)
        state_pos, state_vel, pulled = advance(
            widened,
            state_pos,
            state_vel,
            carried,
            occupied,
            fluid_seen,
            neighbour,
            link_weight,
            block_bins,
        )
        pulled_total = pulled_total + pulled
    pushed_all = -coupling * pulled_total.T
    outgoing = (
        jnp.zeros((box_count * capacity, 3), jnp.float32)
        .at[slot_index]
        .set(pushed_all)
        .reshape(box_count, capacity, 3)
    )
    arrived = lax.all_to_all(outgoing, ("gx", "gy"), split_axis=0, concat_axis=0, tiled=True)
    source = (
        jnp.zeros((3, cell_count), jnp.float32)
        .at[:, received.reshape(-1)]
        .add(arrived.reshape(-1, 3).T)
        .reshape(fluid.shape)
    )

    def fluid_rate(velocity_field):
        padded = padded_2(velocity_field, (("gx", 1), ("gy", 2), ("gz", 3)), 1)
        return viscosity * stencil(padded) + source

    first_rate = fluid_rate(fluid)
    middle = fluid + first_rate
    second_rate = fluid_rate(middle)
    fluid_out = fluid + 0.5 * (first_rate + second_rate)
    return (state_pos, state_vel, fluid_out)


def solution(mesh):
    in_specs = (
        P(None, ("gx", "gy", "gz"), None),
        P(None, ("gx", "gy", "gz"), None),
        P(("gx", "gy", "gz"), None),
        P(("gx", "gy", "gz")),
        P(("gx", "gy", "gz"), None),
        P(("gx", "gy", "gz"), None),
        P(("gx", "gy", "gz"), None),
        P(("gx", "gy", "gz")),
        P(None, "gx", "gy", "gz"),
    )
    out_specs = (
        P(None, ("gx", "gy", "gz"), None),
        P(None, ("gx", "gy", "gz"), None),
        P(None, "gx", "gy", "gz"),
    )
    return jax.shard_map(local, mesh=mesh, in_specs=in_specs, out_specs=out_specs, check_vma=False)
```

profile of v0, /device:TPU:0, one launch (start us, length us, event | category | flops | bytes accessed | tf_op | source)
XLA Modules:
  0.0 129.2 jit_solution(8788199603534144835)
XLA Ops:
  4.3 5.5 %collective-permute-start = (f32[7,16,128]{2,0,1:T(8,128)S(1)}, f32[7,16,128]{2,0,1:T(8,128)S(1)}, u32[]{:S(2)}, u32[]{:S(2)}) collective-permute-start(f32[7,16,128]{2,0,1:T(8,128)S(1)} %pad_maximum_fusion.5), channel_id=1, source_target_pairs={{0,1},{1,2},{2,3},{3,4},{4,5},{5,6},{6,7},{7,8},{8,9},{9,10},{10,1... | collective-permute-start | bytes 172040 | tf_op jit(solution)/shard_map/ppermute | solution.py:26
  13.6 6.4 %all-to-all-start = ((s32[16,1,2]{2,1,0:T(1,128)}), s32[16,1,2]{2,1,0:T(1,128)S(1)}, u32[]{:S(2)}, u32[]{:S(2)}) async-start(s32[16,1,2]{2,1,0:T(1,128)} %bitcast.24), calls=%async_computation | async-start | bytes 16384 | tf_op jit(solution)/shard_map/all_to_all | solution.py:107
  20.7 2.3 %collective-permute-start.5 = (f32[3,1,8,128]{3,2,1,0:T(8,128)S(1)}, f32[3,1,8,128]{3,2,1,0:T(8,128)S(1)}, u32[]{:S(2)}, u32[]{:S(2)}) collective-permute-start(f32[3,1,8,128]{3,2,1,0:T(8,128)S(1)} %get-tuple-element.103), channel_id=1, source_target_pairs={{0,8},{8,16},{16,24},{1,9},{9,17},{17,25},{2,10},{10,18},{18,26},{... | collective-permute-start | bytes 36872 | tf_op jit(solution)/shard_map/ppermute | solution.py:26
  23.0 1.3 collective-permute-start.4
  25.7 1.4 %copy.98 = f32[3,4,8,128]{0,3,2,1:T(8,128)S(1)} copy(f32[3,4,8,128]{3,2,1,0:T(8,128)} %param.17) | data formatting | bytes 98304 | tf_op args[8]
  28.8 8.0 %all-to-all-start.1 = ((f32[16,2,3]{2,1,0:T(2,128)}), f32[16,2,3]{2,1,0:T(2,128)S(1)}, u32[]{:S(2)}, u32[]{:S(2)}) async-start(f32[16,2,3]{2,1,0:T(2,128)} %bitcast.26), calls=%async_computation.1 | async-start | bytes 32768 | tf_op jit(solution)/shard_map/all_to_all | solution.py:109
  38.2 4.5 %collective-permute-start.7 = (f32[3,6,1,128]{3,2,1,0:T(1,128)S(1)}, f32[3,6,1,128]{3,2,1,0:T(1,128)S(1)}, u32[]{:S(2)}, u32[]{:S(2)}) collective-permute-start(f32[3,6,1,128]{3,2,1,0:T(1,128)S(1)} %get-tuple-element.98), channel_id=1, source_target_pairs={{0,2},{2,4},{4,6},{1,3},{3,5},{5,7},{8,10},{10,12},{12,14},{9,11},... | collective-permute-start | bytes 27656 | tf_op jit(solution)/shard_map/ppermute | solution.py:26
  44.8 5.8 %collective-permute-start.9 = (f32[3,6,10,1]{3,2,1,0:T(8,128)S(1)}, f32[3,6,10,1]{3,2,1,0:T(8,128)S(1)}, u32[]{:S(2)}, u32[]{:S(2)}) collective-permute-start(f32[3,6,10,1]{3,2,1,0:T(8,128)S(1)} %get-tuple-element.77), channel_id=1, source_target_pairs={{0,1},{2,3},{4,5},{6,7},{8,9},{10,11},{12,13},{14,15},{16,17},{18,... | collective-permute-start | bytes 2168 | tf_op jit(solution)/shard_map/ppermute | solution.py:26
  52.9 2.3 %fusion.2 = f32[16,128]{1,0:T(8,128)S(1)} fusion(f32[16,4,128]{2,1,0:T(4,128)S(1)} %bitcast.137, f32[16,128]{1,0:T(8,128)S(1)} %get-tuple-element.112, f32[16,4,128]{2,1,0:T(4,128)S(1)} %bitcast.140, f32[16,128]{1,0:T(8,128)S(1)} %get-tuple-element.111, f32[16,4,128]{2,1,0:T(4,128)S(1)} %bitcast.134, f32[16,128]{1,0:T(8,128)S(1)} %get-tuple-element.110, ...), kind=kLoop, calls=%fused_computation.11 | loop fusion | flops 11532288 | bytes 163840 | tf_op jit(solution)/shard_map/while/body/eval_jaxpr/reduce_sum | solution.py:43
  55.2 5.6 %fusion.49 = f32[3,16,128]{2,0,1:T(4,128)S(1)} fusion(f32[16,4,128]{2,1,0:T(4,128)S(1)} %bitcast.138, f32[16,128]{1,0:T(8,128)S(1)} %get-tuple-element.112, f32[16,4,128]{2,1,0:T(4,128)S(1)} %bitcast.141, f32[16,128]{1,0:T(8,128)S(1)} %get-tuple-element.111, f32[16,4,128]{2,1,0:T(4,128)S(1)} %bitcast.135, f32[16,128]{1,0:T(8,128)S(1)} %get-tuple-element.110, ...), kind=kOutput, calls=%fused_computation.58 | convolution fusion | flops 48277504 | bytes 311296 | tf_op jit(solution)/shard_map/while/body/eval_jaxpr/bqij,cbqj->cbi/dot_general | solution.py:44
  60.8 5.9 %multiply_reduce_fusion = (f32[3,16]{0,1:T(8,128)S(1)}, f32[3,16]{0,1:T(8,128)S(1)}, f32[3,16,128]{2,0,1:T(4,128)S(1)}, f32[3,16,128]{2,0,1:T(4,128)S(1)}) fusion(f32[16,128]{1,0:T(8,128)S(1)} %get-tuple-element.116, f32[3,16]{0,1:T(8,128)S(1)} %bitcast.153, f32[3,16,128]{2,1,0:T(8,128)S(1)} %copy-done.2, f32[16,128]{1,0:T(8,128)S(1)} %get-tuple-element.115, ...), kind=kOutput, calls=%fused_computation.146 | convolution fusion | flops 48351136 | bytes 401984 | tf_op jit(solution)/shard_map/while/body/eval_jaxpr/bqij,cbqj->cbi/dot_general | solution.py:45
  67.9 6.3 %all-to-all-start.2 = ((f32[16,2,3]{2,1,0:T(2,128)}), f32[16,2,3]{2,1,0:T(2,128)S(1)}, u32[]{:S(2)}, u32[]{:S(2)}) async-start(f32[16,2,3]{2,1,0:T(2,128)} %bitcast.51), calls=%async_computation.2 | async-start | bytes 32768 | tf_op jit(solution)/shard_map/all_to_all | solution.py:139
  74.2 6.4 %all-to-all-done.2 = f32[16,2,3]{2,1,0:T(2,128)S(1)} async-done(((f32[16,2,3]{2,1,0:T(2,128)}), f32[16,2,3]{2,1,0:T(2,128)S(1)}, u32[]{:S(2)}, u32[]{:S(2)}) %all-to-all-start.2) | async-done | bytes 416 | tf_op jit(solution)/shard_map/all_to_all | solution.py:139
  84.0 3.0 %collective-permute-start.11 = (f32[3,1,8,128]{3,2,1,0:T(8,128)S(1)}, f32[3,1,8,128]{3,2,1,0:T(8,128)S(1)}, u32[]{:S(2)}, u32[]{:S(2)}) collective-permute-start(f32[3,1,8,128]{3,2,1,0:T(8,128)S(1)} %get-tuple-element.100), channel_id=1, source_target_pairs={{0,8},{8,16},{16,24},{1,9},{9,17},{17,25},{2,10},{10,18},{18,26},{... | collective-permute-start | bytes 36872 | tf_op jit(solution)/shard_map/ppermute | solution.py:26
  89.1 4.5 %collective-permute-start.13 = (f32[3,6,1,128]{3,2,1,0:T(1,128)S(1)}, f32[3,6,1,128]{3,2,1,0:T(1,128)S(1)}, u32[]{:S(2)}, u32[]{:S(2)}) collective-permute-start(f32[3,6,1,128]{3,2,1,0:T(1,128)S(1)} %get-tuple-element.96), channel_id=1, source_target_pairs={{0,2},{2,4},{4,6},{1,3},{3,5},{5,7},{8,10},{10,12},{12,14},{9,11},... | collective-permute-start | bytes 27656 | tf_op jit(solution)/shard_map/ppermute | solution.py:26
  93.7 1.3 collective-permute-start.3
  95.0 5.2 %collective-permute-start.2 = (f32[7,16,128]{2,0,1:T(8,128)S(1)}, f32[7,16,128]{2,0,1:T(8,128)S(1)}, u32[]{:S(2)}, u32[]{:S(2)}) collective-permute-start(f32[7,16,128]{2,0,1:T(8,128)S(1)} %pad_maximum_fusion.4), channel_id=1, source_target_pairs={{0,1},{1,2},{2,3},{3,4},{4,5},{5,6},{6,7},{7,8},{8,9},{9,10},{10,1... | collective-permute-start | bytes 172040 | tf_op jit(solution)/shard_map/ppermute | solution.py:26
  100.4 4.8 %collective-permute-start.15 = (f32[3,6,10,1]{3,2,1,0:T(8,128)S(1)}, f32[3,6,10,1]{3,2,1,0:T(8,128)S(1)}, u32[]{:S(2)}, u32[]{:S(2)}) collective-permute-start(f32[3,6,10,1]{3,2,1,0:T(8,128)S(1)} %get-tuple-element.75), channel_id=1, source_target_pairs={{0,1},{2,3},{4,5},{6,7},{8,9},{10,11},{12,13},{14,15},{16,17},{18,... | collective-permute-start | bytes 2168 | tf_op jit(solution)/shard_map/ppermute | solution.py:26
  105.2 1.5 %collective-permute-start.14 = (f32[3,6,10,1]{3,2,1,0:T(8,128)S(1)}, f32[3,6,10,1]{3,2,1,0:T(8,128)S(1)}, u32[]{:S(2)}, u32[]{:S(2)}) collective-permute-start(f32[3,6,10,1]{3,2,1,0:T(8,128)S(1)} %get-tuple-element.74), channel_id=1, source_target_pairs={{1,0},{3,2},{5,4},{7,6},{9,8},{11,10},{13,12},{15,14},{17,16},{19,... | collective-permute-start | bytes 2168 | tf_op jit(solution)/shard_map/ppermute | solution.py:28
  106.7 2.0 %collective-permute-done.15 = f32[3,6,10,1]{3,2,1,0:T(8,128)S(1)} collective-permute-done((f32[3,6,10,1]{3,2,1,0:T(8,128)S(1)}, f32[3,6,10,1]{3,2,1,0:T(8,128)S(1)}, u32[]{:S(2)}, u32[]{:S(2)}) %collective-permute-start.15) | collective-permute-done | bytes 752 | tf_op jit(solution)/shard_map/ppermute | solution.py:26
  108.7 4.1 %collective-permute-done.14 = f32[3,6,10,1]{3,2,1,0:T(8,128)S(1)} collective-permute-done((f32[3,6,10,1]{3,2,1,0:T(8,128)S(1)}, f32[3,6,10,1]{3,2,1,0:T(8,128)S(1)}, u32[]{:S(2)}, u32[]{:S(2)}) %collective-permute-start.14) | collective-permute-done | bytes 752 | tf_op jit(solution)/shard_map/ppermute | solution.py:28
  114.5 2.3 %fusion.5 = f32[16,128]{1,0:T(8,128)S(1)} fusion(f32[16,4,128]{2,1,0:T(4,128)S(1)} %bitcast.146, f32[16,128]{1,0:T(8,128)S(1)} %bitcast.158, f32[16,4,128]{2,1,0:T(4,128)S(1)} %bitcast.149, f32[16,128]{1,0:T(8,128)S(1)} %bitcast.161, f32[16,4,128]{2,1,0:T(4,128)S(1)} %bitcast.143, f32[16,128]{1,0:T(8,128)S(1)} %bitcast.155, f32[16,4,128]{2,1,0:T(4,128)S(1)} %copy.110), kind=kLoop, calls=%fused_computation.14 | loop fusion | flops 11532288 | bytes 163840 | tf_op jit(solution)/shard_map/while/body/eval_jaxpr/reduce_sum | solution.py:43
  116.8 5.6 %fusion.57 = f32[3,16,128]{2,0,1:T(4,128)S(1)} fusion(f32[16,4,128]{2,1,0:T(4,128)S(1)} %bitcast.147, f32[16,128]{1,0:T(8,128)S(1)} %bitcast.159, f32[16,4,128]{2,1,0:T(4,128)S(1)} %bitcast.150, f32[16,128]{1,0:T(8,128)S(1)} %bitcast.162, f32[16,4,128]{2,1,0:T(4,128)S(1)} %bitcast.144, f32[16,128]{1,0:T(8,128)S(1)} %bitcast.156, ...), kind=kOutput, calls=%fused_computation.66 | convolution fusion | flops 48277504 | bytes 311296 | tf_op jit(solution)/shard_map/while/body/eval_jaxpr/bqij,cbqj->cbi/dot_general | solution.py:44
  122.4 5.6 %multiply_add_fusion = (f32[3,16,128]{2,0,1:T(4,128)S(1)}, f32[3,16,128]{2,0,1:T(4,128)S(1)}) fusion(f32[3,16,128]{2,0,1:T(4,128)S(1)} %get-tuple-element.104, f32[16,128]{1,0:T(8,128)S(1)} %get-tuple-element.115, f32[3,16,128]{2,0,1:T(4,128)S(1)} %get-tuple-element.117, f32[3,16]{0,1:T(8,128)S(1)} %bitcast.154, f32[3,16,128]{2,0,1:T(4,128)S(1)} %fusion.57, ...), kind=kOutput, calls=%fused_computation.148 | convolution fusion | flops 48320512 | bytes 393408 | tf_op jit(solution)/shard_map/while/body/eval_jaxpr/bqij,cbqj->cbi/dot_general | solution.py:45
  (93 shorter events, 26.3 us)
Async XLA Ops:
  0.6 36.2 %copy-start = (f32[3,4,8,128]{3,2,1,0:T(8,128)S(1)}, f32[3,4,8,128]{3,2,1,0:T(8,128)}, u32[]{:S(2)}) copy-start(f32[3,4,8,128]{3,2,1,0:T(8,128)} %param.17) | copy-start | bytes 147460
  0.6 42.1 %copy-start.3 = (s32[16,3]{0,1:T(4,128)S(1)}, s32[16,3]{0,1:T(4,128)}, u32[]{:S(2)}) copy-start(s32[16,3]{0,1:T(4,128)} %param.14) | copy-start | bytes 580
  3.0 48.9 %collective-permute-start.1 = (f32[7,16,128]{2,0,1:T(8,128)S(1)}, f32[7,16,128]{2,0,1:T(8,128)S(1)}, u32[]{:S(2)}, u32[]{:S(2)}) collective-permute-start(f32[7,16,128]{2,0,1:T(8,128)S(1)} %pad_maximum_fusion.5), channel_id=1, source_target_pairs={{1,0},{2,1},{3,2},{4,3},{5,4},{6,5},{7,6},{8,7},{9,8},{10,9},{11,1... | collective-permute-start | bytes 172040 | tf_op jit(solution)/shard_map/ppermute | solution.py:28
  4.3 47.6 %collective-permute-start = (f32[7,16,128]{2,0,1:T(8,128)S(1)}, f32[7,16,128]{2,0,1:T(8,128)S(1)}, u32[]{:S(2)}, u32[]{:S(2)}) collective-permute-start(f32[7,16,128]{2,0,1:T(8,128)S(1)} %pad_maximum_fusion.5), channel_id=1, source_target_pairs={{0,1},{1,2},{2,3},{3,4},{4,5},{5,6},{6,7},{7,8},{8,9},{9,10},{10,1... | collective-permute-start | bytes 172040 | tf_op jit(solution)/shard_map/ppermute | solution.py:26
  13.6 13.8 %all-to-all-start = ((s32[16,1,2]{2,1,0:T(1,128)}), s32[16,1,2]{2,1,0:T(1,128)S(1)}, u32[]{:S(2)}, u32[]{:S(2)}) async-start(s32[16,1,2]{2,1,0:T(1,128)} %bitcast.24), calls=%async_computation | async-start | bytes 16384 | tf_op jit(solution)/shard_map/all_to_all | solution.py:107
  20.7 16.1 %collective-permute-start.5 = (f32[3,1,8,128]{3,2,1,0:T(8,128)S(1)}, f32[3,1,8,128]{3,2,1,0:T(8,128)S(1)}, u32[]{:S(2)}, u32[]{:S(2)}) collective-permute-start(f32[3,1,8,128]{3,2,1,0:T(8,128)S(1)} %get-tuple-element.103), channel_id=1, source_target_pairs={{0,8},{8,16},{16,24},{1,9},{9,17},{17,25},{2,10},{10,18},{18,26},{... | collective-permute-start | bytes 36872 | tf_op jit(solution)/shard_map/ppermute | solution.py:26
  23.0 13.8 %collective-permute-start.4 = (f32[3,1,8,128]{3,2,1,0:T(8,128)S(1)}, f32[3,1,8,128]{3,2,1,0:T(8,128)S(1)}, u32[]{:S(2)}, u32[]{:S(2)}) collective-permute-start(f32[3,1,8,128]{3,2,1,0:T(8,128)S(1)} %get-tuple-element.102), channel_id=1, source_target_pairs={{8,0},{16,8},{24,16},{9,1},{17,9},{25,17},{10,2},{18,10},{26,18},{... | collective-permute-start | bytes 36872 | tf_op jit(solution)/shard_map/ppermute | solution.py:28
  28.8 15.2 %all-to-all-start.1 = ((f32[16,2,3]{2,1,0:T(2,128)}), f32[16,2,3]{2,1,0:T(2,128)S(1)}, u32[]{:S(2)}, u32[]{:S(2)}) async-start(f32[16,2,3]{2,1,0:T(2,128)} %bitcast.26), calls=%async_computation.1 | async-start | bytes 32768 | tf_op jit(solution)/shard_map/all_to_all | solution.py:109
  36.9 7.7 %collective-permute-start.6 = (f32[3,6,1,128]{3,2,1,0:T(1,128)S(1)}, f32[3,6,1,128]{3,2,1,0:T(1,128)S(1)}, u32[]{:S(2)}, u32[]{:S(2)}) collective-permute-start(f32[3,6,1,128]{3,2,1,0:T(1,128)S(1)} %get-tuple-element.99), channel_id=1, source_target_pairs={{2,0},{4,2},{6,4},{3,1},{5,3},{7,5},{10,8},{12,10},{14,12},{11,9},... | collective-permute-start | bytes 27656 | tf_op jit(solution)/shard_map/ppermute | solution.py:28
  38.2 6.5 %collective-permute-start.7 = (f32[3,6,1,128]{3,2,1,0:T(1,128)S(1)}, f32[3,6,1,128]{3,2,1,0:T(1,128)S(1)}, u32[]{:S(2)}, u32[]{:S(2)}) collective-permute-start(f32[3,6,1,128]{3,2,1,0:T(1,128)S(1)} %get-tuple-element.98), channel_id=1, source_target_pairs={{0,2},{2,4},{4,6},{1,3},{3,5},{5,7},{8,10},{10,12},{12,14},{9,11},... | collective-permute-start | bytes 27656 | tf_op jit(solution)/shard_map/ppermute | solution.py:26
  44.7 10.5 %copy-start.1 = (f32[3,16,128]{2,1,0:T(8,128)S(1)}, f32[3,16,128]{2,1,0:T(8,128)}, u32[]{:S(2)}) copy-start(f32[3,16,128]{2,1,0:T(8,128)} %param.9) | copy-start | bytes 73732
  44.8 37.7 %collective-permute-start.9 = (f32[3,6,10,1]{3,2,1,0:T(8,128)S(1)}, f32[3,6,10,1]{3,2,1,0:T(8,128)S(1)}, u32[]{:S(2)}, u32[]{:S(2)}) collective-permute-start(f32[3,6,10,1]{3,2,1,0:T(8,128)S(1)} %get-tuple-element.77), channel_id=1, source_target_pairs={{0,1},{2,3},{4,5},{6,7},{8,9},{10,11},{12,13},{14,15},{16,17},{18,... | collective-permute-start | bytes 2168 | tf_op jit(solution)/shard_map/ppermute | solution.py:26
  50.6 31.9 %collective-permute-start.8 = (f32[3,6,10,1]{3,2,1,0:T(8,128)S(1)}, f32[3,6,10,1]{3,2,1,0:T(8,128)S(1)}, u32[]{:S(2)}, u32[]{:S(2)}) collective-permute-start(f32[3,6,10,1]{3,2,1,0:T(8,128)S(1)} %get-tuple-element.76), channel_id=1, source_target_pairs={{1,0},{3,2},{5,4},{7,6},{9,8},{11,10},{13,12},{15,14},{17,16},{19,... | collective-permute-start | bytes 2168 | tf_op jit(solution)/shard_map/ppermute | solution.py:28
  55.2 5.6 %copy-start.2 = (f32[3,16,128]{2,1,0:T(8,128)S(1)}, f32[3,16,128]{2,1,0:T(8,128)}, u32[]{:S(2)}) copy-start(f32[3,16,128]{2,1,0:T(8,128)} %param.10) | copy-start | bytes 73732
  67.9 12.7 %all-to-all-start.2 = ((f32[16,2,3]{2,1,0:T(2,128)}), f32[16,2,3]{2,1,0:T(2,128)S(1)}, u32[]{:S(2)}, u32[]{:S(2)}) async-start(f32[16,2,3]{2,1,0:T(2,128)} %bitcast.51), calls=%async_computation.2 | async-start | bytes 32768 | tf_op jit(solution)/shard_map/all_to_all | solution.py:139
  82.7 4.3 %collective-permute-start.10 = (f32[3,1,8,128]{3,2,1,0:T(8,128)S(1)}, f32[3,1,8,128]{3,2,1,0:T(8,128)S(1)}, u32[]{:S(2)}, u32[]{:S(2)}) collective-permute-start(f32[3,1,8,128]{3,2,1,0:T(8,128)S(1)} %get-tuple-element.101), channel_id=1, source_target_pairs={{8,0},{16,8},{24,16},{9,1},{17,9},{25,17},{10,2},{18,10},{26,18},{... | collective-permute-start | bytes 36872 | tf_op jit(solution)/shard_map/ppermute | solution.py:28
  84.0 3.9 %collective-permute-start.11 = (f32[3,1,8,128]{3,2,1,0:T(8,128)S(1)}, f32[3,1,8,128]{3,2,1,0:T(8,128)S(1)}, u32[]{:S(2)}, u32[]{:S(2)}) collective-permute-start(f32[3,1,8,128]{3,2,1,0:T(8,128)S(1)} %get-tuple-element.100), channel_id=1, source_target_pairs={{0,8},{8,16},{16,24},{1,9},{9,17},{17,25},{2,10},{10,18},{18,26},{... | collective-permute-start | bytes 36872 | tf_op jit(solution)/shard_map/ppermute | solution.py:26
  87.8 12.4 %collective-permute-start.12 = (f32[3,6,1,128]{3,2,1,0:T(1,128)S(1)}, f32[3,6,1,128]{3,2,1,0:T(1,128)S(1)}, u32[]{:S(2)}, u32[]{:S(2)}) collective-permute-start(f32[3,6,1,128]{3,2,1,0:T(1,128)S(1)} %get-tuple-element.97), channel_id=1, source_target_pairs={{2,0},{4,2},{6,4},{3,1},{5,3},{7,5},{10,8},{12,10},{14,12},{11,9},... | collective-permute-start | bytes 27656 | tf_op jit(solution)/shard_map/ppermute | solution.py:28
  89.1 11.1 %collective-permute-start.13 = (f32[3,6,1,128]{3,2,1,0:T(1,128)S(1)}, f32[3,6,1,128]{3,2,1,0:T(1,128)S(1)}, u32[]{:S(2)}, u32[]{:S(2)}) collective-permute-start(f32[3,6,1,128]{3,2,1,0:T(1,128)S(1)} %get-tuple-element.96), channel_id=1, source_target_pairs={{0,2},{2,4},{4,6},{1,3},{3,5},{5,7},{8,10},{10,12},{12,14},{9,11},... | collective-permute-start | bytes 27656 | tf_op jit(solution)/shard_map/ppermute | solution.py:26
  93.7 19.9 %collective-permute-start.3 = (f32[7,16,128]{2,0,1:T(8,128)S(1)}, f32[7,16,128]{2,0,1:T(8,128)S(1)}, u32[]{:S(2)}, u32[]{:S(2)}) collective-permute-start(f32[7,16,128]{2,0,1:T(8,128)S(1)} %pad_maximum_fusion.4), channel_id=1, source_target_pairs={{1,0},{2,1},{3,2},{4,3},{5,4},{6,5},{7,6},{8,7},{9,8},{10,9},{11,1... | collective-permute-start | bytes 172040 | tf_op jit(solution)/shard_map/ppermute | solution.py:28
  95.0 18.6 %collective-permute-start.2 = (f32[7,16,128]{2,0,1:T(8,128)S(1)}, f32[7,16,128]{2,0,1:T(8,128)S(1)}, u32[]{:S(2)}, u32[]{:S(2)}) collective-permute-start(f32[7,16,128]{2,0,1:T(8,128)S(1)} %pad_maximum_fusion.4), channel_id=1, source_target_pairs={{0,1},{1,2},{2,3},{3,4},{4,5},{5,6},{6,7},{7,8},{8,9},{9,10},{10,1... | collective-permute-start | bytes 172040 | tf_op jit(solution)/shard_map/ppermute | solution.py:26
  100.4 8.3 %collective-permute-start.15 = (f32[3,6,10,1]{3,2,1,0:T(8,128)S(1)}, f32[3,6,10,1]{3,2,1,0:T(8,128)S(1)}, u32[]{:S(2)}, u32[]{:S(2)}) collective-permute-start(f32[3,6,10,1]{3,2,1,0:T(8,128)S(1)} %get-tuple-element.75), channel_id=1, source_target_pairs={{0,1},{2,3},{4,5},{6,7},{8,9},{10,11},{12,13},{14,15},{16,17},{18,... | collective-permute-start | bytes 2168 | tf_op jit(solution)/shard_map/ppermute | solution.py:26
  105.2 7.6 %collective-permute-start.14 = (f32[3,6,10,1]{3,2,1,0:T(8,128)S(1)}, f32[3,6,10,1]{3,2,1,0:T(8,128)S(1)}, u32[]{:S(2)}, u32[]{:S(2)}) collective-permute-start(f32[3,6,10,1]{3,2,1,0:T(8,128)S(1)} %get-tuple-element.74), channel_id=1, source_target_pairs={{1,0},{3,2},{5,4},{7,6},{9,8},{11,10},{13,12},{15,14},{17,16},{19,... | collective-permute-start | bytes 2168 | tf_op jit(solution)/shard_map/ppermute | solution.py:28
where the time goes:
time: 130 us; the launch traced here: 129 us
  starting transfers between devices  67 us (52%)
  matrix products  22.8 us (18%)
  waiting for transfers between devices  13.4 us (10%)
  other arithmetic  12.8 us (10%)
  local copies, waits for them, and re-layouts  12.1 us (9%)
    ppermute x8, starting transfers between devices, padded_2(): lax.ppermute(tail, axis, [(i, (i + 1) % count) for i in range(ends)])  35.8 us
    dot_general x2, matrix products, contact(): pull_vel = jnp.einsum('bqij,cbqj->cbi', kernel, near_vel, precision=highest)  11.5 us
    dot_general x2, matrix products, contact(): pull_pos = jnp.einsum('bqij,cbqj->cbi', kernel, near_pos, precision=highest)  11.2 us
    ppermute x8, starting transfers between devices, padded_2(): lax.ppermute(head, axis, [((i + 1) % count, i) for i in range(ends)])  10.5 us
    all_to_all x1, starting transfers between devices, local(): lax.all_to_all(values, ('gx', 'gy'), split_axis=0, concat_axis=0, tiled=T...  7.96 us
    all_to_all x1, waiting for transfers between devices, local(): lax.all_to_all(outgoing, ('gx', 'gy'), split_axis=0, concat_axis=0, tiled...  6.42 us
    all_to_all x1, starting transfers between devices, local(): lax.all_to_all(asking, ('gx', 'gy'), split_axis=0, concat_axis=0, tiled=T...  6.4 us
    all_to_all x1, starting transfers between devices, local(): lax.all_to_all(outgoing, ('gx', 'gy'), split_axis=0, concat_axis=0, tiled...  6.27 us
  transfers between devices with their start and end apart: 19, of which 4 were waited for; matrix products, arithmetic and copies ran while one was open for 22% of the time, Pallas kernels for 0%

commit v1 on v0

v1 whole, which is shorter than its diff:
```python
import functools
import math

import jax
import jax.numpy as jnp
from jax import lax
from jax.experimental import pallas as pl
from jax.experimental.pallas import tpu as pltpu
from jax.sharding import PartitionSpec as P

step_sub = 0.1
stiffness = 0.05
damping = 0.05
drag_rate = 1.0
coupling = 0.004
viscosity = 0.12
log2e = 1.4426950408889634

AXES = ("gx", "gy", "gz")
F32 = jnp.float32
BF16 = jnp.bfloat16
VMEM = pl.BlockSpec(memory_space=pltpu.VMEM)
SMEM = pl.BlockSpec(memory_space=pltpu.SMEM)
LANES = 128


def iota(shape, dim):
    return lax.broadcasted_iota(jnp.int32, shape, dim)


def nt(a, b, precision=None):
    return lax.dot_general(
        a, b, (((1,), (1,)), ((), ())), preferred_element_type=F32, precision=precision
    )


def tn(a, b):
    return lax.dot_general(a, b, (((0,), (0,)), ((), ())), preferred_element_type=F32)


def nn(a, b):
    return jnp.dot(a, b, preferred_element_type=F32)


def pieces_2(value):
    high = value.astype(BF16).astype(F32)
    return high, value - high


def pieces_3(value):
    high = value.astype(BF16).astype(F32)
    rest = value - high
    middle = rest.astype(BF16).astype(F32)
    return high, middle, rest - middle


def call(body, outs, ins, scratch=(), cost=None):
    return pl.pallas_call(
        body,
        out_shape=[jax.ShapeDtypeStruct(shape, F32) for shape in outs],
        in_specs=ins,
        out_specs=[VMEM] * len(outs),
        scratch_shapes=scratch,
        compiler_params=pltpu.CompilerParams(vmem_limit_bytes=24 * 1024 * 1024),
        cost_estimate=cost,
    )


def slot_lane(field, slot, n, bins):
    groups = LANES // n
    per_group = bins // groups
    return (slot // per_group) * (LANES // groups) + field * per_group + slot % per_group


def prep_body(
    n, pos, vel, weights, fluid, counts, box, cell, msg, send, face_low, face_high
):
    bins = pos.shape[1]
    cx, cy, cz = fluid.shape[1:]
    lane = iota((8, LANES), 1)
    row = iota((8, LANES), 0)
    for k in range(bins):
        for c in range(3):
            msg[k, c : c + 1, :] = pos[c, k : k + 1, :]
            msg[k, c + 4 : c + 5, :] = vel[c, k : k + 1, :]
        occupied = iota((1, LANES), 1) < counts[k]
        msg[k, 3:4, :] = jnp.where(occupied, weights[k : k + 1, :], 0.0)
        msg[k, 7:8, :] = jnp.zeros((1, LANES), F32)
    gy_count = lax.axis_size("gy")
    height = lax.axis_index("gz")
    ids = jnp.zeros((8, LANES), F32)
    for k in range(bins):
        target, inside = box[k], cell[k]
        x = lax.div(target, gy_count) * cx + lax.div(inside, cy * cz)
        y = lax.rem(target, gy_count) * cy + lax.rem(lax.div(inside, cz), cy)
        z = height * cz + lax.rem(inside, cz)
        for field, value in enumerate((x, y, z)):
            ids = jnp.where(lane == slot_lane(field, k, n, bins), value.astype(F32), ids)
    pick = jnp.where(
        ((row == 1) & (lane == 0))
        | ((row == 2) & (lane == 1))
        | ((row == 3) & (lane == cz - 2))
        | ((row == 4) & (lane == cz - 1)),
        1.0,
        0.0,
    )
    flat = fluid[...].reshape(3 * cx * cy, cz)
    flat = jnp.concatenate([flat, jnp.zeros((LANES - 3 * cx * cy, cz), F32)], 0)
    faces = nt(pick, flat, lax.Precision.HIGHEST)
    chunk = jnp.where(row == 0, ids, faces)
    for d in range(n):
        send[d] = chunk
    face_low[...] = fluid[:, 0:2]
    face_high[...] = fluid[:, cx - 2 : cx]


def gather_body(n, bins, recv, fluid, out):
    cx, cy, cz = fluid.shape[1:]
    per_group = bins // (LANES // n)
    cells = cx * cy
    ids = recv[:, 0, :]
    x = ids - (lax.axis_index("gx") * cx).astype(F32)
    y = pltpu.roll(ids, LANES - per_group, 1) - (lax.axis_index("gy") * cy).astype(F32)
    z = pltpu.roll(ids, LANES - 2 * per_group, 1) - (lax.axis_index("gz") * cz).astype(F32)
    mine = (x >= 0) & (x < cx) & (y >= 0) & (y < cy) & (z >= 0) & (z < cz)
    column_code = jnp.where(mine, x * cy + y, -1.0).astype(jnp.int32)
    depth_code = jnp.where(mine, z, -1.0).astype(jnp.int32)
    flat = fluid[...].reshape(3 * cells, cz)
    high, low = pieces_2(flat)
    table = jnp.concatenate([high, low, jnp.zeros((256 - 6 * cells, cz), F32)], 0).astype(BF16)
    lane_z = iota((n, cz), 1)
    lane_cell = iota((n, 256), 1) % cells
    one_hot = []
    masks = []
    for k in range(bins):
        at = slot_lane(0, k, n, bins)
        one_hot.append(jnp.where(depth_code[:, at : at + 1] == lane_z, 1.0, 0.0))
        masks.append(column_code[:, at : at + 1] == lane_cell)
    picked = nt(jnp.concatenate(one_hot, 0).astype(BF16), table)
    kept = jnp.where(jnp.concatenate(masks, 0), picked, 0.0).astype(BF16)
    rows = iota((256, LANES), 0)
    fold = jnp.where(
        (rows < 6 * cells) & ((rows // cells) % 3 == iota((256, LANES), 1) % 4), 1.0, 0.0
    ).astype(BF16)
    spread = nn(kept, fold)
    slot_of_lane = iota((n, LANES), 1) // 4
    total = jnp.zeros((n, LANES), F32)
    for k in range(bins):
        total = total + jnp.where(slot_of_lane == k, spread[k * n : (k + 1) * n], 0.0)
    out[...] = total


def load_block(block, row, index, stack, weighted):
    square = block * block
    norm = (-0.5 * log2e) * (
        square[0:1] + square[1:2] + square[2:3]
    )
    near = jnp.where(
        row < 3, block, jnp.where(row == 3, norm, jnp.where(row == 4, 1.0, 0.0))
    )
    high, middle, low = pieces_3(near)
    stack[index] = jnp.concatenate([high, high, middle, middle, high, low], 0).astype(BF16)
    carried = block[3:4]
    product = jnp.where(row == 3, carried, jnp.where(row == 7, 0.0, block * carried))
    high, low = pieces_2(product)
    weighted[index] = jnp.concatenate([high, low], 0).astype(BF16)
    return norm


def own_side(block, norm, row):
    own = jnp.where(
        row < 3, block * log2e, jnp.where(row == 3, 1.0, jnp.where(row == 4, norm, 0.0))
    )
    high, middle, low = pieces_3(own)
    return jnp.concatenate([high, middle, high, middle, low, high], 0).astype(BF16)


def pair_sums(k, d, n, bins, own, stack, weighted, offset, mask):
    near = [bins + k]
    heavy = [bins + k]
    for q in range(offset.shape[0]):
        shift = offset[q, k]
        near.append(bins + k + shift)
        whole = d * bins + k + shift
        linked = (mask[q, k] != 0) & (whole >= 0) & (whole < n * bins)
        heavy.append(jnp.where(linked, bins + k + shift, 3 * bins))
    others = jnp.concatenate([stack[index] for index in near], 1)
    masses = jnp.concatenate([weighted[index] for index in heavy], 1)
    kernel = jnp.exp2(tn(own, others))
    high = kernel.astype(BF16)
    low = (kernel - high.astype(F32)).astype(BF16)
    first = nt(masses, high)
    second = nt(masses, low)
    return first[0:8] + first[8:16] + second[0:8]


def contact_force(block, sums):
    gap = block * sums[3:4] - sums
    return stiffness * pltpu.roll(gap, 4, 0) - damping * gap


def flat_id():
    return (
        lax.axis_index("gx") * lax.axis_size("gy") + lax.axis_index("gy")
    ) * lax.axis_size("gz") + lax.axis_index("gz")


def first_body(
    n, own, before, after, seen, counts, offset, mask, moved, send, stack, weighted, norms
):
    bins = own.shape[0]
    d = flat_id()
    row = iota((8, LANES), 0)
    lane = iota((8, LANES), 1)
    for k in range(bins):
        load_block(before[k], row, k, stack, weighted)
        norms[k : k + 1, :] = load_block(own[k], row, bins + k, stack, weighted)
        load_block(after[k], row, 2 * bins + k, stack, weighted)
    weighted[3 * bins] = jnp.zeros((16, LANES), BF16)
    groups = LANES // n
    per_group = bins // groups
    field = jnp.where(row >= 4, row - 4, 3)
    deposit = jnp.zeros((8, LANES), F32)
    for k in range(bins):
        block = own[k]
        sums = pair_sums(
            k, d, n, bins, own_side(block, norms[k : k + 1, :], row), stack, weighted, offset, mask
        )
        force = contact_force(block, sums)
        occupied = jnp.where(lane < counts[k], step_sub, 0.0)
        new_vel = block + occupied * (force - drag_rate * block)
        new_pos = block + occupied * pltpu.roll(new_vel, 4, 0)
        result = jnp.where(row < 3, new_pos, jnp.where(row == 3, block, new_vel))
        moved[k] = result
        load = jnp.where(row == 3, block, block[3:4] * (block + new_vel))
        column = jnp.sum(load, axis=1, keepdims=True)
        base = slot_lane(0, k, n, bins)
        place = (lane == base + per_group * field) & (row >= 3) & (row < 7)
        deposit = deposit + jnp.where(place, column, 0.0)
    deposit = jnp.sum(deposit, axis=0, keepdims=True)
    send[...] = jnp.broadcast_to(
        jnp.where(row == 3, deposit, 0.0)[None], (n, 8, LANES)
    )
    values = seen[...]
    send[:, 0, :] = pltpu.roll(values, 1, 0)
    send[:, 1, :] = values
    send[:, 2, :] = pltpu.roll(values, n - 1, 0)


def second_body(
    n, own, before, after, recv, counts, offset, mask, pos, vel, stack, weighted, state
):
    bins = own.shape[0]
    d = flat_id()
    row = iota((8, LANES), 0)
    lane = iota((8, LANES), 1)
    seen = recv[0]
    for s in range(1, n):
        seen = seen + recv[s]
    columns = [
        jnp.transpose(jnp.broadcast_to(seen[part : part + 1], (LANES, LANES)))
        for part in range(3)
    ]
    rate = jnp.where(row < 4, step_sub * step_sub, step_sub) * drag_rate

    def push(part, k):
        pair = columns[part][8 * (k // 2) : 8 * (k // 2) + 8]
        other = pltpu.roll(pair, 4, 0)
        here = (row < 4) if k % 2 == 0 else (row >= 4)
        both = jnp.where(here, pair, other)
        return jnp.where((row == 3) | (row == 7), 0.0, both * rate), both

    for k in range(bins):
        load_block(before[k] + push(0, k)[0], row, k, stack, weighted)
        load_block(after[k] + push(2, k)[0], row, 2 * bins + k, stack, weighted)
        block = own[k] + jnp.where(lane < counts[k], push(1, k)[0], 0.0)
        state[k] = block
        load_block(block, row, bins + k, stack, weighted)
    weighted[3 * bins] = jnp.zeros((16, LANES), BF16)
    for k in range(bins):
        block = state[k]
        square = block * block
        norm = (-0.5 * log2e) * (square[0:1] + square[1:2] + square[2:3])
        sums = pair_sums(
            k, d, n, bins, own_side(block, norm, row), stack, weighted, offset, mask
        )
        force = contact_force(block, sums)
        occupied = jnp.where(lane < counts[k], step_sub, 0.0)
        fluid_seen = push(1, k)[1]
        new_vel = block + occupied * (force + drag_rate * (fluid_seen - block))
        new_pos = block + occupied * pltpu.roll(new_vel, 4, 0)
        for c in range(3):
            pos[c, k : k + 1, :] = new_pos[c : c + 1]
            vel[c, k : k + 1, :] = new_vel[c + 4 : c + 5]


def side_body(fluid, from_low, from_high, low, high):
    cx, cy = fluid.shape[1:3]
    gx = lax.axis_index("gx")
    has_low = jnp.where(gx > 0, 1.0, 0.0)
    has_high = jnp.where(gx < lax.axis_size("gx") - 1, 1.0, 0.0)
    for j in range(2):
        for c in range(3):
            for i in range(cx + 2):
                at = (j * 3 + c) * (cx + 2) + i
                for out, y in ((low, j), (high, cy - 2 + j)):
                    if i == 0:
                        line = from_low[c, 1, y : y + 1, :] * has_low
                    elif i == cx + 1:
                        line = from_high[c, 0, y : y + 1, :] * has_high
                    else:
                        line = fluid[c, i - 1, y : y + 1, :]
                    out[at : at + 1, :] = line
    used = 6 * (cx + 2)
    if used < low.shape[0]:
        low[used:, :] = jnp.zeros((low.shape[0] - used, LANES), F32)
        high[used:, :] = jnp.zeros((low.shape[0] - used, LANES), F32)


def laplace(at, x):
    centre = at(x)
    tall, wide = centre.shape
    total = at(x + 1) + at(x - 1)
    total = total + pltpu.roll(centre, 1, 0) + pltpu.roll(centre, tall - 1, 0)
    total = total + pltpu.roll(centre, 1, 1) + pltpu.roll(centre, wide - 1, 1)
    return viscosity * (total - 6.0 * centre)


def stencil_body(
    n, fluid, x_low, x_high, y_low, y_high, recv, around, part, faces, rates
):
    cx, cy, cz = fluid.shape[1:]
    gx, gy, gz = (lax.axis_index(a) for a in AXES)
    nx, ny, nz = (lax.axis_size(a) for a in AXES)
    tall, wide = 2 * cy, 2 * cz
    deep = cx + 4

    def exists(dx, dy, dz):
        ok = (gx + dx >= 0) & (gx + dx < nx) & (gy + dy >= 0) & (gy + dy < ny)
        return ok & (gz + dz >= 0) & (gz + dz < nz)

    def chunk(dx, dy, dz):
        source = ((gx + dx) * ny + gy + dy) * nz + gz + dz
        value = recv[jnp.clip(source, 0, n - 1)]
        return jnp.where(exists(dx, dy, dz), value, 0.0)

    def columns(dx, dy):
        above, below = chunk(dx, dy, 1), chunk(dx, dy, -1)
        faces[...] = jnp.zeros((LANES, LANES), F32)
        faces[0:2, :] = above[1:3]
        faces[cz - 2 : cz, :] = below[3:5]
        return jnp.transpose(faces[...])

    own_z = columns(0, 0)
    low_z, high_z = columns(-1, 0), columns(1, 0)
    left_z, right_z = columns(0, -1), columns(0, 1)
    x_on = [jnp.where(exists(-1, 0, 0), 1.0, 0.0), jnp.where(exists(1, 0, 0), 1.0, 0.0)]
    y_on = [jnp.where(exists(0, -1, 0), 1.0, 0.0), jnp.where(exists(0, 1, 0), 1.0, 0.0)]
    row = iota((cy, cz), 0)

    def y_line(ref, j, c, i):
        at = (j * 3 + c) * (cx + 2) + i
        return ref[at : at + 1, :]

    for c in range(3):
        for x in range(-2, cx + 2):
            if x < 0:
                core = x_low[c, x + 2] * x_on[0]
            elif x >= cx:
                core = x_high[c, x - cx] * x_on[1]
            else:
                core = fluid[c, x]
            beyond = jnp.zeros((cy, cz), F32)
            if 0 <= x < cx:
                at = (c * cx + x) * cy
                beyond = own_z[at : at + cy]
            elif x == -1:
                at = (c * cx + cx - 1) * cy
                beyond = low_z[at : at + cy]
            elif x == cx:
                at = c * cx * cy
                beyond = high_z[at : at + cy]
            around[c, x % deep, 0:cy, 0:cz] = core
            around[c, x % deep, 0:cy, cz:wide] = beyond
            side = jnp.zeros((cy, cz), F32)
            side_z = jnp.zeros((cy, cz), F32)
            if -1 <= x <= cx:
                side = jnp.where(row == 0, y_line(y_high, 0, c, x + 1) * y_on[1], side)
                side = jnp.where(row == 1, y_line(y_high, 1, c, x + 1) * y_on[1], side)
                side = jnp.where(row == cy - 2, y_line(y_low, 0, c, x + 1) * y_on[0], side)
                side = jnp.where(row == cy - 1, y_line(y_low, 1, c, x + 1) * y_on[0], side)
            if 0 <= x < cx:
                at = (c * cx + x) * cy
                side_z = jnp.where(row == 0, right_z[at : at + 1], side_z)
                side_z = jnp.where(row == cy - 1, left_z[at + cy - 1 : at + cy], side_z)
            around[c, x % deep, cy:tall, 0:cz] = side
            around[c, x % deep, cy:tall, cz:wide] = side_z

    y_row, z_lane = iota((tall, wide), 0), iota((tall, wide), 1)
    inside = jnp.where(y_row < cy, 1.0, 0.0)
    inside = jnp.where(y_row == cy, y_on[1], jnp.where(y_row == tall - 1, y_on[0], inside))
    deep_on = jnp.where(z_lane < cz, 1.0, 0.0)
    deep_on = jnp.where(z_lane == cz, jnp.where(exists(0, 0, 1), 1.0, 0.0), deep_on)
    deep_on = jnp.where(z_lane == wide - 1, jnp.where(exists(0, 0, -1), 1.0, 0.0), deep_on)
    inside = inside * deep_on
    for c in range(3):
        for x in range(-1, cx + 1):
            rate = laplace(lambda i: around[c, i % deep], x) * inside
            if x < 0:
                rate = rate * x_on[0]
            elif x == cx:
                rate = rate * x_on[1]
            rates[c, x + 1] = rate
        for x in range(cx):
            again = laplace(lambda i: rates[c, i + 1], x)
            total = around[c, x] + rates[c, x + 1] + 0.5 * again
            part[c, x] = total[0:cy, 0:cz]


def deposit_body(n, bins, part, around, ids, recv, out, table, low_table, depth, field):
    cx, cy, cz = part.shape[1:]
    deep = cx + 4
    tall, wide = 2 * cy, 2 * cz
    groups = LANES // n
    per_group = bins // groups
    planes = (cx + 2) * tall

    def packed(ref, which):
        turned = jnp.transpose(
            jnp.concatenate(
                [ref[:, which, :]] + ([jnp.zeros((LANES - n, LANES), F32)] if n < LANES else []), 0
            )
        )
        span = LANES // groups
        total = turned[0:span]
        for g in range(1, groups):
            total = total + pltpu.roll(turned[g * span : (g + 1) * span], g * n, 1)
        return total

    where = packed(ids, 0)
    loads = packed(recv, 3)
    x = where[0:per_group] - (lax.axis_index("gx") * cx - 1).astype(F32)
    y = where[per_group : 2 * per_group] - (lax.axis_index("gy") * cy).astype(F32)
    z = where[2 * per_group : 3 * per_group] - (lax.axis_index("gz") * cz).astype(F32)
    near = (x >= 0) & (x < cx + 2) & (y >= -1) & (y <= cy) & (z >= -1) & (z <= cz)
    y = jnp.where(y < 0, y + tall, y)
    z = jnp.where(z < 0, z + wide, z)
    plane_code = jnp.where(near, x * tall + y, -1.0).astype(jnp.int32)
    depth_code = jnp.where(near, z, -1.0).astype(jnp.int32)
    plane_row = iota((planes, LANES), 0)
    depth_row = iota((wide, LANES), 0)
    for r in range(per_group):
        at = r * LANES
        hit = plane_code[r : r + 1] == plane_row
        for f in range(4):
            load = loads[f * per_group + r : f * per_group + r + 1]
            high, low = pieces_2(load)
            table[f * planes : (f + 1) * planes, at : at + LANES] = jnp.where(
                hit, high, 0.0
            ).astype(BF16)
            low_table[f * planes : (f + 1) * planes, at : at + LANES] = jnp.where(
                hit, low, 0.0
            ).astype(BF16)
        depth[:, at : at + LANES] = jnp.where(
            depth_code[r : r + 1] == depth_row, 1.0, 0.0
        ).astype(BF16)
    spread = nt(table[...], depth[...]) + nt(low_table[...], depth[...])
    factor = coupling * drag_rate * (2.0 - step_sub * drag_rate)
    for c in range(3):
        for i in range(cx + 2):
            moment = spread[c * planes + i * tall : c * planes + (i + 1) * tall]
            mass = spread[3 * planes + i * tall : 3 * planes + (i + 1) * tall]
            field[c, i] = (coupling * drag_rate) * moment - factor * around[
                c, (i - 1) % deep
            ] * mass
        for x in range(cx):
            rate = laplace(lambda i: field[c, i + 1], x)
            total = field[c, x + 1] + 0.5 * rate
            out[c, x] = part[c, x] + total[0:cy, 0:cz]


def ring(n, step):
    return [(i, (i + step) % n) for i in range(n)]


def local(positions, velocities, weights, counts, link_offset, link_mask, bin_box, bin_cell, fluid):
    n = lax.axis_size(AXES)
    nx, ny = lax.axis_size("gx"), lax.axis_size("gy")
    bins = positions.shape[1]
    cx, cy, cz = fluid.shape[1:]
    offset, mask = link_offset.T, link_mask.T
    side_rows = -(-6 * (cx + 2) // 8) * 8

    own, send, face_low, face_high = call(
        functools.partial(prep_body, n),
        [(bins, 8, LANES), (n, 8, LANES), (3, 2, cy, cz), (3, 2, cy, cz)],
        [VMEM] * 4 + [SMEM] * 3,
    )(positions, velocities, weights, fluid, counts, bin_box[:, 0], bin_cell)
    ids = lax.all_to_all(send, AXES, 0, 0, tiled=True)
    before = lax.ppermute(own, AXES, ring(n, 1))
    after = lax.ppermute(own, AXES, ring(n, -1))
    x_low = lax.ppermute(face_high, "gx", ring(nx, 1))
    x_high = lax.ppermute(face_low, "gx", ring(nx, -1))

    (seen,) = call(functools.partial(gather_body, n, bins), [(n, LANES)], [VMEM] * 2)(ids, fluid)
    pair_scratch = [
        pltpu.VMEM((3 * bins + 1, 48, LANES), BF16),
        pltpu.VMEM((3 * bins + 1, 16, LANES), BF16),
    ]
    moved, send = call(
        functools.partial(first_body, n),
        [(bins, 8, LANES), (n, 8, LANES)],
        [VMEM] * 4 + [SMEM] * 3,
        pair_scratch + [pltpu.VMEM((bins, LANES), F32)],
    )(own, before, after, seen, counts, offset, mask)
    replies = lax.all_to_all(send, AXES, 0, 0, tiled=True)
    before = lax.ppermute(moved, AXES, ring(n, 1))
    after = lax.ppermute(moved, AXES, ring(n, -1))

    side_low, side_high = call(side_body, [(side_rows, LANES)] * 2, [VMEM] * 3)(
        fluid, x_low, x_high
    )
    y_low = lax.ppermute(side_high, "gy", ring(ny, 1))
    y_high = lax.ppermute(side_low, "gy", ring(ny, -1))
    around, part = call(
        functools.partial(stencil_body, n),
        [(3, cx + 4, 2 * cy, 2 * cz), (3, cx, cy, cz)],
        [VMEM] * 6,
        [pltpu.VMEM((LANES, LANES), F32), pltpu.VMEM((3, cx + 2, 2 * cy, 2 * cz), F32)],
    )(fluid, x_low, x_high, y_low, y_high, ids)
    positions_out, velocities_out = call(
        functools.partial(second_body, n),
        [positions.shape, velocities.shape],
        [VMEM] * 4 + [SMEM] * 3,
        pair_scratch + [pltpu.VMEM((bins, 8, LANES), F32)],
    )(moved, before, after, replies, counts, offset, mask)
    lanes = bins * n
    planes = (cx + 2) * 2 * cy
    (fluid_out,) = call(
        functools.partial(deposit_body, n, bins),
        [fluid.shape],
        [VMEM] * 4,
        [
            pltpu.VMEM((4 * planes, lanes), BF16),
            pltpu.VMEM((4 * planes, lanes), BF16),
            pltpu.VMEM((2 * cz, lanes), BF16),
            pltpu.VMEM((3, cx + 2, 2 * cy, 2 * cz), F32),
        ],
    )(part, around, ids, replies)
    return positions_out, velocities_out, fluid_out


def solution(mesh):
    in_specs = (
        P(None, AXES, None),
        P(None, AXES, None),
        P(AXES, None),
        P(AXES),
        P(AXES, None),
        P(AXES, None),
        P(AXES, None),
        P(AXES),
        P(None, "gx", "gy", "gz"),
    )
    out_specs = (
        P(None, AXES, None),
        P(None, AXES, None),
        P(None, "gx", "gy", "gz"),
    )
    return jax.shard_map(local, mesh=mesh, in_specs=in_specs, out_specs=out_specs, check_vma=False)
```

time: 130 us -> 55.2 us (0.42)
  starting transfers between devices: 67 us -> 26 us
  matrix products: 22.8 us -> 0 us
  Pallas kernels: 0 us -> 13.8 us
  other arithmetic: 12.8 us -> 0 us
  local copies, waits for them, and re-layouts: 12.1 us -> 3.64 us
  waiting for transfers between devices: 13.4 us -> 10.5 us
    ppermute x16 -> x8, starting transfers between devices: 46.3 us -> 16.1 us  [the longest x1 5.25 us: local(): after = lax.ppermute(own, AXES, ring(n, -1))]
    dot_general x4 -> x0, matrix products: 22.8 us -> none  [the longest x2 11.5 us: contact(): pull_vel = jnp.einsum('bqij,cbqj->cbi', kernel, near_vel, precision=highest)]
    pallas_call x0 -> x7, Pallas kernels: none -> 13.8 us  [the longest x1 4.99 us: local(): call(functools.partial(second_body, n), [positions.shape, velocities.shap...]
    all_to_all x3 -> x2, starting transfers between devices: 20.6 us -> 9.9 us  [the longest x1 7.33 us: local(): ids = lax.all_to_all(send, AXES, 0, 0, tiled=True)]
    reduce_sum x3 -> x0, other arithmetic: 5.36 us -> none  [the longest x2 4.52 us: contact(): weight_sum = jnp.sum(kernel, axis=(1, 3))]
    all_to_all x3 -> x2, waiting for transfers between devices: 6.43 us -> 2.56 us  [the longest x1 2.55 us: local(): ids = lax.all_to_all(send, AXES, 0, 0, tiled=True)]
    gather x4 -> x0, local copies, waits for them, and re-layouts: 2.94 us -> none  [the longest x2 1.22 us: one_block(): nearby = widened[:, neighbour]]
    select_n x4 -> x0, other arithmetic: 1.36 us -> none  [the longest x1 0.69 us: one_block(): nearby = widened[:, neighbour]]
  transfers between devices with their start and end apart: 19 -> 10, of which waited for: 4 -> 4; matrix products, arithmetic and copies ran while one was open for 22% -> 0% of each run, Pallas kernels for 0% -> 2%
where the time goes in v1:
time: 55.2 us; the launch traced here: 54.7 us
  starting transfers between devices  26 us (47%)
  Pallas kernels  13.8 us (25%)
  waiting for transfers between devices  10.5 us (19%)
  local copies, waits for them, and re-layouts  3.64 us (7%)
  between operations  0.75 us (1%)
    all_to_all x1, starting transfers between devices, local(): ids = lax.all_to_all(send, AXES, 0, 0, tiled=True)  7.33 us
    ppermute x1, starting transfers between devices, local(): after = lax.ppermute(own, AXES, ring(n, -1))  5.25 us
    ppermute x1, starting transfers between devices, local(): after = lax.ppermute(moved, AXES, ring(n, -1))  5.25 us
    pallas_call x1, Pallas kernels, local(): call(functools.partial(second_body, n), [positions.shape, velocities.shap...  4.99 us
    pallas_call x1, Pallas kernels, local(): call(functools.partial(first_body, n), [(bins, 8, LANES), (n, 8, LANES)],...  4.96 us
    ppermute x1, waiting for transfers between devices, local(): before = lax.ppermute(own, AXES, ring(n, 1))  4.54 us
    ppermute x1, starting transfers between devices, local(): y_high = lax.ppermute(side_low, 'gy', ring(ny, -1))  3.81 us
    unnamed x20, local copies, waits for them, and re-layouts  3.64 us
  transfers between devices with their start and end apart: 10, of which 4 were waited for; matrix products, arithmetic and copies ran while one was open for 0% of the time, Pallas kernels for 2%

profile of v1, /device:TPU:0, one launch (start us, length us, event | category | flops | bytes accessed | tf_op | source)
XLA Modules:
  0.0 54.7 jit_solution(13039750649294612428)
XLA Ops:
  0.7 0.6 %copy-done.7 = s32[16]{0:T(128)S(1)} copy-done((s32[16]{0:T(128)S(1)}, s32[16]{0:T(128)}, u32[]{:S(2)}) %copy-start.7) | copy-done | bytes 88
  1.3 0.0 copy-done.9
  1.3 0.0 copy-done.8
  1.3 0.8 %copy-done = f32[3,4,8,128]{3,2,1,0:T(8,128)S(1)} copy-done((f32[3,4,8,128]{3,2,1,0:T(8,128)S(1)}, f32[3,4,8,128]{3,2,1,0:T(8,128)}, u32[]{:S(2)}) %copy-start) | copy-done | bytes 49176
  2.1 0.7 %copy-done.2 = f32[3,16,128]{2,1,0:T(8,128)S(1)} copy-done((f32[3,16,128]{2,1,0:T(8,128)S(1)}, f32[3,16,128]{2,1,0:T(8,128)}, u32[]{:S(2)}) %copy-start.2) | copy-done | bytes 24600
  2.9 0.7 %copy-done.3 = f32[3,16,128]{2,1,0:T(8,128)S(1)} copy-done((f32[3,16,128]{2,1,0:T(8,128)S(1)}, f32[3,16,128]{2,1,0:T(8,128)}, u32[]{:S(2)}) %copy-start.3) | copy-done | bytes 24600
  3.6 0.7 %copy-done.4 = f32[16,128]{1,0:T(8,128)S(1)} copy-done((f32[16,128]{1,0:T(8,128)S(1)}, f32[16,128]{1,0:T(8,128)}, u32[]{:S(2)}) %copy-start.4) | copy-done | bytes 8216
  4.3 1.4 %shard_map.112 = (f32[16,8,128]{2,1,0:T(8,128)S(1)}, f32[32,8,128]{2,1,0:T(8,128)}, f32[3,2,8,128]{3,2,1,0:T(8,128)S(1)}, f32[3,2,8,128]{3,2,1,0:T(8,128)S(1)}) custom-call(f32[3,16,128]{2,1,0:T(8,128)S(1)} %copy-done.2, f32[3,16,128]{2,1,0:T(8,128)S(1)} %copy-done.3, f32[16,128]{1,0:T(8,128)S(1)} %copy-done.4, f32[3,4,8,128]{3,2,1,0:T(8,128)S(1)} %copy-done, ...), custom_call_target="tpu_custom_call" | custom-call | tf_op jit(solution)/shard_map/pallas_call | solution.py:494
  5.7 7.3 %all-to-all-start = ((f32[32,8,128]{2,1,0:T(8,128)}), f32[32,8,128]{2,1,0:T(8,128)S(1)}, u32[]{:S(2)}, u32[]{:S(2)}) async-start(f32[32,8,128]{2,1,0:T(8,128)} %get-tuple-element.16), calls=%async_computation | async-start | bytes 262144 | tf_op jit(solution)/shard_map/all_to_all | solution.py:499
  13.1 5.2 %collective-permute-start.1 = (f32[16,8,128]{2,1,0:T(8,128)S(1)}, f32[16,8,128]{2,1,0:T(8,128)S(1)}, u32[]{:S(2)}, u32[]{:S(2)}) collective-permute-start(f32[16,8,128]{2,1,0:T(8,128)S(1)} %get-tuple-element.15.own), channel_id=1, source_target_pairs={{0,31},{1,0},{2,1},{3,2},{4,3},{5,4},{6,5},{7,6},{8,7},{9,8},{10,9... | collective-permute-start | bytes 196616 | tf_op jit(solution)/shard_map/ppermute | solution.py:501
  18.3 2.6 %all-to-all-done.recv.ids = f32[32,8,128]{2,1,0:T(8,128)S(1)} async-done(((f32[32,8,128]{2,1,0:T(8,128)}), f32[32,8,128]{2,1,0:T(8,128)S(1)}, u32[]{:S(2)}, u32[]{:S(2)}) %all-to-all-start) | async-done | bytes 131104 | tf_op jit(solution)/shard_map/all_to_all | solution.py:499
  20.9 0.5 shard_map.113.seen
  21.4 4.5 %collective-permute-done.before = f32[16,8,128]{2,1,0:T(8,128)S(1)} collective-permute-done((f32[16,8,128]{2,1,0:T(8,128)S(1)}, f32[16,8,128]{2,1,0:T(8,128)S(1)}, u32[]{:S(2)}, u32[]{:S(2)}) %collective-permute-start) | collective-permute-done | bytes 65568 | tf_op jit(solution)/shard_map/ppermute | solution.py:500
  26.0 5.0 %shard_map.114 = (f32[16,8,128]{2,1,0:T(8,128)S(1)}, f32[32,8,128]{2,1,0:T(8,128)}) custom-call(f32[16,8,128]{2,1,0:T(8,128)S(1)} %get-tuple-element.15.own, f32[16,8,128]{2,1,0:T(8,128)S(1)} %collective-permute-done.before, f32[16,8,128]{2,1,0:T(8,128)S(1)} %collective-permute-done.1.after, f32[32,128]{1,0:T(8,128)S(1)} %shard_map.113.seen, ...), custom_call_target="tpu_custom_call" | custom-call | tf_op jit(solution)/shard_map/pallas_call | solution.py:510
  30.9 2.6 %all-to-all-start.1 = ((f32[32,8,128]{2,1,0:T(8,128)}), f32[32,8,128]{2,1,0:T(8,128)S(1)}, u32[]{:S(2)}, u32[]{:S(2)}) async-start(f32[32,8,128]{2,1,0:T(8,128)} %get-tuple-element.18), calls=%async_computation.1 | async-start | bytes 262144 | tf_op jit(solution)/shard_map/all_to_all | solution.py:516
  33.5 5.2 %collective-permute-start.3 = (f32[16,8,128]{2,1,0:T(8,128)S(1)}, f32[16,8,128]{2,1,0:T(8,128)S(1)}, u32[]{:S(2)}, u32[]{:S(2)}) collective-permute-start(f32[16,8,128]{2,1,0:T(8,128)S(1)} %get-tuple-element.17.own), channel_id=1, source_target_pairs={{0,31},{1,0},{2,1},{3,2},{4,3},{5,4},{6,5},{7,6},{8,7},{9,8},{10,9... | collective-permute-start | bytes 196616 | tf_op jit(solution)/shard_map/ppermute | solution.py:518
  38.8 1.7 %collective-permute-start.5 = (f32[3,2,8,128]{3,2,1,0:T(8,128)S(1)}, f32[3,2,8,128]{3,2,1,0:T(8,128)S(1)}, u32[]{:S(2)}, u32[]{:S(2)}) collective-permute-start(f32[3,2,8,128]{3,2,1,0:T(8,128)S(1)} %get-tuple-element.22), channel_id=1, source_target_pairs={{0,24},{8,0},{16,8},{24,16},{1,25},{9,1},{17,9},{25,17},{2,26},{10... | collective-permute-start | bytes 73736 | tf_op jit(solution)/shard_map/ppermute | solution.py:503
  40.5 1.5 %collective-permute-done.4.from_low.x_low = f32[3,2,8,128]{3,2,1,0:T(8,128)S(1)} collective-permute-done((f32[3,2,8,128]{3,2,1,0:T(8,128)S(1)}, f32[3,2,8,128]{3,2,1,0:T(8,128)S(1)}, u32[]{:S(2)}, u32[]{:S(2)}) %collective-permute-start.4) | collective-permute-done | bytes 24608 | tf_op jit(solution)/shard_map/ppermute | solution.py:502
  42.1 0.1 collective-permute-start.6
  42.1 3.8 %collective-permute-start.7 = (f32[40,128]{1,0:T(8,128)S(1)}, f32[40,128]{1,0:T(8,128)S(1)}, u32[]{:S(2)}, u32[]{:S(2)}) collective-permute-start(f32[40,128]{1,0:T(8,128)S(1)} %get-tuple-element.24), channel_id=1, source_target_pairs={{0,6},{2,0},{4,2},{6,4},{1,7},{3,1},{5,3},{7,5},{8,14},{10,8},{12,... | collective-permute-start | bytes 61448 | tf_op jit(solution)/shard_map/ppermute | solution.py:524
  46.0 1.9 %collective-permute-done.6.y_low = f32[40,128]{1,0:T(8,128)S(1)} collective-permute-done((f32[40,128]{1,0:T(8,128)S(1)}, f32[40,128]{1,0:T(8,128)S(1)}, u32[]{:S(2)}, u32[]{:S(2)}) %collective-permute-start.6) | collective-permute-done | bytes 20512 | tf_op jit(solution)/shard_map/ppermute | solution.py:523
  47.8 0.5 shard_map.117
  48.3 5.0 %shard_map.115 = (f32[3,16,128]{2,1,0:T(8,128)}, f32[3,16,128]{2,1,0:T(8,128)}) custom-call(f32[16,8,128]{2,1,0:T(8,128)S(1)} %get-tuple-element.17.own, f32[16,8,128]{2,1,0:T(8,128)S(1)} %collective-permute-done.2.before, f32[16,8,128]{2,1,0:T(8,128)S(1)} %collective-permute-done.3.after, f32[32,8,128]{2,1,0:T(8,128)S(1)} %all-to-all-done.1.recv, ...), custom_call_target="tpu_custom_call" | custom-call | tf_op jit(solution)/shard_map/pallas_call | solution.py:531
  53.3 1.4 %shard_map.118 = f32[3,4,8,128]{3,2,1,0:T(8,128)} custom-call(f32[3,4,8,128]{3,2,1,0:T(8,128)S(1)} %get-tuple-element.25.part, f32[3,8,16,256]{3,2,1,0:T(8,128)S(1)} %get-tuple-element.26.around, f32[32,8,128]{2,1,0:T(8,128)S(1)} %all-to-all-done.recv.ids, f32[32,8,128]{2,1,0:T(8,128)S(1)} %all-to-all-done.1.recv), custom_call_target="tpu_custom_call" | custom-call | tf_op jit(solution)/shard_map/pallas_call | solution.py:539
  (23 shorter events, 0.1 us)
Async XLA Ops:
  0.6 0.7 %copy-start.7 = (s32[16]{0:T(128)S(1)}, s32[16]{0:T(128)}, u32[]{:S(2)}) copy-start(s32[16]{0:T(128)} %counts.5) | copy-start | bytes 196
  0.6 0.7 %copy-start.9 = (s32[16]{0:T(128)S(1)}, s32[16]{0:T(128)}, u32[]{:S(2)}) copy-start(s32[16]{0:T(128)} %cell.1) | copy-start | bytes 196
  0.7 0.7 %copy-start.8 = (s32[16,1]{0,1:T(1,128)S(1)}, s32[16,1]{0,1:T(1,128)}, u32[]{:S(2)}) copy-start(s32[16,1]{0,1:T(1,128)} %param.15) | copy-start | bytes 196
  1.3 0.8 %copy-start = (f32[3,4,8,128]{3,2,1,0:T(8,128)S(1)}, f32[3,4,8,128]{3,2,1,0:T(8,128)}, u32[]{:S(2)}) copy-start(f32[3,4,8,128]{3,2,1,0:T(8,128)} %fluid.7) | copy-start | bytes 147460
  2.1 0.7 %copy-start.2 = (f32[3,16,128]{2,1,0:T(8,128)S(1)}, f32[3,16,128]{2,1,0:T(8,128)}, u32[]{:S(2)}) copy-start(f32[3,16,128]{2,1,0:T(8,128)} %pos.1) | copy-start | bytes 73732
  2.9 0.7 %copy-start.3 = (f32[3,16,128]{2,1,0:T(8,128)S(1)}, f32[3,16,128]{2,1,0:T(8,128)}, u32[]{:S(2)}) copy-start(f32[3,16,128]{2,1,0:T(8,128)} %vel.1) | copy-start | bytes 73732
  3.6 0.7 %copy-start.4 = (f32[16,128]{1,0:T(8,128)S(1)}, f32[16,128]{1,0:T(8,128)}, u32[]{:S(2)}) copy-start(f32[16,128]{1,0:T(8,128)} %weights.1) | copy-start | bytes 24580
  5.7 15.1 %copy-start.1 = (f32[3,4,8,128]{3,2,1,0:T(8,128)S(1)}, f32[3,4,8,128]{3,2,1,0:T(8,128)}, u32[]{:S(2)}) copy-start(f32[3,4,8,128]{3,2,1,0:T(8,128)} %fluid.7) | copy-start | bytes 147460
  5.7 15.1 %all-to-all-start = ((f32[32,8,128]{2,1,0:T(8,128)}), f32[32,8,128]{2,1,0:T(8,128)S(1)}, u32[]{:S(2)}, u32[]{:S(2)}) async-start(f32[32,8,128]{2,1,0:T(8,128)} %get-tuple-element.16), calls=%async_computation | async-start | bytes 262144 | tf_op jit(solution)/shard_map/all_to_all | solution.py:499
  13.1 8.4 %collective-permute-start.1 = (f32[16,8,128]{2,1,0:T(8,128)S(1)}, f32[16,8,128]{2,1,0:T(8,128)S(1)}, u32[]{:S(2)}, u32[]{:S(2)}) collective-permute-start(f32[16,8,128]{2,1,0:T(8,128)S(1)} %get-tuple-element.15.own), channel_id=1, source_target_pairs={{0,31},{1,0},{2,1},{3,2},{4,3},{5,4},{6,5},{7,6},{8,7},{9,8},{10,9... | collective-permute-start | bytes 196616 | tf_op jit(solution)/shard_map/ppermute | solution.py:501
  18.3 7.7 %collective-permute-start = (f32[16,8,128]{2,1,0:T(8,128)S(1)}, f32[16,8,128]{2,1,0:T(8,128)S(1)}, u32[]{:S(2)}, u32[]{:S(2)}) collective-permute-start(f32[16,8,128]{2,1,0:T(8,128)S(1)} %get-tuple-element.15.own), channel_id=1, source_target_pairs={{0,1},{1,2},{2,3},{3,4},{4,5},{5,6},{6,7},{7,8},{8,9},{9,10},{10,1... | collective-permute-start | bytes 196616 | tf_op jit(solution)/shard_map/ppermute | solution.py:500
  20.9 5.1 %copy-start.6 = (s32[16,3]{0,1:T(4,128)S(1)}, s32[16,3]{0,1:T(4,128)}, u32[]{:S(2)}) copy-start(s32[16,3]{0,1:T(4,128)} %param.14) | copy-start | bytes 580
  21.4 4.6 %copy-start.5 = (s32[16,3]{0,1:T(4,128)S(1)}, s32[16,3]{0,1:T(4,128)}, u32[]{:S(2)}) copy-start(s32[16,3]{0,1:T(4,128)} %param.13) | copy-start | bytes 580
  30.9 17.4 %all-to-all-start.1 = ((f32[32,8,128]{2,1,0:T(8,128)}), f32[32,8,128]{2,1,0:T(8,128)S(1)}, u32[]{:S(2)}, u32[]{:S(2)}) async-start(f32[32,8,128]{2,1,0:T(8,128)} %get-tuple-element.18), calls=%async_computation.1 | async-start | bytes 262144 | tf_op jit(solution)/shard_map/all_to_all | solution.py:516
  33.5 14.8 %collective-permute-start.3 = (f32[16,8,128]{2,1,0:T(8,128)S(1)}, f32[16,8,128]{2,1,0:T(8,128)S(1)}, u32[]{:S(2)}, u32[]{:S(2)}) collective-permute-start(f32[16,8,128]{2,1,0:T(8,128)S(1)} %get-tuple-element.17.own), channel_id=1, source_target_pairs={{0,31},{1,0},{2,1},{3,2},{4,3},{5,4},{6,5},{7,6},{8,7},{9,8},{10,9... | collective-permute-start | bytes 196616 | tf_op jit(solution)/shard_map/ppermute | solution.py:518
  38.8 9.5 %collective-permute-start.2 = (f32[16,8,128]{2,1,0:T(8,128)S(1)}, f32[16,8,128]{2,1,0:T(8,128)S(1)}, u32[]{:S(2)}, u32[]{:S(2)}) collective-permute-start(f32[16,8,128]{2,1,0:T(8,128)S(1)} %get-tuple-element.17.own), channel_id=1, source_target_pairs={{0,1},{1,2},{2,3},{3,4},{4,5},{5,6},{6,7},{7,8},{8,9},{9,10},{10,1... | collective-permute-start | bytes 196616 | tf_op jit(solution)/shard_map/ppermute | solution.py:517
  38.8 3.3 %collective-permute-start.4 = (f32[3,2,8,128]{3,2,1,0:T(8,128)S(1)}, f32[3,2,8,128]{3,2,1,0:T(8,128)S(1)}, u32[]{:S(2)}, u32[]{:S(2)}) collective-permute-start(f32[3,2,8,128]{3,2,1,0:T(8,128)S(1)} %get-tuple-element.21), channel_id=1, source_target_pairs={{0,8},{8,16},{16,24},{24,0},{1,9},{9,17},{17,25},{25,1},{2,10},{10... | collective-permute-start | bytes 73736 | tf_op jit(solution)/shard_map/ppermute | solution.py:502
  38.8 3.3 %collective-permute-start.5 = (f32[3,2,8,128]{3,2,1,0:T(8,128)S(1)}, f32[3,2,8,128]{3,2,1,0:T(8,128)S(1)}, u32[]{:S(2)}, u32[]{:S(2)}) collective-permute-start(f32[3,2,8,128]{3,2,1,0:T(8,128)S(1)} %get-tuple-element.22), channel_id=1, source_target_pairs={{0,24},{8,0},{16,8},{24,16},{1,25},{9,1},{17,9},{25,17},{2,26},{10... | collective-permute-start | bytes 73736 | tf_op jit(solution)/shard_map/ppermute | solution.py:503
  42.1 5.8 %collective-permute-start.6 = (f32[40,128]{1,0:T(8,128)S(1)}, f32[40,128]{1,0:T(8,128)S(1)}, u32[]{:S(2)}, u32[]{:S(2)}) collective-permute-start(f32[40,128]{1,0:T(8,128)S(1)} %get-tuple-element.23), channel_id=1, source_target_pairs={{0,2},{2,4},{4,6},{6,0},{1,3},{3,5},{5,7},{7,1},{8,10},{10,12},{12... | collective-permute-start | bytes 61448 | tf_op jit(solution)/shard_map/ppermute | solution.py:523
  42.1 5.7 %collective-permute-start.7 = (f32[40,128]{1,0:T(8,128)S(1)}, f32[40,128]{1,0:T(8,128)S(1)}, u32[]{:S(2)}, u32[]{:S(2)}) collective-permute-start(f32[40,128]{1,0:T(8,128)S(1)} %get-tuple-element.24), channel_id=1, source_target_pairs={{0,6},{2,0},{4,2},{6,4},{1,7},{3,1},{5,3},{7,5},{8,14},{10,8},{12,... | collective-permute-start | bytes 61448 | tf_op jit(solution)/shard_map/ppermute | solution.py:524

commit v2 on v1

--- a/solution.py
+++ b/solution.py
@@ -1,5 +1,4 @@
 import functools
-import math
 
 import jax
 import jax.numpy as jnp
@@ -7,6 +6,7 @@
 from jax.experimental import pallas as pl
 from jax.experimental.pallas import tpu as pltpu
 from jax.sharding import PartitionSpec as P
+
 
 step_sub = 0.1
 stiffness = 0.05
@@ -20,7 +20,8 @@
 F32 = jnp.float32
 BF16 = jnp.bfloat16
 VMEM = pl.BlockSpec(memory_space=pltpu.VMEM)
-SMEM = pl.BlockSpec(memory_space=pltpu.SMEM)
+ANY = pl.BlockSpec(memory_space=pl.ANY)
+HBM = pl.BlockSpec(memory_space=pltpu.HBM)
 LANES = 128
 
 
@@ -72,9 +73,27 @@
     return (slot // per_group) * (LANES // groups) + field * per_group + slot % per_group
 
 
-def prep_body(
-    n, pos, vel, weights, fluid, counts, box, cell, msg, send, face_low, face_high
-):
+def fetch(sources, targets, sems):
+    copies = [
+        pltpu.make_async_copy(source, target, sems.at[i])
+        for i, (source, target) in enumerate(zip(sources, targets))
+    ]
+    for copy in copies:
+        copy.start()
+    return copies
+
+
+def prep_body(n, *refs):
+    sources, (msg, send, face_low, face_high), locals_, sems = (
+        refs[:7],
+        refs[7:11],
+        refs[11:18],
+        refs[18],
+    )
+    copies = fetch(sources, locals_, sems)
+    pos, vel, weights, fluid, counts, box, cell = locals_
+    for copy in copies:
+        copy.wait()
     bins = pos.shape[1]
     cx, cy, cz = fluid.shape[1:]
     lane = iota((8, LANES), 1)
@@ -114,7 +133,7 @@
     face_high[...] = fluid[:, cx - 2 : cx]
 
 
-def gather_body(n, bins, recv, fluid, out):
+def gather_body(n, bins, recv, fluid, deposit, send):
     cx, cy, cz = fluid.shape[1:]
     per_group = bins // (LANES // n)
     cells = cx * cy
@@ -147,7 +166,10 @@
     total = jnp.zeros((n, LANES), F32)
     for k in range(bins):
         total = total + jnp.where(slot_of_lane == k, spread[k * n : (k + 1) * n], 0.0)
-    out[...] = total
+    send[:, 0, :] = pltpu.roll(total, 1, 0)
+    send[:, 1, :] = total
+    send[:, 2, :] = pltpu.roll(total, n - 1, 0)
+    send[:, 3, :] = jnp.broadcast_to(deposit[0:1], (n, LANES))
 
 
 def load_block(block, row, index, stack, weighted):
@@ -175,23 +197,32 @@
     return jnp.concatenate([high, middle, high, middle, low, high], 0).astype(BF16)
 
 
-def pair_sums(k, d, n, bins, own, stack, weighted, offset, mask):
-    near = [bins + k]
-    heavy = [bins + k]
-    for q in range(offset.shape[0]):
-        shift = offset[q, k]
-        near.append(bins + k + shift)
-        whole = d * bins + k + shift
-        linked = (mask[q, k] != 0) & (whole >= 0) & (whole < n * bins)
-        heavy.append(jnp.where(linked, bins + k + shift, 3 * bins))
-    others = jnp.concatenate([stack[index] for index in near], 1)
-    masses = jnp.concatenate([weighted[index] for index in heavy], 1)
-    kernel = jnp.exp2(tn(own, others))
-    high = kernel.astype(BF16)
-    low = (kernel - high.astype(F32)).astype(BF16)
-    first = nt(masses, high)
-    second = nt(masses, low)
-    return first[0:8] + first[8:16] + second[0:8]
+def pair_sums(d, n, bins, own_of, stack, weighted, offset, mask):
+    def exponents(k):
+        near = [bins + k]
+        heavy = [bins + k]
+        for q in range(offset.shape[0]):
+            shift = offset[q, k]
+            near.append(bins + k + shift)
+            whole = d * bins + k + shift
+            linked = (mask[q, k] != 0) & (whole >= 0) & (whole < n * bins)
+            heavy.append(jnp.where(linked, bins + k + shift, 3 * bins))
+        others = jnp.concatenate([stack[index] for index in near], 1)
+        masses = jnp.concatenate([weighted[index] for index in heavy], 1)
+        return tn(own_of(k), others), masses
+
+    sums = []
+    following = exponents(0)
+    for k in range(bins):
+        value, masses = following
+        if k + 1 < bins:
+            following = exponents(k + 1)
+        kernel = jnp.exp2(value)
+        high = kernel.astype(BF16)
+        low = (kernel - high.astype(F32)).astype(BF16)
+        turned = jnp.transpose(nt(high, masses) + nt(low, masses))
+        sums.append(turned[0:8] + turned[8:16])
+    return sums
 
 
 def contact_force(block, sums):
@@ -206,8 +237,10 @@
 
 
 def first_body(
-    n, own, before, after, seen, counts, offset, mask, moved, send, stack, weighted, norms
+    n, own, before, after, *refs
 ):
+    copies = fetch(refs[0:3], refs[8:11], refs[11])
+    moved, deposit, stack, weighted, norms, counts, offset, mask = refs[3:11]
     bins = own.shape[0]
     d = flat_id()
     row = iota((8, LANES), 0)
@@ -217,16 +250,25 @@
         norms[k : k + 1, :] = load_block(own[k], row, bins + k, stack, weighted)
         load_block(after[k], row, 2 * bins + k, stack, weighted)
     weighted[3 * bins] = jnp.zeros((16, LANES), BF16)
+    for copy in copies:
+        copy.wait()
     groups = LANES // n
     per_group = bins // groups
     field = jnp.where(row >= 4, row - 4, 3)
-    deposit = jnp.zeros((8, LANES), F32)
+    sums = pair_sums(
+        d,
+        n,
+        bins,
+        lambda k: own_side(own[k], norms[k : k + 1, :], row),
+        stack,
+        weighted,
+        offset,
+        mask,
+    )
+    total = jnp.zeros((8, LANES), F32)
     for k in range(bins):
         block = own[k]
-        sums = pair_sums(
-            k, d, n, bins, own_side(block, norms[k : k + 1, :], row), stack, weighted, offset, mask
-        )
-        force = contact_force(block, sums)
+        force = contact_force(block, sums[k])
         occupied = jnp.where(lane < counts[k], step_sub, 0.0)
         new_vel = block + occupied * (force - drag_rate * block)
         new_pos = block + occupied * pltpu.roll(new_vel, 4, 0)
@@ -236,20 +278,15 @@
         column = jnp.sum(load, axis=1, keepdims=True)
         base = slot_lane(0, k, n, bins)
         place = (lane == base + per_group * field) & (row >= 3) & (row < 7)
-        deposit = deposit + jnp.where(place, column, 0.0)
-    deposit = jnp.sum(deposit, axis=0, keepdims=True)
-    send[...] = jnp.broadcast_to(
-        jnp.where(row == 3, deposit, 0.0)[None], (n, 8, LANES)
-    )
-    values = seen[...]
-    send[:, 0, :] = pltpu.roll(values, 1, 0)
-    send[:, 1, :] = values
-    send[:, 2, :] = pltpu.roll(values, n - 1, 0)
+        total = total + jnp.where(place, column, 0.0)
+    deposit[...] = jnp.broadcast_to(jnp.sum(total, axis=0, keepdims=True), (8, LANES))
 
 
 def second_body(
-    n, own, before, after, recv, counts, offset, mask, pos, vel, stack, weighted, state
+    n, own, before, after, recv, *refs
 ):
+    copies = fetch(refs[0:3], refs[9:12], refs[12])
+    pos, vel, stack, weighted, norms, state, counts, offset, mask = refs[3:12]
     bins = own.shape[0]
     d = flat_id()
     row = iota((8, LANES), 0)
@@ -273,18 +310,26 @@
     for k in range(bins):
         load_block(before[k] + push(0, k)[0], row, k, stack, weighted)
         load_block(after[k] + push(2, k)[0], row, 2 * bins + k, stack, weighted)
+    for copy in copies:
+        copy.wait()
+    for k in range(bins):
         block = own[k] + jnp.where(lane < counts[k], push(1, k)[0], 0.0)
         state[k] = block
-        load_block(block, row, bins + k, stack, weighted)
+        norms[k : k + 1, :] = load_block(block, row, bins + k, stack, weighted)
     weighted[3 * bins] = jnp.zeros((16, LANES), BF16)
+    sums = pair_sums(
+        d,
+        n,
+        bins,
+        lambda k: own_side(state[k], norms[k : k + 1, :], row),
+        stack,
+        weighted,
+        offset,
+        mask,
+    )
     for k in range(bins):
         block = state[k]
-        square = block * block
-        norm = (-0.5 * log2e) * (square[0:1] + square[1:2] + square[2:3])
-        sums = pair_sums(
-            k, d, n, bins, own_side(block, norm, row), stack, weighted, offset, mask
-        )
-        force = contact_force(block, sums)
+        force = contact_force(block, sums[k])
         occupied = jnp.where(lane < counts[k], step_sub, 0.0)
         fluid_seen = push(1, k)[1]
         new_vel = block + occupied * (force + drag_rate * (fluid_seen - block))
@@ -483,7 +528,7 @@
     return [(i, (i + step) % n) for i in range(n)]
 
 
-def local(positions, velocities, weights, counts, link_offset, link_mask, bin_box, bin_cell, fluid):
+def step(positions, velocities, weights, counts, link_offset, link_mask, bin_box, bin_cell, fluid):
     n = lax.axis_size(AXES)
     nx, ny = lax.axis_size("gx"), lax.axis_size("gy")
     bins = positions.shape[1]
@@ -494,25 +539,46 @@
     own, send, face_low, face_high = call(
         functools.partial(prep_body, n),
         [(bins, 8, LANES), (n, 8, LANES), (3, 2, cy, cz), (3, 2, cy, cz)],
-        [VMEM] * 4 + [SMEM] * 3,
-    )(positions, velocities, weights, fluid, counts, bin_box[:, 0], bin_cell)
+        [HBM] * 7,
+        [
+            pltpu.VMEM(positions.shape, F32),
+            pltpu.VMEM(velocities.shape, F32),
+            pltpu.VMEM(weights.shape, F32),
+            pltpu.VMEM(fluid.shape, F32),
+            pltpu.SMEM((bins,), jnp.int32),
+            pltpu.SMEM((bins,), jnp.int32),
+            pltpu.SMEM((bins,), jnp.int32),
+            pltpu.SemaphoreType.DMA((7,)),
+        ],
+    )(*[
+        pltpu.with_memory_space_constraint(value, pltpu.HBM)
+        for value in (positions, velocities, weights, fluid, counts, bin_box[:, 0], bin_cell)
+    ])
     ids = lax.all_to_all(send, AXES, 0, 0, tiled=True)
     before = lax.ppermute(own, AXES, ring(n, 1))
     after = lax.ppermute(own, AXES, ring(n, -1))
     x_low = lax.ppermute(face_high, "gx", ring(nx, 1))
     x_high = lax.ppermute(face_low, "gx", ring(nx, -1))
 
-    (seen,) = call(functools.partial(gather_body, n, bins), [(n, LANES)], [VMEM] * 2)(ids, fluid)
     pair_scratch = [
         pltpu.VMEM((3 * bins + 1, 48, LANES), BF16),
         pltpu.VMEM((3 * bins + 1, 16, LANES), BF16),
     ]
-    moved, send = call(
+    scalars = [
+        pltpu.SMEM((bins,), jnp.int32),
+        pltpu.SMEM(offset.shape, jnp.int32),
+        pltpu.SMEM(mask.shape, jnp.int32),
+        pltpu.SemaphoreType.DMA((3,)),
+    ]
+    moved, deposit = call(
         functools.partial(first_body, n),
-        [(bins, 8, LANES), (n, 8, LANES)],
-        [VMEM] * 4 + [SMEM] * 3,
-        pair_scratch + [pltpu.VMEM((bins, LANES), F32)],
-    )(own, before, after, seen, counts, offset, mask)
+        [(bins, 8, LANES), (8, LANES)],
+        [VMEM] * 3 + [ANY] * 3,
+        pair_scratch + [pltpu.VMEM((bins, LANES), F32)] + scalars,
+    )(own, before, after, counts, offset, mask)
+    (send,) = call(functools.partial(gather_body, n, bins), [(n, 4, LANES)], [VMEM] * 3)(
+        ids, fluid, deposit
+    )
     replies = lax.all_to_all(send, AXES, 0, 0, tiled=True)
     before = lax.ppermute(moved, AXES, ring(n, 1))
     after = lax.ppermute(moved, AXES, ring(n, -1))
@@ -531,8 +597,10 @@
     positions_out, velocities_out = call(
         functools.partial(second_body, n),
         [positions.shape, velocities.shape],
-        [VMEM] * 4 + [SMEM] * 3,
-        pair_scratch + [pltpu.VMEM((bins, 8, LANES), F32)],
+        [VMEM] * 4 + [ANY] * 3,
+        pair_scratch
+        + [pltpu.VMEM((bins, LANES), F32), pltpu.VMEM((bins, 8, LANES), F32)]
+        + scalars,
     )(moved, before, after, replies, counts, offset, mask)
     lanes = bins * n
     planes = (cx + 2) * 2 * cy
@@ -567,4 +635,4 @@
         P(None, AXES, None),
         P(None, "gx", "gy", "gz"),
     )
-    return jax.shard_map(local, mesh=mesh, in_specs=in_specs, out_specs=out_specs, check_vma=False)
+    return jax.shard_map(step, mesh=mesh, in_specs=in_specs, out_specs=out_specs, check_vma=False)

time: 55.2 us -> 49.6 us (0.90)
  local copies, waits for them, and re-layouts: 3.64 us -> 0.67 us
  Pallas kernels: 13.8 us -> 10.9 us
  waiting for transfers between devices: 10.5 us -> 11.1 us
    ppermute x8, waiting for transfers between devices: 7.95 us -> 11.1 us  [the longest x1 5.75 us: step(): before = lax.ppermute(own, AXES, ring(n, 1))]
    unnamed x20 -> x8, local copies, waits for them, and re-layouts: 3.64 us -> 0.67 us
    pallas_call x7, Pallas kernels: 13.8 us -> 10.9 us  [the longest x1 3.27 us: step(): call(functools.partial(second_body, n), [positions.shape, velocities.shap...]
    all_to_all x2, waiting for transfers between devices: 2.56 us -> 0.01 us  [the longest x1 0.01 us: step(): replies = lax.all_to_all(send, AXES, 0, 0, tiled=True)]
  transfers between devices with their start and end apart: 10 -> 10, of which waited for: 4 -> 4; matrix products, arithmetic and copies ran while one was open for 0% -> 0% of each run, Pallas kernels for 2% -> 7%
where the time goes in v2:
time: 49.6 us; the launch traced here: 49.3 us
  starting transfers between devices  26 us (52%)
  waiting for transfers between devices  11.1 us (22%)
  Pallas kernels  10.9 us (22%)
  between operations  0.75 us (2%)
  local copies, waits for them, and re-layouts  0.67 us (1%)
    all_to_all x1, starting transfers between devices, step(): ids = lax.all_to_all(send, AXES, 0, 0, tiled=True)  7.33 us
    ppermute x1, waiting for transfers between devices, step(): before = lax.ppermute(own, AXES, ring(n, 1))  5.75 us
    ppermute x1, starting transfers between devices, step(): after = lax.ppermute(own, AXES, ring(n, -1))  5.25 us
    ppermute x1, starting transfers between devices, step(): after = lax.ppermute(moved, AXES, ring(n, -1))  5.25 us
    ppermute x1, starting transfers between devices, step(): y_high = lax.ppermute(side_low, 'gy', ring(ny, -1))  3.81 us
    pallas_call x1, Pallas kernels, step(): call(functools.partial(second_body, n), [positions.shape, velocities.shap...  3.27 us
    pallas_call x1, Pallas kernels, step(): call(functools.partial(first_body, n), [(bins, 8, LANES), (8, LANES)], [V...  2.71 us
    all_to_all x1, starting transfers between devices, step(): replies = lax.all_to_all(send, AXES, 0, 0, tiled=True)  2.56 us
  transfers between devices with their start and end apart: 10, of which 4 were waited for; matrix products, arithmetic and copies ran while one was open for 0% of the time, Pallas kernels for 7%

profile of v2, /device:TPU:0, one launch (start us, length us, event | category | flops | bytes accessed | tf_op | source)
XLA Modules:
  0.0 49.3 jit_solution(3497004691064333947)
XLA Ops:
  0.6 1.8 %shard_map.112 = (f32[16,8,128]{2,1,0:T(8,128)S(1)}, f32[32,8,128]{2,1,0:T(8,128)}, f32[3,2,8,128]{3,2,1,0:T(8,128)S(1)}, f32[3,2,8,128]{3,2,1,0:T(8,128)S(1)}) custom-call(f32[3,16,128]{2,1,0:T(8,128)} %refs_0_.3, f32[3,16,128]{2,1,0:T(8,128)} %refs_1_.1, f32[16,128]{1,0:T(8,128)} %refs_2_.1, f32[3,4,8,128]{3,2,1,0:T(8,128)} %fluid.5, s32[16]{0:T(128)} %refs_0_.5, ...), custom_call_target="tpu_custom_call" | custom-call | tf_op jit(solution)/shard_map/pallas_call | solution.py:539
  2.5 7.3 %all-to-all-start = ((f32[32,8,128]{2,1,0:T(8,128)}), f32[32,8,128]{2,1,0:T(8,128)S(1)}, u32[]{:S(2)}, u32[]{:S(2)}) async-start(f32[32,8,128]{2,1,0:T(8,128)} %get-tuple-element.17), calls=%async_computation | async-start | bytes 262144 | tf_op jit(solution)/shard_map/all_to_all | solution.py:557
  9.8 0.0 copy-start.2
  9.8 0.0 copy-start.1
  9.8 5.2 %collective-permute-start.1 = (f32[16,8,128]{2,1,0:T(8,128)S(1)}, f32[16,8,128]{2,1,0:T(8,128)S(1)}, u32[]{:S(2)}, u32[]{:S(2)}) collective-permute-start(f32[16,8,128]{2,1,0:T(8,128)S(1)} %get-tuple-element.15.own), channel_id=1, source_target_pairs={{0,31},{1,0},{2,1},{3,2},{4,3},{5,4},{6,5},{7,6},{8,7},{9,8},{10,9... | collective-permute-start | bytes 196616 | tf_op jit(solution)/shard_map/ppermute | solution.py:559
  15.1 0.0 collective-permute-start
  15.1 1.9 %collective-permute-done.1.after = f32[16,8,128]{2,1,0:T(8,128)S(1)} collective-permute-done((f32[16,8,128]{2,1,0:T(8,128)S(1)}, f32[16,8,128]{2,1,0:T(8,128)S(1)}, u32[]{:S(2)}, u32[]{:S(2)}) %collective-permute-start.1) | collective-permute-done | bytes 65568 | tf_op jit(solution)/shard_map/ppermute | solution.py:559
  17.0 5.8 %collective-permute-done.before = f32[16,8,128]{2,1,0:T(8,128)S(1)} collective-permute-done((f32[16,8,128]{2,1,0:T(8,128)S(1)}, f32[16,8,128]{2,1,0:T(8,128)S(1)}, u32[]{:S(2)}, u32[]{:S(2)}) %collective-permute-start) | collective-permute-done | bytes 65568 | tf_op jit(solution)/shard_map/ppermute | solution.py:558
  22.7 0.6 %copy-done.3 = s32[16]{0:T(128)S(1)} copy-done((s32[16]{0:T(128)S(1)}, s32[16]{0:T(128)}, u32[]{:S(2)}) %copy-start.3) | copy-done | bytes 88
  23.4 2.7 %shard_map.113 = (f32[16,8,128]{2,1,0:T(8,128)S(1)}, f32[8,128]{1,0:T(8,128)S(1)}) custom-call(f32[16,8,128]{2,1,0:T(8,128)S(1)} %get-tuple-element.15.own, f32[16,8,128]{2,1,0:T(8,128)S(1)} %collective-permute-done.before, f32[16,8,128]{2,1,0:T(8,128)S(1)} %collective-permute-done.1.after, s32[16]{0:T(128)S(1)} %copy-done.3, s32[3,16]{1,0:T(4,128)S(1)} %bitcast.3, ...), custom_call_target="tpu_custom_call" | custom-call | tf_op jit(solution)/shard_map/pallas_call | solution.py:573
  26.1 1.2 %shard_map.114 = f32[32,4,128]{2,1,0:T(4,128)} custom-call(f32[32,8,128]{2,1,0:T(8,128)S(1)} %all-to-all-done.recv.ids, f32[3,4,8,128]{3,2,1,0:T(8,128)S(1)} %copy-done, f32[8,128]{1,0:T(8,128)S(1)} %get-tuple-element.18.deposit), custom_call_target="tpu_custom_call" | custom-call | tf_op jit(solution)/shard_map/pallas_call | solution.py:579
  27.3 2.6 %all-to-all-start.1 = ((f32[32,4,128]{2,1,0:T(4,128)}), f32[32,4,128]{2,1,0:T(4,128)S(1)}, u32[]{:S(2)}, u32[]{:S(2)}) async-start(f32[32,4,128]{2,1,0:T(4,128)} %shard_map.114), calls=%async_computation.1 | async-start | bytes 131072 | tf_op jit(solution)/shard_map/all_to_all | solution.py:582
  29.9 5.2 %collective-permute-start.3 = (f32[16,8,128]{2,1,0:T(8,128)S(1)}, f32[16,8,128]{2,1,0:T(8,128)S(1)}, u32[]{:S(2)}, u32[]{:S(2)}) collective-permute-start(f32[16,8,128]{2,1,0:T(8,128)S(1)} %get-tuple-element.16.own), channel_id=1, source_target_pairs={{0,31},{1,0},{2,1},{3,2},{4,3},{5,4},{6,5},{7,6},{8,7},{9,8},{10,9... | collective-permute-start | bytes 196616 | tf_op jit(solution)/shard_map/ppermute | solution.py:584
  35.1 0.0 collective-permute-start.2
  35.1 0.0 collective-permute-start.4
  35.1 1.7 %collective-permute-start.5 = (f32[3,2,8,128]{3,2,1,0:T(8,128)S(1)}, f32[3,2,8,128]{3,2,1,0:T(8,128)S(1)}, u32[]{:S(2)}, u32[]{:S(2)}) collective-permute-start(f32[3,2,8,128]{3,2,1,0:T(8,128)S(1)} %get-tuple-element.22), channel_id=1, source_target_pairs={{0,24},{8,0},{16,8},{24,16},{1,25},{9,1},{17,9},{25,17},{2,26},{10... | collective-permute-start | bytes 73736 | tf_op jit(solution)/shard_map/ppermute | solution.py:561
  36.9 1.5 %collective-permute-done.4.from_low.x_low = f32[3,2,8,128]{3,2,1,0:T(8,128)S(1)} collective-permute-done((f32[3,2,8,128]{3,2,1,0:T(8,128)S(1)}, f32[3,2,8,128]{3,2,1,0:T(8,128)S(1)}, u32[]{:S(2)}, u32[]{:S(2)}) %collective-permute-start.4) | collective-permute-done | bytes 24608 | tf_op jit(solution)/shard_map/ppermute | solution.py:560
  38.4 0.0 collective-permute-done.5.from_high.x_high
  38.4 0.1 collective-permute-start.6
  38.5 3.8 %collective-permute-start.7 = (f32[40,128]{1,0:T(8,128)S(1)}, f32[40,128]{1,0:T(8,128)S(1)}, u32[]{:S(2)}, u32[]{:S(2)}) collective-permute-start(f32[40,128]{1,0:T(8,128)S(1)} %get-tuple-element.24), channel_id=1, source_target_pairs={{0,6},{2,0},{4,2},{6,4},{1,7},{3,1},{5,3},{7,5},{8,14},{10,8},{12,... | collective-permute-start | bytes 61448 | tf_op jit(solution)/shard_map/ppermute | solution.py:590
  42.3 1.9 %collective-permute-done.6.y_low = f32[40,128]{1,0:T(8,128)S(1)} collective-permute-done((f32[40,128]{1,0:T(8,128)S(1)}, f32[40,128]{1,0:T(8,128)S(1)}, u32[]{:S(2)}, u32[]{:S(2)}) %collective-permute-start.6) | collective-permute-done | bytes 20512 | tf_op jit(solution)/shard_map/ppermute | solution.py:589
  44.2 0.5 shard_map.117
  44.7 3.3 %shard_map.115 = (f32[3,16,128]{2,1,0:T(8,128)}, f32[3,16,128]{2,1,0:T(8,128)}) custom-call(f32[16,8,128]{2,1,0:T(8,128)S(1)} %get-tuple-element.16.own, f32[16,8,128]{2,1,0:T(8,128)S(1)} %collective-permute-done.2.before, f32[16,8,128]{2,1,0:T(8,128)S(1)} %collective-permute-done.3.after, f32[32,4,128]{2,1,0:T(4,128)S(1)} %all-to-all-done.1.recv, ...), custom_call_target="tpu_custom_call" | custom-call | tf_op jit(solution)/shard_map/pallas_call | solution.py:597
  47.9 1.4 %shard_map.118 = f32[3,4,8,128]{3,2,1,0:T(8,128)} custom-call(f32[3,4,8,128]{3,2,1,0:T(8,128)S(1)} %get-tuple-element.25.part, f32[3,8,16,256]{3,2,1,0:T(8,128)S(1)} %get-tuple-element.26.around, f32[32,8,128]{2,1,0:T(8,128)S(1)} %all-to-all-done.recv.ids, f32[32,4,128]{2,1,0:T(4,128)S(1)} %all-to-all-done.1.recv), custom_call_target="tpu_custom_call" | custom-call | tf_op jit(solution)/shard_map/pallas_call | solution.py:607
  (11 shorter events, 0.1 us)
Async XLA Ops:
  2.5 23.7 %all-to-all-start = ((f32[32,8,128]{2,1,0:T(8,128)}), f32[32,8,128]{2,1,0:T(8,128)S(1)}, u32[]{:S(2)}, u32[]{:S(2)}) async-start(f32[32,8,128]{2,1,0:T(8,128)} %get-tuple-element.17), calls=%async_computation | async-start | bytes 262144 | tf_op jit(solution)/shard_map/all_to_all | solution.py:557
  9.8 12.9 %copy-start.2 = (s32[16,3]{0,1:T(4,128)S(1)}, s32[16,3]{0,1:T(4,128)}, u32[]{:S(2)}) copy-start(s32[16,3]{0,1:T(4,128)} %param.14) | copy-start | bytes 580
  9.8 12.9 %copy-start.1 = (s32[16,3]{0,1:T(4,128)S(1)}, s32[16,3]{0,1:T(4,128)}, u32[]{:S(2)}) copy-start(s32[16,3]{0,1:T(4,128)} %param.13) | copy-start | bytes 580
  9.8 7.2 %collective-permute-start.1 = (f32[16,8,128]{2,1,0:T(8,128)S(1)}, f32[16,8,128]{2,1,0:T(8,128)S(1)}, u32[]{:S(2)}, u32[]{:S(2)}) collective-permute-start(f32[16,8,128]{2,1,0:T(8,128)S(1)} %get-tuple-element.15.own), channel_id=1, source_target_pairs={{0,31},{1,0},{2,1},{3,2},{4,3},{5,4},{6,5},{7,6},{8,7},{9,8},{10,9... | collective-permute-start | bytes 196616 | tf_op jit(solution)/shard_map/ppermute | solution.py:559
  15.1 7.7 %collective-permute-start = (f32[16,8,128]{2,1,0:T(8,128)S(1)}, f32[16,8,128]{2,1,0:T(8,128)S(1)}, u32[]{:S(2)}, u32[]{:S(2)}) collective-permute-start(f32[16,8,128]{2,1,0:T(8,128)S(1)} %get-tuple-element.15.own), channel_id=1, source_target_pairs={{0,1},{1,2},{2,3},{3,4},{4,5},{5,6},{6,7},{7,8},{8,9},{9,10},{10,1... | collective-permute-start | bytes 196616 | tf_op jit(solution)/shard_map/ppermute | solution.py:558
  22.7 0.7 %copy-start.3 = (s32[16]{0:T(128)S(1)}, s32[16]{0:T(128)}, u32[]{:S(2)}) copy-start(s32[16]{0:T(128)} %refs_0_.5) | copy-start | bytes 196
  23.4 2.7 %copy-start = (f32[3,4,8,128]{3,2,1,0:T(8,128)S(1)}, f32[3,4,8,128]{3,2,1,0:T(8,128)}, u32[]{:S(2)}) copy-start(f32[3,4,8,128]{3,2,1,0:T(8,128)} %fluid.5) | copy-start | bytes 147460
  27.3 17.4 %all-to-all-start.1 = ((f32[32,4,128]{2,1,0:T(4,128)}), f32[32,4,128]{2,1,0:T(4,128)S(1)}, u32[]{:S(2)}, u32[]{:S(2)}) async-start(f32[32,4,128]{2,1,0:T(4,128)} %shard_map.114), calls=%async_computation.1 | async-start | bytes 131072 | tf_op jit(solution)/shard_map/all_to_all | solution.py:582
  29.9 14.8 %collective-permute-start.3 = (f32[16,8,128]{2,1,0:T(8,128)S(1)}, f32[16,8,128]{2,1,0:T(8,128)S(1)}, u32[]{:S(2)}, u32[]{:S(2)}) collective-permute-start(f32[16,8,128]{2,1,0:T(8,128)S(1)} %get-tuple-element.16.own), channel_id=1, source_target_pairs={{0,31},{1,0},{2,1},{3,2},{4,3},{5,4},{6,5},{7,6},{8,7},{9,8},{10,9... | collective-permute-start | bytes 196616 | tf_op jit(solution)/shard_map/ppermute | solution.py:584
  35.1 9.5 %collective-permute-start.2 = (f32[16,8,128]{2,1,0:T(8,128)S(1)}, f32[16,8,128]{2,1,0:T(8,128)S(1)}, u32[]{:S(2)}, u32[]{:S(2)}) collective-permute-start(f32[16,8,128]{2,1,0:T(8,128)S(1)} %get-tuple-element.16.own), channel_id=1, source_target_pairs={{0,1},{1,2},{2,3},{3,4},{4,5},{5,6},{6,7},{7,8},{8,9},{9,10},{10,1... | collective-permute-start | bytes 196616 | tf_op jit(solution)/shard_map/ppermute | solution.py:583
  35.1 3.3 %collective-permute-start.4 = (f32[3,2,8,128]{3,2,1,0:T(8,128)S(1)}, f32[3,2,8,128]{3,2,1,0:T(8,128)S(1)}, u32[]{:S(2)}, u32[]{:S(2)}) collective-permute-start(f32[3,2,8,128]{3,2,1,0:T(8,128)S(1)} %get-tuple-element.21), channel_id=1, source_target_pairs={{0,8},{8,16},{16,24},{24,0},{1,9},{9,17},{17,25},{25,1},{2,10},{10... | collective-permute-start | bytes 73736 | tf_op jit(solution)/shard_map/ppermute | solution.py:560
  35.1 3.3 %collective-permute-start.5 = (f32[3,2,8,128]{3,2,1,0:T(8,128)S(1)}, f32[3,2,8,128]{3,2,1,0:T(8,128)S(1)}, u32[]{:S(2)}, u32[]{:S(2)}) collective-permute-start(f32[3,2,8,128]{3,2,1,0:T(8,128)S(1)} %get-tuple-element.22), channel_id=1, source_target_pairs={{0,24},{8,0},{16,8},{24,16},{1,25},{9,1},{17,9},{25,17},{2,26},{10... | collective-permute-start | bytes 73736 | tf_op jit(solution)/shard_map/ppermute | solution.py:561
  38.4 5.8 %collective-permute-start.6 = (f32[40,128]{1,0:T(8,128)S(1)}, f32[40,128]{1,0:T(8,128)S(1)}, u32[]{:S(2)}, u32[]{:S(2)}) collective-permute-start(f32[40,128]{1,0:T(8,128)S(1)} %get-tuple-element.23), channel_id=1, source_target_pairs={{0,2},{2,4},{4,6},{6,0},{1,3},{3,5},{5,7},{7,1},{8,10},{10,12},{12... | collective-permute-start | bytes 61448 | tf_op jit(solution)/shard_map/ppermute | solution.py:589
  38.5 5.7 %collective-permute-start.7 = (f32[40,128]{1,0:T(8,128)S(1)}, f32[40,128]{1,0:T(8,128)S(1)}, u32[]{:S(2)}, u32[]{:S(2)}) collective-permute-start(f32[40,128]{1,0:T(8,128)S(1)} %get-tuple-element.24), channel_id=1, source_target_pairs={{0,6},{2,0},{4,2},{6,4},{1,7},{3,1},{5,3},{7,5},{8,14},{10,8},{12,... | collective-permute-start | bytes 61448 | tf_op jit(solution)/shard_map/ppermute | solution.py:590

commit v3 on v2

--- a/solution.py
+++ b/solution.py
@@ -83,13 +83,23 @@
     return copies
 
 
+def exists(dx, dy, dz):
+    ok = None
+    for axis, step in zip(AXES, (dx, dy, dz)):
+        at = lax.axis_index(axis) + step
+        here = (at >= 0) & (at < lax.axis_size(axis))
+        ok = here if ok is None else ok & here
+    return ok
+
+
+def neighbour_id(dx, dy, dz):
+    gx, gy, gz = (lax.axis_index(axis) for axis in AXES)
+    return ((gx + dx) * lax.axis_size("gy") + gy + dy) * lax.axis_size("gz") + gz + dz
+
+
 def prep_body(n, *refs):
-    sources, (msg, send, face_low, face_high), locals_, sems = (
-        refs[:7],
-        refs[7:11],
-        refs[11:18],
-        refs[18],
-    )
+    sources, locals_, sems = refs[:7], refs[12:19], refs[19]
+    up, down, send, face_low, face_high = refs[7:12]
     copies = fetch(sources, locals_, sems)
     pos, vel, weights, fluid, counts, box, cell = locals_
     for copy in copies:
@@ -100,11 +110,18 @@
     row = iota((8, LANES), 0)
     for k in range(bins):
         for c in range(3):
-            msg[k, c : c + 1, :] = pos[c, k : k + 1, :]
-            msg[k, c + 4 : c + 5, :] = vel[c, k : k + 1, :]
+            up[k, c : c + 1, :] = pos[c, k : k + 1, :]
+            up[k, c + 4 : c + 5, :] = vel[c, k : k + 1, :]
         occupied = iota((1, LANES), 1) < counts[k]
-        msg[k, 3:4, :] = jnp.where(occupied, weights[k : k + 1, :], 0.0)
-        msg[k, 7:8, :] = jnp.zeros((1, LANES), F32)
+        up[k, 3:4, :] = jnp.where(occupied, weights[k : k + 1, :], 0.0)
+        up[k, 7:8, :] = jnp.zeros((1, LANES), F32)
+    for k in range(bins):
+        down[k] = up[k]
+    for out, y in ((down, 0), (up, cy - 2)):
+        for c in range(3):
+            for x in range(cx):
+                at = (c * cx + x) * 2
+                out[bins + at // 8, at % 8 : at % 8 + 2, :] = fluid[c, x, y : y + 2, :]
     gy_count = lax.axis_size("gy")
     height = lax.axis_index("gz")
     ids = jnp.zeros((8, LANES), F32)
@@ -129,6 +146,17 @@
     chunk = jnp.where(row == 0, ids, faces)
     for d in range(n):
         send[d] = chunk
+    for dx in (-1, 1):
+        for dy in (-1, 1):
+
+            @pl.when(exists(dx, dy, 0))
+            def _(dx=dx, dy=dy):
+                x, y = (0 if dx < 0 else cx - 1), (0 if dy < 0 else cy - 1)
+                value = chunk
+                for c in range(3):
+                    value = jnp.where(row == 5 + c, fluid[c, x, y : y + 1, :], value)
+                send[neighbour_id(dx, dy, 0)] = value
+
     face_low[...] = fluid[:, 0:2]
     face_high[...] = fluid[:, cx - 2 : cx]
 
@@ -239,12 +267,15 @@
 def first_body(
     n, own, before, after, *refs
 ):
-    copies = fetch(refs[0:3], refs[8:11], refs[11])
-    moved, deposit, stack, weighted, norms, counts, offset, mask = refs[3:11]
-    bins = own.shape[0]
+    copies = fetch(refs[0:3], refs[9:12], refs[12])
+    moved, moved_down, deposit, stack, weighted, norms, counts, offset, mask = refs[3:12]
+    bins = norms.shape[0]
     d = flat_id()
     row = iota((8, LANES), 0)
     lane = iota((8, LANES), 1)
+    for k in range(bins, own.shape[0]):
+        moved[k] = before[k]
+        moved_down[k] = after[k]
     for k in range(bins):
         load_block(before[k], row, k, stack, weighted)
         norms[k : k + 1, :] = load_block(own[k], row, bins + k, stack, weighted)
@@ -274,6 +305,7 @@
         new_pos = block + occupied * pltpu.roll(new_vel, 4, 0)
         result = jnp.where(row < 3, new_pos, jnp.where(row == 3, block, new_vel))
         moved[k] = result
+        moved_down[k] = result
         load = jnp.where(row == 3, block, block[3:4] * (block + new_vel))
         column = jnp.sum(load, axis=1, keepdims=True)
         base = slot_lane(0, k, n, bins)
@@ -287,7 +319,7 @@
 ):
     copies = fetch(refs[0:3], refs[9:12], refs[12])
     pos, vel, stack, weighted, norms, state, counts, offset, mask = refs[3:12]
-    bins = own.shape[0]
+    bins = norms.shape[0]
     d = flat_id()
     row = iota((8, LANES), 0)
     lane = iota((8, LANES), 1)
@@ -339,29 +371,6 @@
             vel[c, k : k + 1, :] = new_vel[c + 4 : c + 5]
 
 
-def side_body(fluid, from_low, from_high, low, high):
-    cx, cy = fluid.shape[1:3]
-    gx = lax.axis_index("gx")
-    has_low = jnp.where(gx > 0, 1.0, 0.0)
-    has_high = jnp.where(gx < lax.axis_size("gx") - 1, 1.0, 0.0)
-    for j in range(2):
-        for c in range(3):
-            for i in range(cx + 2):
-                at = (j * 3 + c) * (cx + 2) + i
-                for out, y in ((low, j), (high, cy - 2 + j)):
-                    if i == 0:
-                        line = from_low[c, 1, y : y + 1, :] * has_low
-                    elif i == cx + 1:
-                        line = from_high[c, 0, y : y + 1, :] * has_high
-                    else:
-                        line = fluid[c, i - 1, y : y + 1, :]
-                    out[at : at + 1, :] = line
-    used = 6 * (cx + 2)
-    if used < low.shape[0]:
-        low[used:, :] = jnp.zeros((low.shape[0] - used, LANES), F32)
-        high[used:, :] = jnp.zeros((low.shape[0] - used, LANES), F32)
-
-
 def laplace(at, x):
     centre = at(x)
     tall, wide = centre.shape
@@ -372,21 +381,14 @@
 
 
 def stencil_body(
-    n, fluid, x_low, x_high, y_low, y_high, recv, around, part, faces, rates
+    n, base, fluid, x_low, x_high, y_low, y_high, recv, around, part, faces, rates
 ):
     cx, cy, cz = fluid.shape[1:]
-    gx, gy, gz = (lax.axis_index(a) for a in AXES)
-    nx, ny, nz = (lax.axis_size(a) for a in AXES)
     tall, wide = 2 * cy, 2 * cz
     deep = cx + 4
 
-    def exists(dx, dy, dz):
-        ok = (gx + dx >= 0) & (gx + dx < nx) & (gy + dy >= 0) & (gy + dy < ny)
-        return ok & (gz + dz >= 0) & (gz + dz < nz)
-
     def chunk(dx, dy, dz):
-        source = ((gx + dx) * ny + gy + dy) * nz + gz + dz
-        value = recv[jnp.clip(source, 0, n - 1)]
+        value = recv[jnp.clip(neighbour_id(dx, dy, dz), 0, n - 1)]
         return jnp.where(exists(dx, dy, dz), value, 0.0)
 
     def columns(dx, dy):
@@ -403,9 +405,11 @@
     y_on = [jnp.where(exists(0, -1, 0), 1.0, 0.0), jnp.where(exists(0, 1, 0), 1.0, 0.0)]
     row = iota((cy, cz), 0)
 
-    def y_line(ref, j, c, i):
-        at = (j * 3 + c) * (cx + 2) + i
-        return ref[at : at + 1, :]
+    corners = {(dx, dy): chunk(dx, dy, 0) for dx in (-1, 1) for dy in (-1, 1)}
+
+    def y_line(ref, j, c, x):
+        at = (c * cx + x) * 2 + j
+        return ref[base + at // 8, at % 8 : at % 8 + 1, :]
 
     for c in range(3):
         for x in range(-2, cx + 2):
@@ -429,11 +433,15 @@
             around[c, x % deep, 0:cy, cz:wide] = beyond
             side = jnp.zeros((cy, cz), F32)
             side_z = jnp.zeros((cy, cz), F32)
-            if -1 <= x <= cx:
-                side = jnp.where(row == 0, y_line(y_high, 0, c, x + 1) * y_on[1], side)
-                side = jnp.where(row == 1, y_line(y_high, 1, c, x + 1) * y_on[1], side)
-                side = jnp.where(row == cy - 2, y_line(y_low, 0, c, x + 1) * y_on[0], side)
-                side = jnp.where(row == cy - 1, y_line(y_low, 1, c, x + 1) * y_on[0], side)
+            if 0 <= x < cx:
+                side = jnp.where(row == 0, y_line(y_high, 0, c, x) * y_on[1], side)
+                side = jnp.where(row == 1, y_line(y_high, 1, c, x) * y_on[1], side)
+                side = jnp.where(row == cy - 2, y_line(y_low, 0, c, x) * y_on[0], side)
+                side = jnp.where(row == cy - 1, y_line(y_low, 1, c, x) * y_on[0], side)
+            elif x in (-1, cx):
+                dx = -1 if x < 0 else 1
+                side = jnp.where(row == 0, corners[dx, 1][5 + c : 6 + c], side)
+                side = jnp.where(row == cy - 1, corners[dx, -1][5 + c : 6 + c], side)
             if 0 <= x < cx:
                 at = (c * cx + x) * cy
                 side_z = jnp.where(row == 0, right_z[at : at + 1], side_z)
@@ -534,11 +542,12 @@
     bins = positions.shape[1]
     cx, cy, cz = fluid.shape[1:]
     offset, mask = link_offset.T, link_mask.T
-    side_rows = -(-6 * (cx + 2) // 8) * 8
-
-    own, send, face_low, face_high = call(
+    face_blocks = -(-6 * cx // 8)
+    relay = lax.axis_size("gz") == 2
+
+    up, down, send, face_low, face_high = call(
         functools.partial(prep_body, n),
-        [(bins, 8, LANES), (n, 8, LANES), (3, 2, cy, cz), (3, 2, cy, cz)],
+        [(bins + face_blocks, 8, LANES)] * 2 + [(n, 8, LANES)] + [(3, 2, cy, cz)] * 2,
         [HBM] * 7,
         [
             pltpu.VMEM(positions.shape, F32),
@@ -555,8 +564,8 @@
         for value in (positions, velocities, weights, fluid, counts, bin_box[:, 0], bin_cell)
     ])
     ids = lax.all_to_all(send, AXES, 0, 0, tiled=True)
-    before = lax.ppermute(own, AXES, ring(n, 1))
-    after = lax.ppermute(own, AXES, ring(n, -1))
+    before = lax.ppermute(up, AXES, ring(n, 1))
+    after = lax.ppermute(down, AXES, ring(n, -1))
     x_low = lax.ppermute(face_high, "gx", ring(nx, 1))
     x_high = lax.ppermute(face_low, "gx", ring(nx, -1))
 
@@ -570,26 +579,26 @@
         pltpu.SMEM(mask.shape, jnp.int32),
         pltpu.SemaphoreType.DMA((3,)),
     ]
-    moved, deposit = call(
+    moved, moved_down, deposit = call(
         functools.partial(first_body, n),
-        [(bins, 8, LANES), (8, LANES)],
-        [VMEM] * 3 + [ANY] * 3,
+        [(bins + face_blocks, 8, LANES)] * 2 + [(8, LANES)],
+        [VMEM] * 3 + [HBM] * 3,
         pair_scratch + [pltpu.VMEM((bins, LANES), F32)] + scalars,
-    )(own, before, after, counts, offset, mask)
+    )(up, before, after, *[pltpu.with_memory_space_constraint(v, pltpu.HBM) for v in (counts, offset, mask)])
     (send,) = call(functools.partial(gather_body, n, bins), [(n, 4, LANES)], [VMEM] * 3)(
         ids, fluid, deposit
     )
     replies = lax.all_to_all(send, AXES, 0, 0, tiled=True)
     before = lax.ppermute(moved, AXES, ring(n, 1))
-    after = lax.ppermute(moved, AXES, ring(n, -1))
-
-    side_low, side_high = call(side_body, [(side_rows, LANES)] * 2, [VMEM] * 3)(
-        fluid, x_low, x_high
-    )
-    y_low = lax.ppermute(side_high, "gy", ring(ny, 1))
-    y_high = lax.ppermute(side_low, "gy", ring(ny, -1))
+    after = lax.ppermute(moved_down, AXES, ring(n, -1))
+
+    y_low, y_high, base = before, after, bins
+    if not relay:
+        y_low = lax.ppermute(up[bins:], "gy", ring(ny, 1))
+        y_high = lax.ppermute(down[bins:], "gy", ring(ny, -1))
+        base = 0
     around, part = call(
-        functools.partial(stencil_body, n),
+        functools.partial(stencil_body, n, base),
         [(3, cx + 4, 2 * cy, 2 * cz), (3, cx, cy, cz)],
         [VMEM] * 6,
         [pltpu.VMEM((LANES, LANES), F32), pltpu.VMEM((3, cx + 2, 2 * cy, 2 * cz), F32)],
@@ -597,11 +606,11 @@
     positions_out, velocities_out = call(
         functools.partial(second_body, n),
         [positions.shape, velocities.shape],
-        [VMEM] * 4 + [ANY] * 3,
+        [VMEM] * 4 + [HBM] * 3,
         pair_scratch
         + [pltpu.VMEM((bins, LANES), F32), pltpu.VMEM((bins, 8, LANES), F32)]
         + scalars,
-    )(moved, before, after, replies, counts, offset, mask)
+    )(moved, before, after, replies, *[pltpu.with_memory_space_constraint(v, pltpu.HBM) for v in (counts, offset, mask)])
     lanes = bins * n
     planes = (cx + 2) * 2 * cy
     (fluid_out,) = call(

time: 49.6 us -> 48.6 us (0.980)
  starting transfers between devices: 26 us -> 22.1 us
  waiting for transfers between devices: 11.1 us -> 14.1 us
  local copies, waits for them, and re-layouts: 0.67 us -> 0.01 us
    ppermute x1, waiting for transfers between devices: 0.01 us -> 4.65 us  [step(): before = lax.ppermute(moved, AXES, ring(n, 1))]
    ppermute x5 -> x3, starting transfers between devices: 14.4 us -> 10.5 us  [the longest x1 5.25 us: step(): after = lax.ppermute(down, AXES, ring(n, -1))]
    ppermute x5 -> x3, waiting for transfers between devices: 9.53 us -> 7.92 us  [the longest x1 5.9 us: step(): before = lax.ppermute(up, AXES, ring(n, 1))]
    unnamed x8 -> x2, local copies, waits for them, and re-layouts: 0.67 us -> 0.01 us
    pallas_call x4 -> x3, Pallas kernels: 5.03 us -> 5.32 us  [the longest x1 2.98 us: step(): call(functools.partial(first_body, n), [(bins + face_blocks, 8, LANES)] *...]
  transfers between devices with their start and end apart: 10 -> 8, of which waited for: 4 -> 4; matrix products, arithmetic and copies ran while one was open for 0% -> 0% of each run, Pallas kernels for 7% -> 7%
where the time goes in v3:
time: 48.6 us; the launch traced here: 48.2 us
  starting transfers between devices  22.1 us (45%)
  waiting for transfers between devices  14.1 us (29%)
  Pallas kernels  11.3 us (23%)
  between operations  0.71 us (1%)
    all_to_all x1, starting transfers between devices, step(): ids = lax.all_to_all(send, AXES, 0, 0, tiled=True)  7.33 us
    ppermute x1, waiting for transfers between devices, step(): before = lax.ppermute(up, AXES, ring(n, 1))  5.9 us
    ppermute x1, starting transfers between devices, step(): after = lax.ppermute(down, AXES, ring(n, -1))  5.25 us
    ppermute x1, starting transfers between devices, step(): after = lax.ppermute(moved_down, AXES, ring(n, -1))  5.25 us
    ppermute x1, waiting for transfers between devices, step(): before = lax.ppermute(moved, AXES, ring(n, 1))  4.65 us
    pallas_call x1, Pallas kernels, step(): call(functools.partial(second_body, n), [positions.shape, velocities.shap...  3.41 us
    pallas_call x1, Pallas kernels, step(): call(functools.partial(first_body, n), [(bins + face_blocks, 8, LANES)] *...  2.98 us
    all_to_all x1, starting transfers between devices, step(): replies = lax.all_to_all(send, AXES, 0, 0, tiled=True)  2.55 us
  transfers between devices with their start and end apart: 8, of which 4 were waited for; matrix products, arithmetic and copies ran while one was open for 0% of the time, Pallas kernels for 7%

profile of v3, /device:TPU:0, one launch (start us, length us, event | category | flops | bytes accessed | tf_op | source)
XLA Modules:
  0.0 48.2 jit_solution(1325608231506690663)
XLA Ops:
  0.6 1.9 %shard_map.112 = (f32[19,8,128]{2,1,0:T(8,128)S(1)}, f32[19,8,128]{2,1,0:T(8,128)S(1)}, f32[32,8,128]{2,1,0:T(8,128)}, f32[3,2,8,128]{3,2,1,0:T(8,128)S(1)}, f32[3,2,8,128]{3,2,1,0:T(8,128)S(1)}) custom-call(f32[3,16,128]{2,1,0:T(8,128)} %refs_0_.3, f32[3,16,128]{2,1,0:T(8,128)} %refs_1_.1, f32[16,128]{1,0:T(8,128)} %refs_2_.1, f32[3,4,8,128]{3,2,1,0:T(8,128)} %fluid.3, ...), custom_call_target="tpu_custom_call" | custom-call | tf_op jit(solution)/shard_map/pallas_call | solution.py:548
  2.5 7.3 %all-to-all-start = ((f32[32,8,128]{2,1,0:T(8,128)}), f32[32,8,128]{2,1,0:T(8,128)S(1)}, u32[]{:S(2)}, u32[]{:S(2)}) async-start(f32[32,8,128]{2,1,0:T(8,128)} %get-tuple-element.19), calls=%async_computation | async-start | bytes 262144 | tf_op jit(solution)/shard_map/all_to_all | solution.py:566
  9.8 5.2 %collective-permute-start.1 = (f32[19,8,128]{2,1,0:T(8,128)S(1)}, f32[19,8,128]{2,1,0:T(8,128)S(1)}, u32[]{:S(2)}, u32[]{:S(2)}) collective-permute-start(f32[19,8,128]{2,1,0:T(8,128)S(1)} %get-tuple-element.16), channel_id=1, source_target_pairs={{0,31},{1,0},{2,1},{3,2},{4,3},{5,4},{6,5},{7,6},{8,7},{9,8},{10,9... | collective-permute-start | bytes 233480 | tf_op jit(solution)/shard_map/ppermute | solution.py:568
  15.1 0.0 collective-permute-start
  15.1 2.0 %collective-permute-done.1.after = f32[19,8,128]{2,1,0:T(8,128)S(1)} collective-permute-done((f32[19,8,128]{2,1,0:T(8,128)S(1)}, f32[19,8,128]{2,1,0:T(8,128)S(1)}, u32[]{:S(2)}, u32[]{:S(2)}) %collective-permute-start.1) | collective-permute-done | bytes 77856 | tf_op jit(solution)/shard_map/ppermute | solution.py:568
  17.1 5.9 %collective-permute-done.before = f32[19,8,128]{2,1,0:T(8,128)S(1)} collective-permute-done((f32[19,8,128]{2,1,0:T(8,128)S(1)}, f32[19,8,128]{2,1,0:T(8,128)S(1)}, u32[]{:S(2)}, u32[]{:S(2)}) %collective-permute-start) | collective-permute-done | bytes 77856 | tf_op jit(solution)/shard_map/ppermute | solution.py:567
  23.0 0.0 copy-start
  23.0 3.0 %shard_map.113 = (f32[19,8,128]{2,1,0:T(8,128)S(1)}, f32[19,8,128]{2,1,0:T(8,128)S(1)}, f32[8,128]{1,0:T(8,128)S(1)}) custom-call(f32[19,8,128]{2,1,0:T(8,128)S(1)} %get-tuple-element.15.own, f32[19,8,128]{2,1,0:T(8,128)S(1)} %collective-permute-done.before, f32[19,8,128]{2,1,0:T(8,128)S(1)} %collective-permute-done.1.after, s32[16]{0:T(128)} %refs_0_.5, ...), custom_call_target="tpu_custom_call" | custom-call | tf_op jit(solution)/shard_map/pallas_call | solution.py:582
  26.0 0.0 all-to-all-done.recv.ids
  26.0 0.0 copy-done
  26.0 1.2 %shard_map.114 = f32[32,4,128]{2,1,0:T(4,128)} custom-call(f32[32,8,128]{2,1,0:T(8,128)S(1)} %all-to-all-done.recv.ids, f32[3,4,8,128]{3,2,1,0:T(8,128)S(1)} %copy-done, f32[8,128]{1,0:T(8,128)S(1)} %get-tuple-element.20.deposit), custom_call_target="tpu_custom_call" | custom-call | tf_op jit(solution)/shard_map/pallas_call | solution.py:588
  27.2 2.6 %all-to-all-start.1 = ((f32[32,4,128]{2,1,0:T(4,128)}), f32[32,4,128]{2,1,0:T(4,128)S(1)}, u32[]{:S(2)}, u32[]{:S(2)}) async-start(f32[32,4,128]{2,1,0:T(4,128)} %shard_map.114), calls=%async_computation.1 | async-start | bytes 131072 | tf_op jit(solution)/shard_map/all_to_all | solution.py:591
  29.8 5.2 %collective-permute-start.3 = (f32[19,8,128]{2,1,0:T(8,128)S(1)}, f32[19,8,128]{2,1,0:T(8,128)S(1)}, u32[]{:S(2)}, u32[]{:S(2)}) collective-permute-start(f32[19,8,128]{2,1,0:T(8,128)S(1)} %get-tuple-element.18), channel_id=1, source_target_pairs={{0,31},{1,0},{2,1},{3,2},{4,3},{5,4},{6,5},{7,6},{8,7},{9,8},{10,9... | collective-permute-start | bytes 233480 | tf_op jit(solution)/shard_map/ppermute | solution.py:593
  35.0 0.0 collective-permute-start.2
  35.0 0.0 collective-permute-start.4
  35.0 1.7 %collective-permute-start.5 = (f32[3,2,8,128]{3,2,1,0:T(8,128)S(1)}, f32[3,2,8,128]{3,2,1,0:T(8,128)S(1)}, u32[]{:S(2)}, u32[]{:S(2)}) collective-permute-start(f32[3,2,8,128]{3,2,1,0:T(8,128)S(1)} %get-tuple-element.24), channel_id=1, source_target_pairs={{0,24},{8,0},{16,8},{24,16},{1,25},{9,1},{17,9},{25,17},{2,26},{10... | collective-permute-start | bytes 73736 | tf_op jit(solution)/shard_map/ppermute | solution.py:570
  36.8 1.5 %collective-permute-done.4.x_low = f32[3,2,8,128]{3,2,1,0:T(8,128)S(1)} collective-permute-done((f32[3,2,8,128]{3,2,1,0:T(8,128)S(1)}, f32[3,2,8,128]{3,2,1,0:T(8,128)S(1)}, u32[]{:S(2)}, u32[]{:S(2)}) %collective-permute-start.4) | collective-permute-done | bytes 24608 | tf_op jit(solution)/shard_map/ppermute | solution.py:569
  38.3 0.0 collective-permute-done.5.x_high
  38.3 0.0 collective-permute-done.3.after.y_high
  38.3 4.6 %collective-permute-done.2.before.y_low = f32[19,8,128]{2,1,0:T(8,128)S(1)} collective-permute-done((f32[19,8,128]{2,1,0:T(8,128)S(1)}, f32[19,8,128]{2,1,0:T(8,128)S(1)}, u32[]{:S(2)}, u32[]{:S(2)}) %collective-permute-start.2) | collective-permute-done | bytes 77856 | tf_op jit(solution)/shard_map/ppermute | solution.py:592
  42.9 0.5 shard_map.116
  43.4 0.0 all-to-all-done.1.recv
  43.4 3.4 %shard_map.115 = (f32[3,16,128]{2,1,0:T(8,128)}, f32[3,16,128]{2,1,0:T(8,128)}) custom-call(f32[19,8,128]{2,1,0:T(8,128)S(1)} %get-tuple-element.17.own, f32[19,8,128]{2,1,0:T(8,128)S(1)} %collective-permute-done.2.before.y_low, f32[19,8,128]{2,1,0:T(8,128)S(1)} %collective-permute-done.3.after.y_high, f32[32,4,128]{2,1,0:T(4,128)S(1)} %all-to-all-done.1.recv, ...), custom_call_target="tpu_custom_call" | custom-call | tf_op jit(solution)/shard_map/pallas_call | solution.py:606
  46.8 1.4 %shard_map.117 = f32[3,4,8,128]{3,2,1,0:T(8,128)} custom-call(f32[3,4,8,128]{3,2,1,0:T(8,128)S(1)} %get-tuple-element.25.part, f32[3,8,16,256]{3,2,1,0:T(8,128)S(1)} %get-tuple-element.26.around, f32[32,8,128]{2,1,0:T(8,128)S(1)} %all-to-all-done.recv.ids, f32[32,4,128]{2,1,0:T(4,128)S(1)} %all-to-all-done.1.recv), custom_call_target="tpu_custom_call" | custom-call | tf_op jit(solution)/shard_map/pallas_call | solution.py:616
Async XLA Ops:
  2.5 23.5 %all-to-all-start = ((f32[32,8,128]{2,1,0:T(8,128)}), f32[32,8,128]{2,1,0:T(8,128)S(1)}, u32[]{:S(2)}, u32[]{:S(2)}) async-start(f32[32,8,128]{2,1,0:T(8,128)} %get-tuple-element.19), calls=%async_computation | async-start | bytes 262144 | tf_op jit(solution)/shard_map/all_to_all | solution.py:566
  9.8 7.3 %collective-permute-start.1 = (f32[19,8,128]{2,1,0:T(8,128)S(1)}, f32[19,8,128]{2,1,0:T(8,128)S(1)}, u32[]{:S(2)}, u32[]{:S(2)}) collective-permute-start(f32[19,8,128]{2,1,0:T(8,128)S(1)} %get-tuple-element.16), channel_id=1, source_target_pairs={{0,31},{1,0},{2,1},{3,2},{4,3},{5,4},{6,5},{7,6},{8,7},{9,8},{10,9... | collective-permute-start | bytes 233480 | tf_op jit(solution)/shard_map/ppermute | solution.py:568
  15.1 7.9 %collective-permute-start = (f32[19,8,128]{2,1,0:T(8,128)S(1)}, f32[19,8,128]{2,1,0:T(8,128)S(1)}, u32[]{:S(2)}, u32[]{:S(2)}) collective-permute-start(f32[19,8,128]{2,1,0:T(8,128)S(1)} %get-tuple-element.15.own), channel_id=1, source_target_pairs={{0,1},{1,2},{2,3},{3,4},{4,5},{5,6},{6,7},{7,8},{8,9},{9,10},{10,1... | collective-permute-start | bytes 233480 | tf_op jit(solution)/shard_map/ppermute | solution.py:567
  23.0 3.0 %copy-start = (f32[3,4,8,128]{3,2,1,0:T(8,128)S(1)}, f32[3,4,8,128]{3,2,1,0:T(8,128)}, u32[]{:S(2)}) copy-start(f32[3,4,8,128]{3,2,1,0:T(8,128)} %fluid.3) | copy-start | bytes 147460
  27.2 16.2 %all-to-all-start.1 = ((f32[32,4,128]{2,1,0:T(4,128)}), f32[32,4,128]{2,1,0:T(4,128)S(1)}, u32[]{:S(2)}, u32[]{:S(2)}) async-start(f32[32,4,128]{2,1,0:T(4,128)} %shard_map.114), calls=%async_computation.1 | async-start | bytes 131072 | tf_op jit(solution)/shard_map/all_to_all | solution.py:591
  29.8 8.5 %collective-permute-start.3 = (f32[19,8,128]{2,1,0:T(8,128)S(1)}, f32[19,8,128]{2,1,0:T(8,128)S(1)}, u32[]{:S(2)}, u32[]{:S(2)}) collective-permute-start(f32[19,8,128]{2,1,0:T(8,128)S(1)} %get-tuple-element.18), channel_id=1, source_target_pairs={{0,31},{1,0},{2,1},{3,2},{4,3},{5,4},{6,5},{7,6},{8,7},{9,8},{10,9... | collective-permute-start | bytes 233480 | tf_op jit(solution)/shard_map/ppermute | solution.py:593
  35.0 7.9 %collective-permute-start.2 = (f32[19,8,128]{2,1,0:T(8,128)S(1)}, f32[19,8,128]{2,1,0:T(8,128)S(1)}, u32[]{:S(2)}, u32[]{:S(2)}) collective-permute-start(f32[19,8,128]{2,1,0:T(8,128)S(1)} %get-tuple-element.17.own), channel_id=1, source_target_pairs={{0,1},{1,2},{2,3},{3,4},{4,5},{5,6},{6,7},{7,8},{8,9},{9,10},{10,1... | collective-permute-start | bytes 233480 | tf_op jit(solution)/shard_map/ppermute | solution.py:592
  35.0 3.3 %collective-permute-start.4 = (f32[3,2,8,128]{3,2,1,0:T(8,128)S(1)}, f32[3,2,8,128]{3,2,1,0:T(8,128)S(1)}, u32[]{:S(2)}, u32[]{:S(2)}) collective-permute-start(f32[3,2,8,128]{3,2,1,0:T(8,128)S(1)} %get-tuple-element.23), channel_id=1, source_target_pairs={{0,8},{8,16},{16,24},{24,0},{1,9},{9,17},{17,25},{25,1},{2,10},{10... | collective-permute-start | bytes 73736 | tf_op jit(solution)/shard_map/ppermute | solution.py:569
  35.0 3.3 %collective-permute-start.5 = (f32[3,2,8,128]{3,2,1,0:T(8,128)S(1)}, f32[3,2,8,128]{3,2,1,0:T(8,128)S(1)}, u32[]{:S(2)}, u32[]{:S(2)}) collective-permute-start(f32[3,2,8,128]{3,2,1,0:T(8,128)S(1)} %get-tuple-element.24), channel_id=1, source_target_pairs={{0,24},{8,0},{16,8},{24,16},{1,25},{9,1},{17,9},{25,17},{2,26},{10... | collective-permute-start | bytes 73736 | tf_op jit(solution)/shard_map/ppermute | solution.py:570

commit v4 on v3

--- a/solution.py
+++ b/solution.py
@@ -55,15 +55,15 @@
     return high, middle, rest - middle
 
 
-def call(body, outs, ins, scratch=(), cost=None):
+def call(body, outs, ins, scratch=(), out_spec=None):
+    shapes = [out if isinstance(out[-1], type) else (out, F32) for out in outs]
     return pl.pallas_call(
         body,
-        out_shape=[jax.ShapeDtypeStruct(shape, F32) for shape in outs],
+        out_shape=[jax.ShapeDtypeStruct(shape, dtype) for shape, dtype in shapes],
         in_specs=ins,
-        out_specs=[VMEM] * len(outs),
+        out_specs=[out_spec or VMEM] * len(outs),
         scratch_shapes=scratch,
         compiler_params=pltpu.CompilerParams(vmem_limit_bytes=24 * 1024 * 1024),
-        cost_estimate=cost,
     )
 
 
@@ -98,13 +98,18 @@
 
 
 def prep_body(n, *refs):
-    sources, locals_, sems = refs[:7], refs[12:19], refs[19]
-    up, down, send, face_low, face_high = refs[7:12]
+    sources, locals_, sems = refs[:10], refs[16:26], refs[26]
+    up, down, send, face_low, face_high, table = refs[10:16]
     copies = fetch(sources, locals_, sems)
-    pos, vel, weights, fluid, counts, box, cell = locals_
+    pos, vel, weights, fluid, counts, box, cell, count_row, offset, mask = locals_
     for copy in copies:
         copy.wait()
     bins = pos.shape[1]
+    links = offset.shape[0]
+    table[...] = jnp.zeros(table.shape, jnp.int32)
+    table[0:1, 0:bins] = count_row[...]
+    table[1 : 1 + links, 0:bins] = offset[...]
+    table[1 + links : 1 + 2 * links, 0:bins] = mask[...]
     cx, cy, cz = fluid.shape[1:]
     lane = iota((8, LANES), 1)
     row = iota((8, LANES), 0)
@@ -225,30 +230,24 @@
     return jnp.concatenate([high, middle, high, middle, low, high], 0).astype(BF16)
 
 
-def pair_sums(d, n, bins, own_of, stack, weighted, offset, mask):
-    def exponents(k):
-        near = [bins + k]
+def pair_sums(d, n, bins, links, own_of, stack, weighted, highs, lows, table):
+    for k in range(bins):
+        near = [bins + k] + [bins + k + table[1 + q, k] for q in range(links)]
+        others = jnp.concatenate([stack[index] for index in near], 1)
+        kernel = jnp.exp2(tn(own_of(k), others))
+        high = kernel.astype(BF16)
+        highs[k] = high
+        lows[k] = (kernel - high.astype(F32)).astype(BF16)
+    sums = []
+    for k in range(bins):
         heavy = [bins + k]
-        for q in range(offset.shape[0]):
-            shift = offset[q, k]
-            near.append(bins + k + shift)
+        for q in range(links):
+            shift = table[1 + q, k]
             whole = d * bins + k + shift
-            linked = (mask[q, k] != 0) & (whole >= 0) & (whole < n * bins)
+            linked = (table[1 + links + q, k] != 0) & (whole >= 0) & (whole < n * bins)
             heavy.append(jnp.where(linked, bins + k + shift, 3 * bins))
-        others = jnp.concatenate([stack[index] for index in near], 1)
         masses = jnp.concatenate([weighted[index] for index in heavy], 1)
-        return tn(own_of(k), others), masses
-
-    sums = []
-    following = exponents(0)
-    for k in range(bins):
-        value, masses = following
-        if k + 1 < bins:
-            following = exponents(k + 1)
-        kernel = jnp.exp2(value)
-        high = kernel.astype(BF16)
-        low = (kernel - high.astype(F32)).astype(BF16)
-        turned = jnp.transpose(nt(high, masses) + nt(low, masses))
+        turned = jnp.transpose(nt(highs[k], masses) + nt(lows[k], masses))
         sums.append(turned[0:8] + turned[8:16])
     return sums
 
@@ -265,10 +264,10 @@
 
 
 def first_body(
-    n, own, before, after, *refs
+    n, links, own, before, after, *refs
 ):
-    copies = fetch(refs[0:3], refs[9:12], refs[12])
-    moved, moved_down, deposit, stack, weighted, norms, counts, offset, mask = refs[3:12]
+    copies = fetch(refs[0:1], refs[9:10], refs[10])
+    moved, moved_down, deposit, stack, weighted, highs, lows, norms, table = refs[1:10]
     bins = norms.shape[0]
     d = flat_id()
     row = iota((8, LANES), 0)
@@ -290,17 +289,19 @@
         d,
         n,
         bins,
+        links,
         lambda k: own_side(own[k], norms[k : k + 1, :], row),
         stack,
         weighted,
-        offset,
-        mask,
+        highs,
+        lows,
+        table,
     )
     total = jnp.zeros((8, LANES), F32)
     for k in range(bins):
         block = own[k]
         force = contact_force(block, sums[k])
-        occupied = jnp.where(lane < counts[k], step_sub, 0.0)
+        occupied = jnp.where(lane < table[0, k], step_sub, 0.0)
         new_vel = block + occupied * (force - drag_rate * block)
         new_pos = block + occupied * pltpu.roll(new_vel, 4, 0)
         result = jnp.where(row < 3, new_pos, jnp.where(row == 3, block, new_vel))
@@ -314,11 +315,12 @@
     deposit[...] = jnp.broadcast_to(jnp.sum(total, axis=0, keepdims=True), (8, LANES))
 
 
-def second_body(
-    n, own, before, after, recv, *refs
-):
-    copies = fetch(refs[0:3], refs[9:12], refs[12])
-    pos, vel, stack, weighted, norms, state, counts, offset, mask = refs[3:12]
+def final_body(n, links, own, before, after, recv, scalars, part, around, planes, depth, *refs):
+    outs, refs = refs[0:3], refs[3:]
+    stack, weighted, highs, lows, norms, state, table, pos, vel, fluid = refs[0:10]
+    copies = fetch([scalars], [table], refs[10])
+    deposit(n, norms.shape[0], part, around, planes, depth, recv, fluid, *refs[12:15])
+    written = fetch([fluid], outs[2:3], refs[11].at[2:3])
     bins = norms.shape[0]
     d = flat_id()
     row = iota((8, LANES), 0)
@@ -345,7 +347,7 @@
     for copy in copies:
         copy.wait()
     for k in range(bins):
-        block = own[k] + jnp.where(lane < counts[k], push(1, k)[0], 0.0)
+        block = own[k] + jnp.where(lane < table[0, k], push(1, k)[0], 0.0)
         state[k] = block
         norms[k : k + 1, :] = load_block(block, row, bins + k, stack, weighted)
     weighted[3 * bins] = jnp.zeros((16, LANES), BF16)
@@ -353,22 +355,27 @@
         d,
         n,
         bins,
+        links,
         lambda k: own_side(state[k], norms[k : k + 1, :], row),
         stack,
         weighted,
-        offset,
-        mask,
+        highs,
+        lows,
+        table,
     )
     for k in range(bins):
         block = state[k]
         force = contact_force(block, sums[k])
-        occupied = jnp.where(lane < counts[k], step_sub, 0.0)
+        occupied = jnp.where(lane < table[0, k], step_sub, 0.0)
         fluid_seen = push(1, k)[1]
         new_vel = block + occupied * (force + drag_rate * (fluid_seen - block))
         new_pos = block + occupied * pltpu.roll(new_vel, 4, 0)
         for c in range(3):
             pos[c, k : k + 1, :] = new_pos[c : c + 1]
             vel[c, k : k + 1, :] = new_vel[c + 4 : c + 5]
+    written += fetch([pos, vel], outs[0:2], refs[11])
+    for copy in written:
+        copy.wait()
 
 
 def laplace(at, x):
@@ -381,7 +388,7 @@
 
 
 def stencil_body(
-    n, base, fluid, x_low, x_high, y_low, y_high, recv, around, part, faces, rates
+    n, bins, base, fluid, x_low, x_high, y_low, y_high, recv, around, part, planes, depth, faces, rates
 ):
     cx, cy, cz = fluid.shape[1:]
     tall, wide = 2 * cy, 2 * cz
@@ -468,61 +475,69 @@
             again = laplace(lambda i: rates[c, i + 1], x)
             total = around[c, x] + rates[c, x + 1] + 0.5 * again
             part[c, x] = total[0:cy, 0:cz]
-
-
-def deposit_body(n, bins, part, around, ids, recv, out, table, low_table, depth, field):
-    cx, cy, cz = part.shape[1:]
-    deep = cx + 4
+    locate(n, bins, (cx, cy, cz), recv, planes, depth)
+
+
+def packed(n, ref, which):
+    groups = LANES // n
+    rows = [ref[:, which, :]]
+    if n < LANES:
+        rows.append(jnp.zeros((LANES - n, LANES), F32))
+    turned = jnp.transpose(jnp.concatenate(rows, 0))
+    span = LANES // groups
+    total = turned[0:span]
+    for g in range(1, groups):
+        total = total + pltpu.roll(turned[g * span : (g + 1) * span], g * n, 1)
+    return total
+
+
+def locate(n, bins, sizes, ids, planes, depth):
+    cx, cy, cz = sizes
     tall, wide = 2 * cy, 2 * cz
-    groups = LANES // n
-    per_group = bins // groups
-    planes = (cx + 2) * tall
-
-    def packed(ref, which):
-        turned = jnp.transpose(
-            jnp.concatenate(
-                [ref[:, which, :]] + ([jnp.zeros((LANES - n, LANES), F32)] if n < LANES else []), 0
-            )
-        )
-        span = LANES // groups
-        total = turned[0:span]
-        for g in range(1, groups):
-            total = total + pltpu.roll(turned[g * span : (g + 1) * span], g * n, 1)
-        return total
-
-    where = packed(ids, 0)
-    loads = packed(recv, 3)
+    per_group = bins // (LANES // n)
+    where = packed(n, ids, 0)
     x = where[0:per_group] - (lax.axis_index("gx") * cx - 1).astype(F32)
     y = where[per_group : 2 * per_group] - (lax.axis_index("gy") * cy).astype(F32)
     z = where[2 * per_group : 3 * per_group] - (lax.axis_index("gz") * cz).astype(F32)
     near = (x >= 0) & (x < cx + 2) & (y >= -1) & (y <= cy) & (z >= -1) & (z <= cz)
     y = jnp.where(y < 0, y + tall, y)
     z = jnp.where(z < 0, z + wide, z)
-    plane_code = jnp.where(near, x * tall + y, -1.0).astype(jnp.int32)
+    planes[...] = jnp.where(near, x * tall + y, -1.0)
     depth_code = jnp.where(near, z, -1.0).astype(jnp.int32)
-    plane_row = iota((planes, LANES), 0)
     depth_row = iota((wide, LANES), 0)
+    for r in range(per_group):
+        depth[:, r * LANES : (r + 1) * LANES] = jnp.where(
+            depth_code[r : r + 1] == depth_row, 1.0, 0.0
+        ).astype(BF16)
+
+
+def deposit(n, bins, part, around, planes, depth, recv, out, table, low_table, field):
+    cx, cy, cz = part.shape[1:]
+    deep = cx + 4
+    tall = 2 * cy
+    per_group = bins // (LANES // n)
+    count = (cx + 2) * tall
+    loads = packed(n, recv, 3)
+    plane_code = planes[...].astype(jnp.int32)
+    plane_row = iota((count, LANES), 0)
     for r in range(per_group):
         at = r * LANES
         hit = plane_code[r : r + 1] == plane_row
         for f in range(4):
             load = loads[f * per_group + r : f * per_group + r + 1]
             high, low = pieces_2(load)
-            table[f * planes : (f + 1) * planes, at : at + LANES] = jnp.where(
+            table[f * count : (f + 1) * count, at : at + LANES] = jnp.where(
                 hit, high, 0.0
             ).astype(BF16)
-            low_table[f * planes : (f + 1) * planes, at : at + LANES] = jnp.where(
+            low_table[f * count : (f + 1) * count, at : at + LANES] = jnp.where(
                 hit, low, 0.0
             ).astype(BF16)
-        depth[:, at : at + LANES] = jnp.where(
-            depth_code[r : r + 1] == depth_row, 1.0, 0.0
-        ).astype(BF16)
     spread = nt(table[...], depth[...]) + nt(low_table[...], depth[...])
     factor = coupling * drag_rate * (2.0 - step_sub * drag_rate)
     for c in range(3):
         for i in range(cx + 2):
-            moment = spread[c * planes + i * tall : c * planes + (i + 1) * tall]
-            mass = spread[3 * planes + i * tall : 3 * planes + (i + 1) * tall]
+            moment = spread[c * count + i * tall : c * count + (i + 1) * tall]
+            mass = spread[3 * count + i * tall : 3 * count + (i + 1) * tall]
             field[c, i] = (coupling * drag_rate) * moment - factor * around[
                 c, (i - 1) % deep
             ] * mass
@@ -545,10 +560,14 @@
     face_blocks = -(-6 * cx // 8)
     relay = lax.axis_size("gz") == 2
 
-    up, down, send, face_low, face_high = call(
+    links = offset.shape[0]
+    up, down, send, face_low, face_high, table = call(
         functools.partial(prep_body, n),
-        [(bins + face_blocks, 8, LANES)] * 2 + [(n, 8, LANES)] + [(3, 2, cy, cz)] * 2,
-        [HBM] * 7,
+        [(bins + face_blocks, 8, LANES)] * 2
+        + [(n, 8, LANES)]
+        + [(3, 2, cy, cz)] * 2
+        + [((8, LANES), jnp.int32)],
+        [HBM] * 10,
         [
             pltpu.VMEM(positions.shape, F32),
             pltpu.VMEM(velocities.shape, F32),
@@ -557,12 +576,28 @@
             pltpu.SMEM((bins,), jnp.int32),
             pltpu.SMEM((bins,), jnp.int32),
             pltpu.SMEM((bins,), jnp.int32),
-            pltpu.SemaphoreType.DMA((7,)),
+            pltpu.VMEM((1, bins), jnp.int32),
+            pltpu.VMEM(offset.shape, jnp.int32),
+            pltpu.VMEM(mask.shape, jnp.int32),
+            pltpu.SemaphoreType.DMA((10,)),
         ],
-    )(*[
-        pltpu.with_memory_space_constraint(value, pltpu.HBM)
-        for value in (positions, velocities, weights, fluid, counts, bin_box[:, 0], bin_cell)
-    ])
+    )(
+        *[
+            pltpu.with_memory_space_constraint(value, pltpu.HBM)
+            for value in (
+                positions,
+                velocities,
+                weights,
+                fluid,
+                counts,
+                bin_box[:, 0],
+                bin_cell,
+                counts[None],
+                offset,
+                mask,
+            )
+        ]
+    )
     ids = lax.all_to_all(send, AXES, 0, 0, tiled=True)
     before = lax.ppermute(up, AXES, ring(n, 1))
     after = lax.ppermute(down, AXES, ring(n, -1))
@@ -572,21 +607,21 @@
     pair_scratch = [
         pltpu.VMEM((3 * bins + 1, 48, LANES), BF16),
         pltpu.VMEM((3 * bins + 1, 16, LANES), BF16),
+        pltpu.VMEM((bins, LANES, (offset.shape[0] + 1) * LANES), BF16),
+        pltpu.VMEM((bins, LANES, (offset.shape[0] + 1) * LANES), BF16),
     ]
-    scalars = [
-        pltpu.SMEM((bins,), jnp.int32),
-        pltpu.SMEM(offset.shape, jnp.int32),
-        pltpu.SMEM(mask.shape, jnp.int32),
-        pltpu.SemaphoreType.DMA((3,)),
-    ]
-    moved, moved_down, deposit = call(
-        functools.partial(first_body, n),
+    held = [pltpu.SMEM((8, LANES), jnp.int32)]
+    moved, moved_down, deposits = call(
+        functools.partial(first_body, n, links),
         [(bins + face_blocks, 8, LANES)] * 2 + [(8, LANES)],
-        [VMEM] * 3 + [HBM] * 3,
-        pair_scratch + [pltpu.VMEM((bins, LANES), F32)] + scalars,
-    )(up, before, after, *[pltpu.with_memory_space_constraint(v, pltpu.HBM) for v in (counts, offset, mask)])
+        [VMEM] * 4,
+        pair_scratch
+        + [pltpu.VMEM((bins, LANES), F32)]
+        + held
+        + [pltpu.SemaphoreType.DMA((1,))],
+    )(up, before, after, table)
     (send,) = call(functools.partial(gather_body, n, bins), [(n, 4, LANES)], [VMEM] * 3)(
-        ids, fluid, deposit
+        ids, fluid, deposits
     )
     replies = lax.all_to_all(send, AXES, 0, 0, tiled=True)
     before = lax.ppermute(moved, AXES, ring(n, 1))
@@ -597,33 +632,34 @@
         y_low = lax.ppermute(up[bins:], "gy", ring(ny, 1))
         y_high = lax.ppermute(down[bins:], "gy", ring(ny, -1))
         base = 0
-    around, part = call(
-        functools.partial(stencil_body, n, base),
-        [(3, cx + 4, 2 * cy, 2 * cz), (3, cx, cy, cz)],
+    lanes = bins * n
+    per_group = bins // (LANES // n)
+    around, part, planes, depth = call(
+        functools.partial(stencil_body, n, bins, base),
+        [(3, cx + 4, 2 * cy, 2 * cz), (3, cx, cy, cz), (per_group, LANES), ((2 * cz, lanes), BF16)],
         [VMEM] * 6,
         [pltpu.VMEM((LANES, LANES), F32), pltpu.VMEM((3, cx + 2, 2 * cy, 2 * cz), F32)],
     )(fluid, x_low, x_high, y_low, y_high, ids)
-    positions_out, velocities_out = call(
-        functools.partial(second_body, n),
-        [positions.shape, velocities.shape],
-        [VMEM] * 4 + [HBM] * 3,
+    count = (cx + 2) * 2 * cy
+    positions_out, velocities_out, fluid_out = call(
+        functools.partial(final_body, n, links),
+        [positions.shape, velocities.shape, fluid.shape],
+        [VMEM] * 9,
         pair_scratch
         + [pltpu.VMEM((bins, LANES), F32), pltpu.VMEM((bins, 8, LANES), F32)]
-        + scalars,
-    )(moved, before, after, replies, *[pltpu.with_memory_space_constraint(v, pltpu.HBM) for v in (counts, offset, mask)])
-    lanes = bins * n
-    planes = (cx + 2) * 2 * cy
-    (fluid_out,) = call(
-        functools.partial(deposit_body, n, bins),
-        [fluid.shape],
-        [VMEM] * 4,
-        [
-            pltpu.VMEM((4 * planes, lanes), BF16),
-            pltpu.VMEM((4 * planes, lanes), BF16),
-            pltpu.VMEM((2 * cz, lanes), BF16),
+        + held
+        + [
+            pltpu.VMEM(positions.shape, F32),
+            pltpu.VMEM(velocities.shape, F32),
+            pltpu.VMEM(fluid.shape, F32),
+            pltpu.SemaphoreType.DMA((1,)),
+            pltpu.SemaphoreType.DMA((3,)),
+            pltpu.VMEM((4 * count, lanes), BF16),
+            pltpu.VMEM((4 * count, lanes), BF16),
             pltpu.VMEM((3, cx + 2, 2 * cy, 2 * cz), F32),
         ],
-    )(part, around, ids, replies)
+        HBM,
+    )(moved, before, after, replies, table, part, around, planes, depth)
     return positions_out, velocities_out, fluid_out
 
 

time: 48.6 us -> 42 us (0.86)
  the two profiles are of different devices: /device:TPU:0 before, /device:TPU:1 now
where the time goes in v4:
time: 42 us; the launch traced here: 41.7 us
  starting transfers between devices  22.9 us (55%)
  Pallas kernels  10.1 us (24%)
  waiting for transfers between devices  7.98 us (19%)
  between operations  0.7 us (2%)
    all_to_all x1, starting transfers between devices, step(): ids = lax.all_to_all(send, AXES, 0, 0, tiled=True)  7.09 us
    ppermute x1, waiting for transfers between devices, step(): before = lax.ppermute(up, AXES, ring(n, 1))  4.72 us
    all_to_all x1, starting transfers between devices, step(): replies = lax.all_to_all(send, AXES, 0, 0, tiled=True)  4.23 us
    pallas_call x1, Pallas kernels, step(): call(functools.partial(final_body, n, links), [positions.shape, velocitie...  3.76 us
    ppermute x1, starting transfers between devices, step(): after = lax.ppermute(down, AXES, ring(n, -1))  3.13 us
    ppermute x1, starting transfers between devices, step(): after = lax.ppermute(moved_down, AXES, ring(n, -1))  3.13 us
    pallas_call x1, Pallas kernels, step(): call(functools.partial(first_body, n, links), [(bins + face_blocks, 8, LA...  2.61 us
    ppermute x1, starting transfers between devices, step(): x_low = lax.ppermute(face_high, 'gx', ring(nx, 1))  2.49 us
  transfers between devices with their start and end apart: 8, of which 3 were waited for; matrix products, arithmetic and copies ran while one was open for 0% of the time, Pallas kernels for 8%

profile of v4, /device:TPU:1, one launch (start us, length us, event | category | flops | bytes accessed | tf_op | source)
XLA Modules:
  0.0 41.7 jit_solution(8528095850931606854)
XLA Ops:
  0.6 1.9 %shard_map.112 = (f32[19,8,128]{2,1,0:T(8,128)S(1)}, f32[19,8,128]{2,1,0:T(8,128)S(1)}, f32[32,8,128]{2,1,0:T(8,128)}, f32[3,2,8,128]{3,2,1,0:T(8,128)S(1)}, f32...) custom-call(f32[3,16,128]{2,1,0:T(8,128)} %refs_0_.1, f32[3,16,128]{2,1,0:T(8,128)} %refs_1_.1, f32[16,128]{1,0:T(8,128)} %refs_2_.1, ...), custom_call_target="tpu_custom_call" | custom-call | tf_op jit(solution)/shard_map/pallas_call | solution.py:564
  2.5 7.1 %all-to-all-start = ((f32[32,8,128]{2,1,0:T(8,128)}), f32[32,8,128]{2,1,0:T(8,128)S(1)}, u32[]{:S(2)}, u32[]{:S(2)}) async-start(f32[32,8,128]{2,1,0:T(8,128)} %get-tuple-element.21), calls=%async_computation | async-start | bytes 262144 | tf_op jit(solution)/shard_map/all_to_all | solution.py:601
  9.6 1.4 %collective-permute-start = (f32[19,8,128]{2,1,0:T(8,128)S(1)}, f32[19,8,128]{2,1,0:T(8,128)S(1)}, u32[]{:S(2)}, u32[]{:S(2)}) collective-permute-start(f32[19,8,128]{2,1,0:T(8,128)S(1)} %get-tuple-element.16.own), channel_id=1, source_target_pairs={{0,1},{1,2},{2,3},{3,4},{4,5},{5,6},{6,7},{7,8},{8,9},{9,10},{10,1... | collective-permute-start | bytes 233480 | tf_op jit(solution)/shard_map/ppermute | solution.py:602
  11.1 3.1 %collective-permute-start.1 = (f32[19,8,128]{2,1,0:T(8,128)S(1)}, f32[19,8,128]{2,1,0:T(8,128)S(1)}, u32[]{:S(2)}, u32[]{:S(2)}) collective-permute-start(f32[19,8,128]{2,1,0:T(8,128)S(1)} %get-tuple-element.17), channel_id=1, source_target_pairs={{0,31},{1,0},{2,1},{3,2},{4,3},{5,4},{6,5},{7,6},{8,7},{9,8},{10,9... | collective-permute-start | bytes 233480 | tf_op jit(solution)/shard_map/ppermute | solution.py:603
  14.2 4.7 %collective-permute-done.before = f32[19,8,128]{2,1,0:T(8,128)S(1)} collective-permute-done((f32[19,8,128]{2,1,0:T(8,128)S(1)}, f32[19,8,128]{2,1,0:T(8,128)S(1)}, u32[]{:S(2)}, u32[]{:S(2)}) %collective-permute-start) | collective-permute-done | bytes 77856 | tf_op jit(solution)/shard_map/ppermute | solution.py:602
  18.9 0.0 collective-permute-done.1.after
  18.9 0.0 copy-start
  18.9 2.6 %shard_map.113 = (f32[19,8,128]{2,1,0:T(8,128)S(1)}, f32[19,8,128]{2,1,0:T(8,128)S(1)}, f32[8,128]{1,0:T(8,128)S(1)}) custom-call(f32[19,8,128]{2,1,0:T(8,128)S(1)} %get-tuple-element.16.own, f32[19,8,128]{2,1,0:T(8,128)S(1)} %collective-permute-done.before, f32[19,8,128]{2,1,0:T(8,128)S(1)} %collective-permute-done.1.after, ...), custom_call_target="tpu_custom_call" | custom-call | tf_op jit(solution)/shard_map/pallas_call | solution.py:614
  21.5 0.0 all-to-all-done.recv
  21.5 0.0 copy-done
  21.5 1.2 %shard_map.114 = f32[32,4,128]{2,1,0:T(4,128)} custom-call(f32[32,8,128]{2,1,0:T(8,128)S(1)} %all-to-all-done.recv, f32[3,4,8,128]{3,2,1,0:T(8,128)S(1)} %copy-done, f32[8,128]{1,0:T(8,128)S(1)} %get-tuple-element.22.deposit), custom_call_target="tpu_custom_call" | custom-call | tf_op jit(solution)/shard_map/pallas_call | solution.py:623
  22.7 4.2 %all-to-all-start.1 = ((f32[32,4,128]{2,1,0:T(4,128)}), f32[32,4,128]{2,1,0:T(4,128)S(1)}, u32[]{:S(2)}, u32[]{:S(2)}) async-start(f32[32,4,128]{2,1,0:T(4,128)} %shard_map.114), calls=%async_computation.1 | async-start | bytes 131072 | tf_op jit(solution)/shard_map/all_to_all | solution.py:626
  26.9 1.4 %collective-permute-start.2 = (f32[19,8,128]{2,1,0:T(8,128)S(1)}, f32[19,8,128]{2,1,0:T(8,128)S(1)}, u32[]{:S(2)}, u32[]{:S(2)}) collective-permute-start(f32[19,8,128]{2,1,0:T(8,128)S(1)} %get-tuple-element.19.own), channel_id=1, source_target_pairs={{0,1},{1,2},{2,3},{3,4},{4,5},{5,6},{6,7},{7,8},{8,9},{9,10},{10,1... | collective-permute-start | bytes 233480 | tf_op jit(solution)/shard_map/ppermute | solution.py:627
  28.4 3.1 %collective-permute-start.3 = (f32[19,8,128]{2,1,0:T(8,128)S(1)}, f32[19,8,128]{2,1,0:T(8,128)S(1)}, u32[]{:S(2)}, u32[]{:S(2)}) collective-permute-start(f32[19,8,128]{2,1,0:T(8,128)S(1)} %get-tuple-element.20), channel_id=1, source_target_pairs={{0,31},{1,0},{2,1},{3,2},{4,3},{5,4},{6,5},{7,6},{8,7},{9,8},{10,9... | collective-permute-start | bytes 233480 | tf_op jit(solution)/shard_map/ppermute | solution.py:628
  31.5 2.5 %collective-permute-start.4 = (f32[3,2,8,128]{3,2,1,0:T(8,128)S(1)}, f32[3,2,8,128]{3,2,1,0:T(8,128)S(1)}, u32[]{:S(2)}, u32[]{:S(2)}) collective-permute-start(f32[3,2,8,128]{3,2,1,0:T(8,128)S(1)} %get-tuple-element.23), channel_id=1, source_target_pairs={{0,8},{8,16},{16,24},{24,0},{1,9},{9,17},{17,25},{25,1},{2,10},{10... | collective-permute-start | bytes 73736 | tf_op jit(solution)/shard_map/ppermute | solution.py:604
  34.0 0.0 collective-permute-start.5
  34.0 0.9 %collective-permute-done.4.x_low = f32[3,2,8,128]{3,2,1,0:T(8,128)S(1)} collective-permute-done((f32[3,2,8,128]{3,2,1,0:T(8,128)S(1)}, f32[3,2,8,128]{3,2,1,0:T(8,128)S(1)}, u32[]{:S(2)}, u32[]{:S(2)}) %collective-permute-start.4) | collective-permute-done | bytes 24608 | tf_op jit(solution)/shard_map/ppermute | solution.py:604
  34.9 2.3 %collective-permute-done.5.x_high = f32[3,2,8,128]{3,2,1,0:T(8,128)S(1)} collective-permute-done((f32[3,2,8,128]{3,2,1,0:T(8,128)S(1)}, f32[3,2,8,128]{3,2,1,0:T(8,128)S(1)}, u32[]{:S(2)}, u32[]{:S(2)}) %collective-permute-start.5) | collective-permute-done | bytes 24608 | tf_op jit(solution)/shard_map/ppermute | solution.py:605
  37.2 0.0 collective-permute-done.2.y_low.before
  37.2 0.0 collective-permute-done.3.y_high.after
  37.2 0.7 %shard_map.115 = (f32[3,8,16,256]{3,2,1,0:T(8,128)S(1)}, f32[3,4,8,128]{3,2,1,0:T(8,128)S(1)}, f32[4,128]{1,0:T(4,128)S(1)}, bf16[256,512]{1,0:T(8,128)(2,1)S(1)}) custom-call(f32[3,4,8,128]{3,2,1,0:T(8,128)S(1)} %copy-done, f32[3,2,8,128]{3,2,1,0:T(8,128)S(1)} %collective-permute-done.4.x_low, f32[3,2,8,128]{3,2,1,0:T(8,128)S(1)} %collective-permute-done.5.x_high, ...), custom_call_target="tpu_custom_call" | custom-call | tf_op jit(solution)/shard_map/pallas_call | solution.py:637
  37.9 0.0 all-to-all-done.1.recv
  37.9 3.8 %shard_map.116 = (f32[3,16,128]{2,1,0:T(8,128)}, f32[3,16,128]{2,1,0:T(8,128)}, f32[3,4,8,128]{3,2,1,0:T(8,128)}) custom-call(f32[19,8,128]{2,1,0:T(8,128)S(1)} %get-tuple-element.19.own, f32[19,8,128]{2,1,0:T(8,128)S(1)} %collective-permute-done.2.y_low.before, f32[19,8,128]{2,1,0:T(8,128)S(1)} %collective-permute-done.3.y_high.after, ...), custom_call_target="tpu_custom_call" | custom-call | tf_op jit(solution)/shard_map/pallas_call | solution.py:644
Async XLA Ops:
  2.5 19.0 %all-to-all-start = ((f32[32,8,128]{2,1,0:T(8,128)}), f32[32,8,128]{2,1,0:T(8,128)S(1)}, u32[]{:S(2)}, u32[]{:S(2)}) async-start(f32[32,8,128]{2,1,0:T(8,128)} %get-tuple-element.21), calls=%async_computation | async-start | bytes 262144 | tf_op jit(solution)/shard_map/all_to_all | solution.py:601
  9.6 9.3 %collective-permute-start = (f32[19,8,128]{2,1,0:T(8,128)S(1)}, f32[19,8,128]{2,1,0:T(8,128)S(1)}, u32[]{:S(2)}, u32[]{:S(2)}) collective-permute-start(f32[19,8,128]{2,1,0:T(8,128)S(1)} %get-tuple-element.16.own), channel_id=1, source_target_pairs={{0,1},{1,2},{2,3},{3,4},{4,5},{5,6},{6,7},{7,8},{8,9},{9,10},{10,1... | collective-permute-start | bytes 233480 | tf_op jit(solution)/shard_map/ppermute | solution.py:602
  11.1 7.9 %collective-permute-start.1 = (f32[19,8,128]{2,1,0:T(8,128)S(1)}, f32[19,8,128]{2,1,0:T(8,128)S(1)}, u32[]{:S(2)}, u32[]{:S(2)}) collective-permute-start(f32[19,8,128]{2,1,0:T(8,128)S(1)} %get-tuple-element.17), channel_id=1, source_target_pairs={{0,31},{1,0},{2,1},{3,2},{4,3},{5,4},{6,5},{7,6},{8,7},{9,8},{10,9... | collective-permute-start | bytes 233480 | tf_op jit(solution)/shard_map/ppermute | solution.py:603
  18.9 2.6 %copy-start = (f32[3,4,8,128]{3,2,1,0:T(8,128)S(1)}, f32[3,4,8,128]{3,2,1,0:T(8,128)}, u32[]{:S(2)}) copy-start(f32[3,4,8,128]{3,2,1,0:T(8,128)} %fluid.3) | copy-start | bytes 147460
  22.7 15.2 %all-to-all-start.1 = ((f32[32,4,128]{2,1,0:T(4,128)}), f32[32,4,128]{2,1,0:T(4,128)S(1)}, u32[]{:S(2)}, u32[]{:S(2)}) async-start(f32[32,4,128]{2,1,0:T(4,128)} %shard_map.114), calls=%async_computation.1 | async-start | bytes 131072 | tf_op jit(solution)/shard_map/all_to_all | solution.py:626
  26.9 10.3 %collective-permute-start.2 = (f32[19,8,128]{2,1,0:T(8,128)S(1)}, f32[19,8,128]{2,1,0:T(8,128)S(1)}, u32[]{:S(2)}, u32[]{:S(2)}) collective-permute-start(f32[19,8,128]{2,1,0:T(8,128)S(1)} %get-tuple-element.19.own), channel_id=1, source_target_pairs={{0,1},{1,2},{2,3},{3,4},{4,5},{5,6},{6,7},{7,8},{8,9},{9,10},{10,1... | collective-permute-start | bytes 233480 | tf_op jit(solution)/shard_map/ppermute | solution.py:627
  28.4 8.9 %collective-permute-start.3 = (f32[19,8,128]{2,1,0:T(8,128)S(1)}, f32[19,8,128]{2,1,0:T(8,128)S(1)}, u32[]{:S(2)}, u32[]{:S(2)}) collective-permute-start(f32[19,8,128]{2,1,0:T(8,128)S(1)} %get-tuple-element.20), channel_id=1, source_target_pairs={{0,31},{1,0},{2,1},{3,2},{4,3},{5,4},{6,5},{7,6},{8,7},{9,8},{10,9... | collective-permute-start | bytes 233480 | tf_op jit(solution)/shard_map/ppermute | solution.py:628
  31.5 3.4 %collective-permute-start.4 = (f32[3,2,8,128]{3,2,1,0:T(8,128)S(1)}, f32[3,2,8,128]{3,2,1,0:T(8,128)S(1)}, u32[]{:S(2)}, u32[]{:S(2)}) collective-permute-start(f32[3,2,8,128]{3,2,1,0:T(8,128)S(1)} %get-tuple-element.23), channel_id=1, source_target_pairs={{0,8},{8,16},{16,24},{24,0},{1,9},{9,17},{17,25},{25,1},{2,10},{10... | collective-permute-start | bytes 73736 | tf_op jit(solution)/shard_map/ppermute | solution.py:604
  34.0 3.3 %collective-permute-start.5 = (f32[3,2,8,128]{3,2,1,0:T(8,128)S(1)}, f32[3,2,8,128]{3,2,1,0:T(8,128)S(1)}, u32[]{:S(2)}, u32[]{:S(2)}) collective-permute-start(f32[3,2,8,128]{3,2,1,0:T(8,128)S(1)} %get-tuple-element.24), channel_id=1, source_target_pairs={{0,24},{8,0},{16,8},{24,16},{1,25},{9,1},{17,9},{25,17},{2,26},{10... | collective-permute-start | bytes 73736 | tf_op jit(solution)/shard_map/ppermute | solution.py:605

commit v5 on v4

--- a/solution.py
+++ b/solution.py
@@ -61,7 +61,7 @@
         body,
         out_shape=[jax.ShapeDtypeStruct(shape, dtype) for shape, dtype in shapes],
         in_specs=ins,
-        out_specs=[out_spec or VMEM] * len(outs),
+        out_specs=out_spec or [VMEM] * len(outs),
         scratch_shapes=scratch,
         compiler_params=pltpu.CompilerParams(vmem_limit_bytes=24 * 1024 * 1024),
     )
@@ -99,34 +99,17 @@
 
 def prep_body(n, *refs):
     sources, locals_, sems = refs[:10], refs[16:26], refs[26]
-    up, down, send, face_low, face_high, table = refs[10:16]
+    up, down, sent, face_low, face_high, table = refs[10:16]
+    send, sent_sem = refs[27:29]
     copies = fetch(sources, locals_, sems)
     pos, vel, weights, fluid, counts, box, cell, count_row, offset, mask = locals_
     for copy in copies:
         copy.wait()
     bins = pos.shape[1]
     links = offset.shape[0]
-    table[...] = jnp.zeros(table.shape, jnp.int32)
-    table[0:1, 0:bins] = count_row[...]
-    table[1 : 1 + links, 0:bins] = offset[...]
-    table[1 + links : 1 + 2 * links, 0:bins] = mask[...]
     cx, cy, cz = fluid.shape[1:]
     lane = iota((8, LANES), 1)
     row = iota((8, LANES), 0)
-    for k in range(bins):
-        for c in range(3):
-            up[k, c : c + 1, :] = pos[c, k : k + 1, :]
-            up[k, c + 4 : c + 5, :] = vel[c, k : k + 1, :]
-        occupied = iota((1, LANES), 1) < counts[k]
-        up[k, 3:4, :] = jnp.where(occupied, weights[k : k + 1, :], 0.0)
-        up[k, 7:8, :] = jnp.zeros((1, LANES), F32)
-    for k in range(bins):
-        down[k] = up[k]
-    for out, y in ((down, 0), (up, cy - 2)):
-        for c in range(3):
-            for x in range(cx):
-                at = (c * cx + x) * 2
-                out[bins + at // 8, at % 8 : at % 8 + 2, :] = fluid[c, x, y : y + 2, :]
     gy_count = lax.axis_size("gy")
     height = lax.axis_index("gz")
     ids = jnp.zeros((8, LANES), F32)
@@ -137,6 +120,8 @@
         z = height * cz + lax.rem(inside, cz)
         for field, value in enumerate((x, y, z)):
             ids = jnp.where(lane == slot_lane(field, k, n, bins), value.astype(F32), ids)
+    flat = fluid[...].reshape(3 * cx * cy, cz)
+    flat = jnp.concatenate([flat, jnp.zeros((LANES - 3 * cx * cy, cz), F32)], 0)
     pick = jnp.where(
         ((row == 1) & (lane == 0))
         | ((row == 2) & (lane == 1))
@@ -145,9 +130,9 @@
         1.0,
         0.0,
     )
-    flat = fluid[...].reshape(3 * cx * cy, cz)
-    flat = jnp.concatenate([flat, jnp.zeros((LANES - 3 * cx * cy, cz), F32)], 0)
-    faces = nt(pick, flat, lax.Precision.HIGHEST)
+    pick = jnp.concatenate([pick, jnp.zeros((8, LANES), F32)], 0).astype(BF16)
+    faces = nt(pick, jnp.concatenate(pieces_3(flat), 0).astype(BF16))[0:8]
+    faces = faces[:, 0:LANES] + faces[:, LANES : 2 * LANES] + faces[:, 2 * LANES :]
     chunk = jnp.where(row == 0, ids, faces)
     for d in range(n):
         send[d] = chunk
@@ -162,8 +147,29 @@
                     value = jnp.where(row == 5 + c, fluid[c, x, y : y + 1, :], value)
                 send[neighbour_id(dx, dy, 0)] = value
 
+    written = fetch([send], [sent], sent_sem)
+    for k in range(bins):
+        for c in range(3):
+            up[k, c : c + 1, :] = pos[c, k : k + 1, :]
+            up[k, c + 4 : c + 5, :] = vel[c, k : k + 1, :]
+        occupied = iota((1, LANES), 1) < counts[k]
+        up[k, 3:4, :] = jnp.where(occupied, weights[k : k + 1, :], 0.0)
+        up[k, 7:8, :] = jnp.zeros((1, LANES), F32)
+    for k in range(bins):
+        down[k] = up[k]
+    for out, y in ((down, 0), (up, cy - 2)):
+        for c in range(3):
+            for x in range(cx):
+                at = (c * cx + x) * 2
+                out[bins + at // 8, at % 8 : at % 8 + 2, :] = fluid[c, x, y : y + 2, :]
+    table[...] = jnp.zeros(table.shape, jnp.int32)
+    table[0:1, 0:bins] = count_row[...]
+    table[1 : 1 + links, 0:bins] = offset[...]
+    table[1 + links : 1 + 2 * links, 0:bins] = mask[...]
     face_low[...] = fluid[:, 0:2]
     face_high[...] = fluid[:, cx - 2 : cx]
+    for copy in written:
+        copy.wait()
 
 
 def gather_body(n, bins, recv, fluid, deposit, send):
@@ -195,14 +201,19 @@
         (rows < 6 * cells) & ((rows // cells) % 3 == iota((256, LANES), 1) % 4), 1.0, 0.0
     ).astype(BF16)
     spread = nn(kept, fold)
-    slot_of_lane = iota((n, LANES), 1) // 4
-    total = jnp.zeros((n, LANES), F32)
-    for k in range(bins):
-        total = total + jnp.where(slot_of_lane == k, spread[k * n : (k + 1) * n], 0.0)
-    send[:, 0, :] = pltpu.roll(total, 1, 0)
-    send[:, 1, :] = total
-    send[:, 2, :] = pltpu.roll(total, n - 1, 0)
-    send[:, 3, :] = jnp.broadcast_to(deposit[0:1], (n, LANES))
+    span = 8 * per_group
+    lane = iota((n, LANES), 1)
+    plain_slot = jnp.where(lane < 4 * bins, lane // 4, -1)
+    within = lane % span - 4 * per_group
+    mixed_slot = jnp.where(within >= 0, lane // span * per_group + within // 4, -1)
+    plain = jnp.zeros((n, LANES), F32)
+    mixed = jnp.zeros((n, LANES), F32)
+    for k in range(bins):
+        value = spread[k * n : (k + 1) * n]
+        plain = plain + jnp.where(plain_slot == k, value, 0.0)
+        mixed = mixed + jnp.where(mixed_slot == k, value, 0.0)
+    send[:, 0, :] = pltpu.roll(plain, 1, 0) + pltpu.roll(plain, 4 * bins, 1)
+    send[:, 1, :] = pltpu.roll(mixed, n - 1, 0) + deposit[0:1]
 
 
 def load_block(block, row, index, stack, weighted):
@@ -325,19 +336,22 @@
     d = flat_id()
     row = iota((8, LANES), 0)
     lane = iota((8, LANES), 1)
-    seen = recv[0]
-    for s in range(1, n):
-        seen = seen + recv[s]
+    per_group = bins // (LANES // n)
     columns = [
-        jnp.transpose(jnp.broadcast_to(seen[part : part + 1], (LANES, LANES)))
-        for part in range(3)
+        jnp.transpose(
+            jnp.broadcast_to(jnp.sum(recv[:, part, :], axis=0, keepdims=True), (LANES, LANES))
+        )
+        for part in range(2)
     ]
     rate = jnp.where(row < 4, step_sub * step_sub, step_sub) * drag_rate
 
     def push(part, k):
-        pair = columns[part][8 * (k // 2) : 8 * (k // 2) + 8]
+        at = 4 * bins * part + 4 * k
+        if part == 2:
+            at = k // per_group * 8 * per_group + 4 * per_group + 4 * (k % per_group)
+        pair = columns[part // 2][at // 8 * 8 : at // 8 * 8 + 8]
         other = pltpu.roll(pair, 4, 0)
-        here = (row < 4) if k % 2 == 0 else (row >= 4)
+        here = (row < 4) if at % 8 == 0 else (row >= 4)
         both = jnp.where(here, pair, other)
         return jnp.where((row == 3) | (row == 7), 0.0, both * rate), both
 
@@ -517,7 +531,7 @@
     tall = 2 * cy
     per_group = bins // (LANES // n)
     count = (cx + 2) * tall
-    loads = packed(n, recv, 3)
+    loads = packed(n, recv, 1)
     plane_code = planes[...].astype(jnp.int32)
     plane_row = iota((count, LANES), 0)
     for r in range(per_group):
@@ -580,7 +594,10 @@
             pltpu.VMEM(offset.shape, jnp.int32),
             pltpu.VMEM(mask.shape, jnp.int32),
             pltpu.SemaphoreType.DMA((10,)),
+            pltpu.VMEM((n, 8, LANES), F32),
+            pltpu.SemaphoreType.DMA((1,)),
         ],
+        [VMEM] * 2 + [HBM] + [VMEM] * 3,
     )(
         *[
             pltpu.with_memory_space_constraint(value, pltpu.HBM)
@@ -620,7 +637,7 @@
         + held
         + [pltpu.SemaphoreType.DMA((1,))],
     )(up, before, after, table)
-    (send,) = call(functools.partial(gather_body, n, bins), [(n, 4, LANES)], [VMEM] * 3)(
+    (send,) = call(functools.partial(gather_body, n, bins), [(n, 2, LANES)], [VMEM] * 3)(
         ids, fluid, deposits
     )
     replies = lax.all_to_all(send, AXES, 0, 0, tiled=True)
@@ -658,7 +675,7 @@
             pltpu.VMEM((4 * count, lanes), BF16),
             pltpu.VMEM((3, cx + 2, 2 * cy, 2 * cz), F32),
         ],
-        HBM,
+        [HBM] * 3,
     )(moved, before, after, replies, table, part, around, planes, depth)
     return positions_out, velocities_out, fluid_out
 

time: 42 us -> 42.6 us (1.014)
  the two profiles are of different devices: /device:TPU:1 before, /device:TPU:0 now
where the time goes in v5:
time: 42.6 us; the launch traced here: 42.4 us
  starting transfers between devices  22.5 us (53%)
  Pallas kernels  10 us (23%)
  waiting for transfers between devices  9.16 us (22%)
  between operations  0.69 us (2%)
    all_to_all x1, starting transfers between devices, step(): ids = lax.all_to_all(send, AXES, 0, 0, tiled=True)  7.33 us
    ppermute x1, starting transfers between devices, step(): after = lax.ppermute(moved_down, AXES, ring(n, -1))  5.33 us
    ppermute x1, waiting for transfers between devices, step(): before = lax.ppermute(up, AXES, ring(n, 1))  4.46 us
    pallas_call x1, Pallas kernels, step(): call(functools.partial(final_body, n, links), [positions.shape, velocitie...  3.69 us
    ppermute x1, starting transfers between devices, step(): after = lax.ppermute(down, AXES, ring(n, -1))  3.57 us
    all_to_all x1, waiting for transfers between devices, step(): replies = lax.all_to_all(send, AXES, 0, 0, tiled=True)  3.16 us
    pallas_call x1, Pallas kernels, step(): call(functools.partial(first_body, n, links), [(bins + face_blocks, 8, LA...  2.61 us
    all_to_all x1, starting transfers between devices, step(): replies = lax.all_to_all(send, AXES, 0, 0, tiled=True)  2.57 us
  transfers between devices with their start and end apart: 8, of which 3 were waited for; matrix products, arithmetic and copies ran while one was open for 0% of the time, Pallas kernels for 11%

profile of v5, /device:TPU:0, one launch (start us, length us, event | category | flops | bytes accessed | tf_op | source)
XLA Modules:
  0.0 42.4 jit_solution(2696486713304777711)
XLA Ops:
  0.6 1.9 %shard_map.112 = (f32[19,8,128]{2,1,0:T(8,128)S(1)}, f32[19,8,128]{2,1,0:T(8,128)S(1)}, f32[32,8,128]{2,1,0:T(8,128)}, f32[3,2,8,128]{3,2,1,0:T(8,128)S(1)}, f32...) custom-call(f32[3,16,128]{2,1,0:T(8,128)} %refs_0_.1, f32[3,16,128]{2,1,0:T(8,128)} %refs_1_.1, f32[16,128]{1,0:T(8,128)} %refs_2_.1, ...), custom_call_target="tpu_custom_call" | custom-call | tf_op jit(solution)/shard_map/pallas_call | solution.py:578
  2.5 7.3 %all-to-all-start = ((f32[32,8,128]{2,1,0:T(8,128)}), f32[32,8,128]{2,1,0:T(8,128)S(1)}, u32[]{:S(2)}, u32[]{:S(2)}) async-start(f32[32,8,128]{2,1,0:T(8,128)} %get-tuple-element.21), calls=%async_computation | async-start | bytes 262144 | tf_op jit(solution)/shard_map/all_to_all | solution.py:618
  9.8 1.8 %collective-permute-start = (f32[19,8,128]{2,1,0:T(8,128)S(1)}, f32[19,8,128]{2,1,0:T(8,128)S(1)}, u32[]{:S(2)}, u32[]{:S(2)}) collective-permute-start(f32[19,8,128]{2,1,0:T(8,128)S(1)} %get-tuple-element.16.own), channel_id=1, source_target_pairs={{0,1},{1,2},{2,3},{3,4},{4,5},{5,6},{6,7},{7,8},{8,9},{9,10},{10,1... | collective-permute-start | bytes 233480 | tf_op jit(solution)/shard_map/ppermute | solution.py:619
  11.7 3.6 %collective-permute-start.1 = (f32[19,8,128]{2,1,0:T(8,128)S(1)}, f32[19,8,128]{2,1,0:T(8,128)S(1)}, u32[]{:S(2)}, u32[]{:S(2)}) collective-permute-start(f32[19,8,128]{2,1,0:T(8,128)S(1)} %get-tuple-element.17), channel_id=1, source_target_pairs={{0,31},{1,0},{2,1},{3,2},{4,3},{5,4},{6,5},{7,6},{8,7},{9,8},{10,9... | collective-permute-start | bytes 233480 | tf_op jit(solution)/shard_map/ppermute | solution.py:620
  15.2 4.5 %collective-permute-done.before = f32[19,8,128]{2,1,0:T(8,128)S(1)} collective-permute-done((f32[19,8,128]{2,1,0:T(8,128)S(1)}, f32[19,8,128]{2,1,0:T(8,128)S(1)}, u32[]{:S(2)}, u32[]{:S(2)}) %collective-permute-start) | collective-permute-done | bytes 77856 | tf_op jit(solution)/shard_map/ppermute | solution.py:619
  19.7 0.0 collective-permute-done.1.after
  19.7 0.0 copy-start
  19.7 2.6 %shard_map.113 = (f32[19,8,128]{2,1,0:T(8,128)S(1)}, f32[19,8,128]{2,1,0:T(8,128)S(1)}, f32[8,128]{1,0:T(8,128)S(1)}) custom-call(f32[19,8,128]{2,1,0:T(8,128)S(1)} %get-tuple-element.16.own, f32[19,8,128]{2,1,0:T(8,128)S(1)} %collective-permute-done.before, f32[19,8,128]{2,1,0:T(8,128)S(1)} %collective-permute-done.1.after, ...), custom_call_target="tpu_custom_call" | custom-call | tf_op jit(solution)/shard_map/pallas_call | solution.py:631
  22.3 0.1 collective-permute-start.2
  22.4 5.3 %collective-permute-start.3 = (f32[19,8,128]{2,1,0:T(8,128)S(1)}, f32[19,8,128]{2,1,0:T(8,128)S(1)}, u32[]{:S(2)}, u32[]{:S(2)}) collective-permute-start(f32[19,8,128]{2,1,0:T(8,128)S(1)} %get-tuple-element.20), channel_id=1, source_target_pairs={{0,31},{1,0},{2,1},{3,2},{4,3},{5,4},{6,5},{7,6},{8,7},{9,8},{10,9... | collective-permute-start | bytes 233480 | tf_op jit(solution)/shard_map/ppermute | solution.py:645
  27.7 0.0 all-to-all-done.recv
  27.7 0.0 copy-done
  27.7 1.2 %shard_map.114 = f32[32,2,128]{2,1,0:T(2,128)} custom-call(f32[32,8,128]{2,1,0:T(8,128)S(1)} %all-to-all-done.recv, f32[3,4,8,128]{3,2,1,0:T(8,128)S(1)} %copy-done, f32[8,128]{1,0:T(8,128)S(1)} %get-tuple-element.22.deposit), custom_call_target="tpu_custom_call" | custom-call | tf_op jit(solution)/shard_map/pallas_call | solution.py:640
  28.9 2.6 %all-to-all-start.1 = ((f32[32,2,128]{2,1,0:T(2,128)}), f32[32,2,128]{2,1,0:T(2,128)S(1)}, u32[]{:S(2)}, u32[]{:S(2)}) async-start(f32[32,2,128]{2,1,0:T(2,128)} %shard_map.114), calls=%async_computation.1 | async-start | bytes 65536 | tf_op jit(solution)/shard_map/all_to_all | solution.py:643
  31.5 0.2 collective-permute-start.4
  31.7 1.6 %collective-permute-start.5 = (f32[3,2,8,128]{3,2,1,0:T(8,128)S(1)}, f32[3,2,8,128]{3,2,1,0:T(8,128)S(1)}, u32[]{:S(2)}, u32[]{:S(2)}) collective-permute-start(f32[3,2,8,128]{3,2,1,0:T(8,128)S(1)} %get-tuple-element.24), channel_id=1, source_target_pairs={{0,24},{8,0},{16,8},{24,16},{1,25},{9,1},{17,9},{25,17},{2,26},{10... | collective-permute-start | bytes 73736 | tf_op jit(solution)/shard_map/ppermute | solution.py:622
  33.3 1.5 %collective-permute-done.4.x_low = f32[3,2,8,128]{3,2,1,0:T(8,128)S(1)} collective-permute-done((f32[3,2,8,128]{3,2,1,0:T(8,128)S(1)}, f32[3,2,8,128]{3,2,1,0:T(8,128)S(1)}, u32[]{:S(2)}, u32[]{:S(2)}) %collective-permute-start.4) | collective-permute-done | bytes 24608 | tf_op jit(solution)/shard_map/ppermute | solution.py:621
  34.8 0.0 collective-permute-done.5.x_high
  34.8 0.0 collective-permute-done.2.y_low.before
  34.8 0.0 collective-permute-done.3.y_high.after
  34.8 0.7 %shard_map.115 = (f32[3,8,16,256]{3,2,1,0:T(8,128)S(1)}, f32[3,4,8,128]{3,2,1,0:T(8,128)S(1)}, f32[4,128]{1,0:T(4,128)S(1)}, bf16[256,512]{1,0:T(8,128)(2,1)S(1)}) custom-call(f32[3,4,8,128]{3,2,1,0:T(8,128)S(1)} %copy-done, f32[3,2,8,128]{3,2,1,0:T(8,128)S(1)} %collective-permute-done.4.x_low, f32[3,2,8,128]{3,2,1,0:T(8,128)S(1)} %collective-permute-done.5.x_high, ...), custom_call_target="tpu_custom_call" | custom-call | tf_op jit(solution)/shard_map/pallas_call | solution.py:654
  35.5 3.2 %all-to-all-done.1.recv = f32[32,2,128]{2,1,0:T(2,128)S(1)} async-done(((f32[32,2,128]{2,1,0:T(2,128)}), f32[32,2,128]{2,1,0:T(2,128)S(1)}, u32[]{:S(2)}, u32[]{:S(2)}) %all-to-all-start.1) | async-done | bytes 32800 | tf_op jit(solution)/shard_map/all_to_all | solution.py:643
  38.7 3.7 %shard_map.116 = (f32[3,16,128]{2,1,0:T(8,128)}, f32[3,16,128]{2,1,0:T(8,128)}, f32[3,4,8,128]{3,2,1,0:T(8,128)}) custom-call(f32[19,8,128]{2,1,0:T(8,128)S(1)} %get-tuple-element.19.own, f32[19,8,128]{2,1,0:T(8,128)S(1)} %collective-permute-done.2.y_low.before, f32[19,8,128]{2,1,0:T(8,128)S(1)} %collective-permute-done.3.y_high.after, ...), custom_call_target="tpu_custom_call" | custom-call | tf_op jit(solution)/shard_map/pallas_call | solution.py:661
Async XLA Ops:
  2.5 25.2 %all-to-all-start = ((f32[32,8,128]{2,1,0:T(8,128)}), f32[32,8,128]{2,1,0:T(8,128)S(1)}, u32[]{:S(2)}, u32[]{:S(2)}) async-start(f32[32,8,128]{2,1,0:T(8,128)} %get-tuple-element.21), calls=%async_computation | async-start | bytes 262144 | tf_op jit(solution)/shard_map/all_to_all | solution.py:618
  9.8 9.9 %collective-permute-start = (f32[19,8,128]{2,1,0:T(8,128)S(1)}, f32[19,8,128]{2,1,0:T(8,128)S(1)}, u32[]{:S(2)}, u32[]{:S(2)}) collective-permute-start(f32[19,8,128]{2,1,0:T(8,128)S(1)} %get-tuple-element.16.own), channel_id=1, source_target_pairs={{0,1},{1,2},{2,3},{3,4},{4,5},{5,6},{6,7},{7,8},{8,9},{9,10},{10,1... | collective-permute-start | bytes 233480 | tf_op jit(solution)/shard_map/ppermute | solution.py:619
  11.7 8.0 %collective-permute-start.1 = (f32[19,8,128]{2,1,0:T(8,128)S(1)}, f32[19,8,128]{2,1,0:T(8,128)S(1)}, u32[]{:S(2)}, u32[]{:S(2)}) collective-permute-start(f32[19,8,128]{2,1,0:T(8,128)S(1)} %get-tuple-element.17), channel_id=1, source_target_pairs={{0,31},{1,0},{2,1},{3,2},{4,3},{5,4},{6,5},{7,6},{8,7},{9,8},{10,9... | collective-permute-start | bytes 233480 | tf_op jit(solution)/shard_map/ppermute | solution.py:620
  19.7 8.0 %copy-start = (f32[3,4,8,128]{3,2,1,0:T(8,128)S(1)}, f32[3,4,8,128]{3,2,1,0:T(8,128)}, u32[]{:S(2)}) copy-start(f32[3,4,8,128]{3,2,1,0:T(8,128)} %fluid.3) | copy-start | bytes 147460
  22.3 12.5 %collective-permute-start.2 = (f32[19,8,128]{2,1,0:T(8,128)S(1)}, f32[19,8,128]{2,1,0:T(8,128)S(1)}, u32[]{:S(2)}, u32[]{:S(2)}) collective-permute-start(f32[19,8,128]{2,1,0:T(8,128)S(1)} %get-tuple-element.19.own), channel_id=1, source_target_pairs={{0,1},{1,2},{2,3},{3,4},{4,5},{5,6},{6,7},{7,8},{8,9},{9,10},{10,1... | collective-permute-start | bytes 233480 | tf_op jit(solution)/shard_map/ppermute | solution.py:644
  22.4 12.5 %collective-permute-start.3 = (f32[19,8,128]{2,1,0:T(8,128)S(1)}, f32[19,8,128]{2,1,0:T(8,128)S(1)}, u32[]{:S(2)}, u32[]{:S(2)}) collective-permute-start(f32[19,8,128]{2,1,0:T(8,128)S(1)} %get-tuple-element.20), channel_id=1, source_target_pairs={{0,31},{1,0},{2,1},{3,2},{4,3},{5,4},{6,5},{7,6},{8,7},{9,8},{10,9... | collective-permute-start | bytes 233480 | tf_op jit(solution)/shard_map/ppermute | solution.py:645
  28.9 9.8 %all-to-all-start.1 = ((f32[32,2,128]{2,1,0:T(2,128)}), f32[32,2,128]{2,1,0:T(2,128)S(1)}, u32[]{:S(2)}, u32[]{:S(2)}) async-start(f32[32,2,128]{2,1,0:T(2,128)} %shard_map.114), calls=%async_computation.1 | async-start | bytes 65536 | tf_op jit(solution)/shard_map/all_to_all | solution.py:643
  31.5 3.3 %collective-permute-start.4 = (f32[3,2,8,128]{3,2,1,0:T(8,128)S(1)}, f32[3,2,8,128]{3,2,1,0:T(8,128)S(1)}, u32[]{:S(2)}, u32[]{:S(2)}) collective-permute-start(f32[3,2,8,128]{3,2,1,0:T(8,128)S(1)} %get-tuple-element.23), channel_id=1, source_target_pairs={{0,8},{8,16},{16,24},{24,0},{1,9},{9,17},{17,25},{25,1},{2,10},{10... | collective-permute-start | bytes 73736 | tf_op jit(solution)/shard_map/ppermute | solution.py:621
  31.7 3.2 %collective-permute-start.5 = (f32[3,2,8,128]{3,2,1,0:T(8,128)S(1)}, f32[3,2,8,128]{3,2,1,0:T(8,128)S(1)}, u32[]{:S(2)}, u32[]{:S(2)}) collective-permute-start(f32[3,2,8,128]{3,2,1,0:T(8,128)S(1)} %get-tuple-element.24), channel_id=1, source_target_pairs={{0,24},{8,0},{16,8},{24,16},{1,25},{9,1},{17,9},{25,17},{2,26},{10... | collective-permute-start | bytes 73736 | tf_op jit(solution)/shard_map/ppermute | solution.py:622
